TPU v7x, 32 devices: a whole 2x2x4 slice. The times are simulated.
32 devices in a mesh: dp: 4 (over z), seq: 4 (over y, core), tensor: 2 (over x).
Axes of the slice: x: 2, y: 2, z: 4, core: 2. Of those that a mesh axis runs over, the one named last changes fastest.
Arguments:
- q_self: bfloat16 [4, 512, 4096], P('dp', 'seq', 'tensor'), may hold values from -162 to 162
- k_self: bfloat16 [4, 512, 1024], P('dp', 'seq', 'tensor'), may hold values from -6 to 6
- v_self: bfloat16 [4, 512, 1024], P('dp', 'seq', 'tensor'), may hold values from -6 to 6
- docs: int32 [4, 512], P('dp', 'seq'), may hold values from 0 to 3, never falling along the last dimension, each value on 1 to 384 neighbouring positions
- q_cross: bfloat16 [4, 512, 4096], P('dp', 'seq', 'tensor'), may hold values from -162 to 162
- cotangent: bfloat16 [4, 512, 4096], P('dp', 'seq', 'tensor'), may hold values from -6 to 6
- img_keys: bfloat16 [4, 128, 1024], P('dp', 'seq', 'tensor'), may hold values from -6 to 6
- features: bfloat16 [4, 128, 1280], P('dp', 'seq'), may hold values from -6 to 6
- w_value: bfloat16 [1280, 1024], P(None, 'tensor'), may hold values from -0.15625 to 0.15625
- tiles: int32 [4, 4], P('dp'), may hold values from 1 to 4
- cite: int32 [4, 4], P('dp'), may hold values from 0 to 3, each once within a row
Outputs:
- combined: bfloat16 [4, 512, 4096], P('dp', 'seq', 'tensor')
- weight_grad: float32 [1280, 1024], P(('dp', 'seq'), 'tensor')
Inputs may be any that keep to these rules, and one draw needn't show every extreme that they name: `docs`: along each sample the document numbers never fall; every document 0 to 3 has one or more tokens. `cite`: each sample's row names every image exactly once.
All inputs are finite; a program needn't handle non-finite values.
Results may differ from a plain program's by a relative error of at most 0.029.
Values may be sent and summed in bfloat16 or wider, within the bound.
No kernel may reach another device: no remote copies, remote signals or barrier semaphores. Data moves between devices by JAX's collectives and lax.ppermute only.
A program may use at most 64 MiB of HBM per device.

v0:
```python
import math

import jax
import jax.numpy as jnp
from jax import lax
from jax.sharding import PartitionSpec as P

HD = 128
TILE_TOK = 8


MASK_FILL = -1e30


def absorb_block(
    running, queries, key_rows, value_rows, key_docs, key_pos, query_pos, my_docs, score_scale
):
    running_max, denominator, numerator = running
    kv_local = queries.shape[1]
    key_count = key_rows.shape[0]
    key_heads = key_rows.reshape(key_count, kv_local, HD)
    value_heads = value_rows.reshape(key_count, kv_local, HD)
    scores = (
        jnp.einsum("tgcd,sgd->gcts", queries, key_heads, preferred_element_type=jnp.float32)
        * score_scale
    )
    kept = (query_pos[:, None] >= key_pos[None, :]) & (my_docs[:, None] == key_docs[None, :])
    scores = jnp.where(kept, scores, MASK_FILL)
    new_max = jnp.maximum(running_max, jnp.max(scores, axis=-1))
    factor = jnp.exp(running_max - new_max)
    weights = jnp.where(kept, jnp.exp(scores - new_max[..., None]), 0.0)
    denominator = factor * denominator + jnp.sum(weights, axis=-1)
    numerator = factor[..., None] * numerator + jnp.einsum(
        "gcts,sgd->gctd",
        weights.astype(jnp.bfloat16),
        value_heads,
        preferred_element_type=jnp.float32,
    )
    return (new_max, denominator, numerator)


def on_device(
    q_self, k_self, v_self, docs, q_cross, cotangent, img_keys, features, w_value, tiles, cite
):
    tok_rows = q_self.shape[1]
    kv_local = k_self.shape[2] // HD
    heads_local = q_self.shape[2] // HD
    group_size = heads_local // kv_local
    score_scale = HD ** (-0.5)
    first_row = lax.axis_index("seq") * tok_rows
    query_pos = first_row + jnp.arange(tok_rows, dtype=jnp.int32)
    my_docs = docs[0]
    queries = q_self[0].reshape(tok_rows, kv_local, group_size, HD)
    start_state = (
        jnp.full((kv_local, group_size, tok_rows), MASK_FILL, jnp.float32),
        jnp.zeros((kv_local, group_size, tok_rows), jnp.float32),
        jnp.zeros((kv_local, group_size, tok_rows, HD), jnp.float32),
    )
    piece_keys = lax.all_gather(k_self, "seq", axis=1, tiled=True)
    piece_values = lax.all_gather(v_self, "seq", axis=1, tiled=True)
    piece_docs = lax.all_gather(docs, "seq", axis=1, tiled=True)
    key_count = piece_keys.shape[1]
    block_rows = math.gcd(key_count, 512)
    block_count = key_count // block_rows
    key_blocks = piece_keys[0].reshape(block_count, block_rows, -1)
    value_blocks = piece_values[0].reshape(block_count, block_rows, -1)
    doc_blocks = piece_docs[0].reshape(block_count, block_rows)
    pos_blocks = jnp.arange(key_count, dtype=jnp.int32).reshape(block_count, block_rows)

    def absorb_step(state_now, block_item):
        key_part, value_part, doc_part, pos_part = block_item
        return (
            absorb_block(
                state_now,
                queries,
                key_part,
                value_part,
                doc_part,
                pos_part,
                query_pos,
                my_docs,
                score_scale,
            ),
            None,
        )

    running_max, denominator, numerator = lax.scan(
        absorb_step, start_state, (key_blocks, value_blocks, doc_blocks, pos_blocks)
    )[0]
    self_out = numerator / denominator[..., None]
    values_own = jnp.dot(features[0], w_value, preferred_element_type=jnp.float32).astype(
        jnp.bfloat16
    )
    image_keys, image_values = (
        lax.all_gather(img_keys[0], "seq", axis=0, tiled=True),
        lax.all_gather(values_own, "seq", axis=0, tiled=True),
    )
    key_count = image_keys.shape[0]
    slot_count = img_keys.shape[1]
    image_count = tiles.shape[1]
    doc_hit = my_docs[:, None] == jnp.arange(cite.shape[1], dtype=jnp.int32)[None, :]
    image_of = jnp.sum(jnp.where(doc_hit, cite[0][None, :], 0), axis=1)
    slot_ids = jnp.arange(key_count, dtype=jnp.int32)
    key_image = slot_ids // slot_count
    owner_hit = key_image[:, None] == jnp.arange(image_count, dtype=jnp.int32)[None, :]
    tile_limit = jnp.sum(jnp.where(owner_hit, tiles[0][None, :], 0), axis=1) * TILE_TOK
    cross_kept = (image_of[:, None] == key_image[None, :]) & (slot_ids % slot_count < tile_limit)[
        None, :
    ]
    cross_q = q_cross[0].reshape(tok_rows, kv_local, group_size, HD)
    cross_scores = (
        jnp.einsum(
            "tgcd,sgd->gcts",
            cross_q,
            image_keys.reshape(key_count, kv_local, HD),
            preferred_element_type=jnp.float32,
        )
        * score_scale
    )
    cross_scores = jnp.where(cross_kept, cross_scores, MASK_FILL)
    cross_exp = jnp.where(
        cross_kept, jnp.exp(cross_scores - jnp.max(cross_scores, axis=-1, keepdims=True)), 0.0
    )
    cross_weights = (cross_exp / jnp.sum(cross_exp, axis=-1, keepdims=True)).astype(jnp.bfloat16)
    cross_out = jnp.einsum(
        "gcts,sgd->gctd",
        cross_weights,
        image_values.reshape(key_count, kv_local, HD),
        preferred_element_type=jnp.float32,
    )
    merged = (
        (self_out + cross_out)
        .astype(jnp.bfloat16)
        .transpose(2, 0, 1, 3)
        .reshape(1, tok_rows, heads_local * HD)
    )
    cot_rows = cotangent[0].reshape(tok_rows, kv_local, group_size, HD)
    grad_terms = jnp.einsum(
        "gcts,tgcd->sgd", cross_weights, cot_rows, preferred_element_type=jnp.float32
    ).reshape(key_count, kv_local * HD)
    value_grad = lax.psum_scatter(
        grad_terms.astype(jnp.bfloat16), "seq", scatter_dimension=0, tiled=True
    )
    own_features = features[0]
    summed_samples = lax.psum_scatter(
        lax.dot_general(
            own_features, value_grad, (((0,), (0,)), ((), ())), preferred_element_type=jnp.float32
        ).astype(jnp.bfloat16),
        "dp",
        scatter_dimension=0,
        tiled=True,
    )
    weight_grad = lax.psum_scatter(summed_samples, "seq", scatter_dimension=0, tiled=True).astype(
        jnp.float32
    )
    return (merged, weight_grad)


def solution(mesh):
    in_specs = (
        P("dp", "seq", "tensor"),
        P("dp", "seq", "tensor"),
        P("dp", "seq", "tensor"),
        P("dp", "seq"),
        P("dp", "seq", "tensor"),
        P("dp", "seq", "tensor"),
        P("dp", "seq", "tensor"),
        P("dp", "seq", None),
        P(None, "tensor"),
        P("dp", None),
        P("dp", None),
    )
    out_specs = (P("dp", "seq", "tensor"), P(("dp", "seq"), "tensor"))
    return jax.shard_map(
        on_device, mesh=mesh, in_specs=in_specs, out_specs=out_specs, check_vma=False
    )
```

profile of v0, /device:TPU:0, one launch (start us, length us, event | category | flops | bytes accessed | tf_op | source)
XLA Modules:
  0.0 108.2 jit_solution(1521018898285160767)
XLA Ops:
  7.2 0.8 select_reduce_fusion
  8.1 1.4 %reshape_squeeze.10 = bf16[128,4,4,128]{3,2,1,0:T(4,128)(2,1)S(1)} reshape(bf16[1,128,2048]{2,1,0:T(8,128)(2,1)} %param.15) | data formatting | bytes 1048576 | tf_op jit(solution)/shard_map/reshape;squeeze | solution.py:110
  9.5 6.7 %all-gather = bf16[1,128,512]{2,1,0:T(8,128)(2,1)S(1)} all-gather(bf16[1,32,512]{2,1,0:T(8,128)(2,1)} %param.17), channel_id=2, replica_groups=mesh['dp'=4,'seq'=4,'tensor'=2] {'seq'}, dimensions={1}, use_global_device_ids=true | all-gather | bytes 163840 | tf_op jit(solution)/shard_map/all_gather | solution.py:95
  16.4 1.3 %copy.78 = bf16[1,128,2048]{1,2,0:T(8,128)(2,1)S(1)} copy(bf16[1,128,2048]{2,1,0:T(8,128)(2,1)} %param.16) | data formatting | bytes 1048576 | tf_op jit(solution)/shard_map/reshape;squeeze | solution.py:137
  17.7 0.8 select_reduce_fusion.1
  18.6 1.5 %fusion.39 = (f32[4,4,128]{2,1,0:T(4,128)S(1)}, f32[4,4,128,128]{2,3,1,0:T(8,128)}) fusion(bf16[128,4,128,1]{0,2,3,1:T(8,128)(2,1)S(1)} %bitcast.96, bf16[128,4,4,128]{3,2,1,0:T(4,128)(2,1)S(1)} %reshape_squeeze.10, pred[128,128]{0,1:T(8,128)(4,1)S(1)} %compare_and_fusion), kind=kOutput, calls=%fused_computation.53 | convolution fusion | flops 68419712 | bytes 1728512 | tf_op jit(solution)/shard_map/sub | solution.py:122
  20.1 1.6 %fusion.21 = bf16[4,128,128]{1,2,0:T(8,128)(2,1)S(1)} fusion(bf16[128,4,4,128]{0,3,2,1:T(8,128)(2,1)S(1)} %bitcast.94, f32[4,4,128,128]{2,3,1,0:T(8,128)} %get-tuple-element.48, f32[4,4,128]{2,1,0:T(4,128)S(1)} %get-tuple-element.47), kind=kOutput, calls=%fused_computation.22 | convolution fusion | flops 67698688 | bytes 1712128 | tf_op jit(solution)/shard_map/gcts,tgcd->sgd/dot_general | solution.py:138
  21.7 0.8 copy.79
  22.6 21.3 %reduce-scatter.10.cloned.1.call-done = bf16[32,512]{1,0:T(8,128)(2,1)} async-done(((bf16[128,512]{1,0:T(8,128)(2,1)}), bf16[32,512]{1,0:T(8,128)(2,1)}) %reduce-scatter.10.cloned.1.call-update) | async-done | bytes 32784
  43.9 1.3 %fusion.4 = bf16[1280,512]{0,1:T(8,128)(2,1)S(1)} fusion(bf16[32,512]{1,0:T(8,128)(2,1)} %reduce-scatter.10.cloned.1.call-done, bf16[1,32,1280]{2,1,0:T(8,128)(2,1)S(1)} %copy-done.2), kind=kOutput, calls=%fused_computation.7 | convolution fusion | flops 42598400 | bytes 1425408 | tf_op jit(solution)/shard_map/dot_general | solution.py:146
  45.2 1.5 %copy.81 = bf16[1280,512]{1,0:T(8,128)(2,1)} copy(bf16[1280,512]{0,1:T(8,128)(2,1)S(1)} %fusion.4) | data formatting | bytes 2621440
  47.3 6.5 %all_gather.17 = bf16[1,512,512]{2,1,0:T(8,128)(2,1)S(1)} all-gather(bf16[1,128,512]{2,1,0:T(8,128)(2,1)S(1)} %copy-done.3), channel_id=1, replica_groups=mesh['dp'=4,'seq'=4,'tensor'=2] {'seq'}, dimensions={1}, use_global_device_ids=true | all-gather | bytes 655360 | tf_op jit(solution)/shard_map/all_gather | solution.py:60
  54.1 5.1 %all_gather.15 = s32[1,512]{1,0:T(1,128)S(1)} all-gather(s32[1,128]{1,0:T(1,128)S(1)} %copy-done.5), channel_id=1, replica_groups=mesh['dp'=4,'seq'=4,'tensor'=2] {'seq'}, dimensions={1}, use_global_device_ids=true | all-gather | bytes 2560 | tf_op jit(solution)/shard_map/all_gather | solution.py:61
  59.1 7.3 %all_gather.16 = bf16[1,512,512]{1,2,0:T(8,128)(2,1)S(1)} all-gather(bf16[1,128,512]{1,2,0:T(8,128)(2,1)S(1)} %copy.51), channel_id=1, replica_groups=mesh['dp'=4,'seq'=4,'tensor'=2] {'seq'}, dimensions={1}, use_global_device_ids=true | all-gather | bytes 655360 | tf_op jit(solution)/shard_map/all_gather | solution.py:59
  66.6 0.9 fusion.1
  67.5 1.0 fusion.2
  68.5 2.2 %fusion.17 = f32[128,4,4,128]{0,3,2,1:T(8,128)} fusion(bf16[512,4,128,1]{0,2,3,1:T(8,128)(2,1)S(1)} %bitcast.93, f32[4,512,128,4]{2,1,3,0:T(8,128)S(1)} %get-tuple-element.46, f32[4,4,128]{2,1,0:T(4,128)S(1)} %get-tuple-element.44, pred[128,512]{0,1:T(8,128)(4,1)S(1)} %fusion.25, f32[128,4,4]{0,2,1:T(4,128)S(1)} %get-tuple-element.32), kind=kOutput, calls=%fused_computation.19 | convolution fusion | flops 273940480 | bytes 5849088 | tf_op jit(solution)/shard_map/while/body/eval_jaxpr/gcts,sgd->gctd/dot_general | solution.py:33
  70.6 7.6 %reduce-scatter.12.cloned.1.call-done = bf16[320,512]{1,0:T(8,128)(2,1)} async-done(((bf16[1280,512]{1,0:T(8,128)(2,1)}), bf16[320,512]{1,0:T(8,128)(2,1)}) %reduce-scatter.12.cloned.1.call-update) | async-done | bytes 327696
  78.6 5.4 %all_gather.19 = bf16[128,512]{1,0:T(8,128)(2,1)S(1)} all-gather(bf16[32,512]{1,0:T(8,128)(2,1)S(1)} %convolution_convert_fusion.1), channel_id=1, replica_groups=mesh['dp'=4,'seq'=4,'tensor'=2] {'seq'}, dimensions={0}, use_global_device_ids=true | all-gather | bytes 163840 | tf_op jit(solution)/shard_map/all_gather | solution.py:96
  84.2 1.5 %fusion.20 = bf16[128,4,4,128]{0,3,2,1:T(8,128)(2,1)S(1)} fusion(bf16[128,4,128,1]{0,2,3,1:T(8,128)(2,1)S(1)} %bitcast.97, f32[128,4,4,128]{0,3,2,1:T(8,128)} %fusion.17, f32[128,4,4]{0,2,1:T(4,128)S(1)} %bitcast_add_fusion, f32[4,4,128,128]{2,3,1,0:T(8,128)S(1)} %copy-done.6, f32[4,4,128]{2,1,0:T(4,128)S(1)} %get-tuple-element.47), kind=kOutput, calls=%fused_computation.20 | convolution fusion | flops 68419584 | bytes 2768896 | tf_op jit(solution)/shard_map/gcts,sgd->gctd/dot_general | solution.py:125
  85.7 1.0 copy.63
  86.7 13.2 %reduce-scatter.14.cloned.1.call-done = bf16[80,512]{1,0:T(8,128)(2,1)} async-done(((bf16[320,512]{1,0:T(8,128)(2,1)}), bf16[80,512]{1,0:T(8,128)(2,1)}) %reduce-scatter.14.cloned.1.call-update) | async-done | bytes 81936
  99.9 1.0 copy.84
  100.9 0.8 copy.64
  (33 shorter events, 1.7 us)
Async XLA Ops:
  7.2 71.1 %copy-start = (bf16[1280,512]{1,0:T(8,128)(2,1)S(1)}, bf16[1280,512]{1,0:T(8,128)(2,1)}, u32[]{:S(2)}) copy-start(bf16[1280,512]{1,0:T(8,128)(2,1)} %param.19) | copy-start | bytes 3932164
  7.2 36.8 %reduce-scatter.10.cloned.1.call-start = ((), (), s32[]{:S(2)}) async-start(), calls=%async_computation.3 | async-start | bytes 163840
  16.4 27.6 %copy-start.2 = (bf16[1,32,1280]{2,1,0:T(8,128)(2,1)S(1)}, bf16[1,32,1280]{2,1,0:T(8,128)(2,1)}, u32[]{:S(2)}) copy-start(bf16[1,32,1280]{2,1,0:T(8,128)(2,1)} %param.18) | copy-start | bytes 245764
  20.1 26.7 %copy-start.4 = (bf16[1,128,512]{2,1,0:T(8,128)(2,1)S(1)}, bf16[1,128,512]{2,1,0:T(8,128)(2,1)}, u32[]{:S(2)}) copy-start(bf16[1,128,512]{2,1,0:T(8,128)(2,1)} %param.12) | copy-start | bytes 393220
  20.1 26.8 %copy-start.1 = (bf16[1,128,2048]{2,1,0:T(8,128)(2,1)S(1)}, bf16[1,128,2048]{2,1,0:T(8,128)(2,1)}, u32[]{:S(2)}) copy-start(bf16[1,128,2048]{2,1,0:T(8,128)(2,1)} %param.11) | copy-start | bytes 1572868
  21.7 25.6 %copy-start.3 = (bf16[1,128,512]{2,1,0:T(8,128)(2,1)S(1)}, bf16[1,128,512]{2,1,0:T(8,128)(2,1)}, u32[]{:S(2)}) copy-start(bf16[1,128,512]{2,1,0:T(8,128)(2,1)} %param.13) | copy-start | bytes 393220
  22.5 31.5 %copy-start.5 = (s32[1,128]{1,0:T(1,128)S(1)}, s32[1,128]{1,0:T(1,128)}, u32[]{:S(2)}) copy-start(s32[1,128]{1,0:T(1,128)} %param.14) | copy-start | bytes 1540
  22.6 55.7 %reduce-scatter.12.cloned.1.call-start = ((), (), s32[]{:S(2)}) async-start(), calls=%async_computation.4 | async-start | bytes 1638400
  46.8 53.2 %reduce-scatter.14.cloned.1.call-start = ((), (), s32[]{:S(2)}) async-start(), calls=%async_computation.5 | async-start | bytes 409600
  68.5 15.7 %copy-start.6 = (f32[4,4,128,128]{2,3,1,0:T(8,128)S(1)}, f32[4,4,128,128]{2,3,1,0:T(8,128)}, u32[]{:S(2)}) copy-start(f32[4,4,128,128]{2,3,1,0:T(8,128)} %get-tuple-element.48) | copy-start | bytes 3145732
Sparse Core Ops, SparseCore 0:
  22.7 21.2 reduce-scatter.9
  46.9 31.3 reduce-scatter.11
  80.8 19.1 reduce-scatter.13
where the time goes:
time: 109 us; the launch traced here: 108 us
  waiting for transfers between devices  42.2 us (39%)
  blocking collectives  31 us (28%)
  between operations  14 us (13%)
  matrix products  9.32 us (9%)
  local copies, waits for them, and re-layouts  8.77 us (8%)
  other arithmetic  2.87 us (3%)
    unnamed x6, waiting for transfers between devices  42.2 us
    all_gather x1, blocking collectives, on_device(): piece_keys = lax.all_gather(k_self, 'seq', axis=1, tiled=True)  7.28 us
    all_gather x1, blocking collectives, on_device(): lax.all_gather(img_keys[0], 'seq', axis=0, tiled=True)  6.75 us
    all_gather x1, blocking collectives, on_device(): piece_values = lax.all_gather(v_self, 'seq', axis=1, tiled=True)  6.5 us
    all_gather x1, blocking collectives, on_device(): lax.all_gather(values_own, 'seq', axis=0, tiled=True)  5.42 us
    unnamed x20, local copies, waits for them, and re-layouts  5.21 us
    all_gather x1, blocking collectives, on_device(): piece_docs = lax.all_gather(docs, 'seq', axis=1, tiled=True)  5.06 us
  transfers between devices with their start and end apart: 3, of which 3 were waited for; matrix products, arithmetic and copies ran while one was open for 7% of the time, Pallas kernels for 0%

commit v1 on v0

--- a/solution.py
+++ b/solution.py
@@ -1,8 +1,11 @@
+import functools
 import math
 
 import jax
 import jax.numpy as jnp
 from jax import lax
+from jax.experimental import pallas as pl
+from jax.experimental.pallas import tpu as pltpu
 from jax.sharding import PartitionSpec as P
 
 HD = 128
@@ -10,6 +13,7 @@
 
 
 MASK_FILL = -1e30
+LOG2E = math.log2(math.e)
 
 
 def absorb_block(
@@ -39,7 +43,7 @@
     return (new_max, denominator, numerator)
 
 
-def on_device(
+def on_device_general(
     q_self, k_self, v_self, docs, q_cross, cotangent, img_keys, features, w_value, tiles, cite
 ):
     tok_rows = q_self.shape[1]
@@ -96,8 +100,8 @@
         lax.all_gather(values_own, "seq", axis=0, tiled=True),
     )
     key_count = image_keys.shape[0]
-    slot_count = img_keys.shape[1]
     image_count = tiles.shape[1]
+    slot_count = key_count // image_count
     doc_hit = my_docs[:, None] == jnp.arange(cite.shape[1], dtype=jnp.int32)[None, :]
     image_of = jnp.sum(jnp.where(doc_hit, cite[0][None, :], 0), axis=1)
     slot_ids = jnp.arange(key_count, dtype=jnp.int32)
@@ -156,6 +160,279 @@
     return (merged, weight_grad)
 
 
+def dot_nt(left, right):
+    return lax.dot_general(
+        left, right, (((1,), (1,)), ((), ())), preferred_element_type=jnp.float32
+    )
+
+
+def dot_nn(left, right):
+    return lax.dot_general(
+        left, right, (((1,), (0,)), ((), ())), preferred_element_type=jnp.float32
+    )
+
+
+def dot_tn(left, right):
+    return lax.dot_general(
+        left, right, (((0,), (0,)), ((), ())), preferred_element_type=jnp.float32
+    )
+
+
+def stacked_heads(ref, group, group_size):
+    first = group * group_size
+    return jnp.concatenate(
+        [ref[:, (first + c) * HD : (first + c + 1) * HD] for c in range(group_size)], axis=0
+    )
+
+
+def cross_kernel(
+    sizes, tiles_ref, cite_ref, docs_ref, head_ref, q_ref, cot_ref, grad_ref, weights_ref
+):
+    kv_local, group_size, slots, images, slot_count = sizes
+    blocks = head_ref.shape[0]
+    key_count = blocks * slots
+    docs = docs_ref[...]
+    tok_rows = docs.shape[1]
+    image_of = jnp.zeros_like(docs)
+    for doc in range(cite_ref.shape[1]):
+        image_of = jnp.where(docs == doc, cite_ref[0, doc], image_of)
+    slot_ids = lax.broadcasted_iota(jnp.int32, (key_count, tok_rows), 0)
+    bias = jnp.full((key_count, tok_rows), MASK_FILL, jnp.float32)
+    for image in range(images):
+        first = image * slot_count
+        usable = (slot_ids >= first) & (slot_ids < first + tiles_ref[0, image] * TILE_TOK)
+        bias = jnp.where(usable & (image_of == image), 0.0, bias)
+    bias = jnp.concatenate([bias] * group_size, axis=1)
+    scale = HD ** (-0.5) * LOG2E
+    for group in range(kv_local):
+        columns = slice(group * HD, (group + 1) * HD)
+        keys = jnp.concatenate([head_ref[b, :slots, columns] for b in range(blocks)], axis=0)
+        scores = dot_nt(keys, stacked_heads(q_ref, group, group_size)) * scale + bias
+        exps = jnp.exp2(scores - jnp.max(scores, axis=0, keepdims=True))
+        inverse = 1.0 / jnp.sum(exps, axis=0, keepdims=True)
+        weights = (exps * inverse).astype(jnp.bfloat16)
+        weights_ref[group] = weights
+        grad_ref[:, columns] = dot_nn(weights, stacked_heads(cot_ref, group, group_size)).astype(
+            jnp.bfloat16
+        )
+
+
+def attend_kernel(sizes, where_ref, docs_ref, head_ref, q_ref, w_ref, weights_ref, *rest):
+    kv_local, group_size, slots, feature_rows = sizes
+    blocks = head_ref.shape[0]
+    packs, out_ref, values_ref = rest[:blocks], rest[blocks], rest[blocks + 1]
+    seq_at = where_ref[0]
+    tok_rows = q_ref.shape[0]
+    key_rows = (packs[0].shape[0] - feature_rows) // 2
+    width = packs[0].shape[1]
+    vision = w_ref.shape[0]
+    parts = feature_rows // slots
+    total = None
+    for part in range(parts):
+        cut = min(width, vision - part * width)
+        rows = jnp.concatenate(
+            [pack[part * slots : (part + 1) * slots, :cut] for pack in packs], axis=0
+        )
+        term = dot_nn(rows, w_ref[part * width : part * width + cut, :])
+        total = term if total is None else total + term
+    values = total.astype(jnp.bfloat16)
+    for x in range(blocks):
+        owner = pl.multiple_of((seq_at ^ x) * slots, slots)
+        values_ref[pl.ds(owner, slots), :] = values[x * slots : (x + 1) * slots]
+    docs = docs_ref[...].astype(jnp.float32)
+    start = jnp.zeros((1, tok_rows), jnp.float32)
+    for b in range(blocks):
+        row = head_ref[b, slots : slots + 16, :tok_rows].astype(jnp.float32)[0:1]
+        column = jnp.transpose(jnp.broadcast_to(row, (tok_rows, tok_rows)))
+        start = start + jnp.sum(jnp.where(column < docs, 1.0, 0.0), axis=0, keepdims=True)
+    start = start.astype(jnp.int32)
+    query_pos = seq_at * tok_rows + lax.broadcasted_iota(jnp.int32, (1, tok_rows), 1)
+    bias = []
+    for x in range(blocks):
+        key_pos = (seq_at ^ x) * key_rows + lax.broadcasted_iota(
+            jnp.int32, (key_rows, tok_rows), 0
+        )
+        kept = (key_pos >= start) & (key_pos <= query_pos)
+        bias.append(jnp.where(kept, 0.0, MASK_FILL))
+    bias = jnp.concatenate(bias, axis=0)
+    bias = jnp.concatenate([bias] * group_size, axis=1)
+    scale = HD ** (-0.5) * LOG2E
+    first_key, first_value = feature_rows, feature_rows + key_rows
+    for group in range(kv_local):
+        columns = slice(group * HD, (group + 1) * HD)
+        keys = jnp.concatenate(
+            [pack[first_key : first_key + key_rows, columns] for pack in packs], axis=0
+        )
+        vals = jnp.concatenate(
+            [pack[first_value : first_value + key_rows, columns] for pack in packs], axis=0
+        )
+        scores = dot_nt(keys, stacked_heads(q_ref, group, group_size)) * scale + bias
+        exps = jnp.exp2(scores - jnp.max(scores, axis=0, keepdims=True))
+        inverse = 1.0 / jnp.sum(exps, axis=0, keepdims=True)
+        self_out = dot_tn(vals, exps.astype(jnp.bfloat16)) * inverse
+        cross_out = dot_tn(values_ref[:, columns], weights_ref[group])
+        merged = (self_out + cross_out).astype(jnp.bfloat16)
+        for c in range(group_size):
+            head = group * group_size + c
+            out_ref[:, head * HD : (head + 1) * HD] = jnp.transpose(
+                merged[:, c * tok_rows : (c + 1) * tok_rows]
+            )
+
+
+def product_kernel(sizes, where_ref, terms_ref, *rest):
+    slots, vision, out_rows, steps = sizes
+    blocks = terms_ref.shape[0]
+    packs, outs = rest[:blocks], rest[blocks : blocks + steps]
+    sum_ref, turned_ref = rest[blocks + steps :]
+    seq_at, dp_at = where_ref[0], where_ref[1]
+    width = packs[0].shape[1]
+    total = terms_ref[0].astype(jnp.float32)
+    for b in range(1, blocks):
+        total = total + terms_ref[b].astype(jnp.float32)
+    sum_ref[...] = total.astype(jnp.bfloat16)
+    grads = jnp.concatenate(
+        [
+            sum_ref[pl.ds(pl.multiple_of((seq_at ^ x) * slots, slots), slots), :]
+            for x in range(blocks)
+        ],
+        axis=0,
+    )
+    for part in range(-(-vision // width)):
+        cut = min(width, vision - part * width)
+        rows = jnp.concatenate(
+            [pack[part * slots : (part + 1) * slots, :cut] for pack in packs], axis=0
+        )
+        turned_ref[part * width : part * width + cut, :] = jnp.transpose(rows)
+    for x in range(steps):
+        row = pl.multiple_of(((dp_at ^ x) * blocks + seq_at) * out_rows, out_rows)
+        block = dot_nn(turned_ref[pl.ds(row, out_rows), :], grads)
+        outs[x][...] = block.astype(outs[x].dtype)
+
+
+def vmem_specs(count):
+    return [pl.BlockSpec(memory_space=pltpu.VMEM)] * count
+
+
+def swap(array, axis, size, x):
+    return lax.ppermute(array, axis, [(i, i ^ x) for i in range(size)])
+
+
+def on_device_small(
+    seq_size,
+    dp_size,
+    q_self,
+    k_self,
+    v_self,
+    docs,
+    q_cross,
+    cotangent,
+    img_keys,
+    features,
+    w_value,
+    tiles,
+    cite,
+):
+    tok_rows = q_self.shape[1]
+    width = k_self.shape[2]
+    kv_local = width // HD
+    heads_local = q_self.shape[2] // HD
+    group_size = heads_local // kv_local
+    slots = img_keys.shape[1]
+    vision = features.shape[2]
+    images = tiles.shape[1]
+    out_rows = vision // (seq_size * dp_size)
+    key_count = slots * seq_size
+    smem = pl.BlockSpec(memory_space=pltpu.SMEM)
+    seq_at = lax.axis_index("seq")
+    dp_at = lax.axis_index("dp")
+    where_at = jnp.stack([seq_at, dp_at]).astype(jnp.int32)
+
+    doc_row = jnp.pad(docs.astype(jnp.bfloat16), ((0, 15), (0, width - tok_rows)))
+    heads_all = lax.all_gather(jnp.concatenate([img_keys[0], doc_row], axis=0), "seq", axis=0)
+
+    parts = -(-vision // width)
+    feature_rows = parts * slots
+    padded = jnp.pad(features[0], ((0, 0), (0, parts * width - vision)))
+    pieces = [padded[:, p * width : (p + 1) * width] for p in range(parts)]
+    packs = [jnp.concatenate(pieces + [k_self[0], v_self[0]], axis=0)]
+    bit = seq_size // 2
+    order = {0: packs[0]}
+    while bit:
+        for x in list(order):
+            order[x ^ bit] = swap(order[x], "seq", seq_size, bit)
+        bit //= 2
+    packs = [order[x] for x in range(seq_size)]
+
+    grad_terms, weights = pl.pallas_call(
+        functools.partial(
+            cross_kernel, (kv_local, group_size, slots, images, key_count // images)
+        ),
+        out_shape=(
+            jax.ShapeDtypeStruct((key_count, width), jnp.bfloat16),
+            jax.ShapeDtypeStruct((kv_local, key_count, group_size * tok_rows), jnp.bfloat16),
+        ),
+        in_specs=[smem, smem] + vmem_specs(4),
+        out_specs=tuple(vmem_specs(2)),
+        compiler_params=pltpu.CompilerParams(vmem_limit_bytes=24 << 20),
+        name="cross",
+    )(tiles, cite, docs, heads_all, q_cross[0], cotangent[0])
+
+    terms_all = lax.all_gather(grad_terms, "seq", axis=0)
+    blocks_out = pl.pallas_call(
+        functools.partial(product_kernel, (slots, vision, out_rows, dp_size)),
+        out_shape=tuple(
+            jax.ShapeDtypeStruct((out_rows, width), jnp.bfloat16 if x else jnp.float32)
+            for x in range(dp_size)
+        ),
+        in_specs=[smem] + vmem_specs(1 + seq_size),
+        out_specs=tuple(vmem_specs(dp_size)),
+        scratch_shapes=[
+            pltpu.VMEM((key_count, width), jnp.bfloat16),
+            pltpu.VMEM((vision, key_count), jnp.bfloat16),
+        ],
+        compiler_params=pltpu.CompilerParams(vmem_limit_bytes=16 << 20),
+        name="product",
+    )(where_at, terms_all, *packs)
+    weight_grad = blocks_out[0]
+    for x in range(1, dp_size):
+        weight_grad = weight_grad + swap(blocks_out[x], "dp", dp_size, x).astype(jnp.float32)
+
+    merged = pl.pallas_call(
+        functools.partial(attend_kernel, (kv_local, group_size, slots, feature_rows)),
+        out_shape=jax.ShapeDtypeStruct((tok_rows, heads_local * HD), jnp.bfloat16),
+        in_specs=[smem] + vmem_specs(5 + seq_size),
+        out_specs=vmem_specs(1)[0],
+        scratch_shapes=[pltpu.VMEM((key_count, width), jnp.bfloat16)],
+        compiler_params=pltpu.CompilerParams(vmem_limit_bytes=32 << 20),
+        name="attend",
+    )(where_at, docs, heads_all, q_self[0], w_value, weights, *packs)
+    return (merged[None], weight_grad)
+
+
+def fits_small(mesh, shapes):
+    seq_size, dp_size = mesh.shape["seq"], mesh.shape["dp"]
+    q_self, k_self, img_keys, features, w_value, cite = shapes
+    tensor = mesh.shape["tensor"]
+    powers = all(n & (n - 1) == 0 for n in (seq_size, dp_size))
+    tok_rows, width = q_self[1] // seq_size, k_self[2] // tensor
+    slots = img_keys[1] // seq_size
+    rows, left = divmod(features[2], seq_size * dp_size)
+    return (
+        powers
+        and seq_size <= 4
+        and dp_size <= 8
+        and tok_rows == HD
+        and tok_rows <= width
+        and slots % 32 == 0
+        and slots * seq_size == HD
+        and left == 0
+        and rows % 16 == 0
+        and features[2] % HD == 0
+        and width % HD == 0
+        and cite[1] <= 256
+    )
+
+
 def solution(mesh):
     in_specs = (
         P("dp", "seq", "tensor"),
@@ -171,6 +448,14 @@
         P("dp", None),
     )
     out_specs = (P("dp", "seq", "tensor"), P(("dp", "seq"), "tensor"))
-    return jax.shard_map(
-        on_device, mesh=mesh, in_specs=in_specs, out_specs=out_specs, check_vma=False
-    )
+
+    def run(*arrays):
+        shapes = [arrays[i].shape for i in (0, 1, 6, 7, 8, 10)]
+        body = on_device_general
+        if fits_small(mesh, shapes):
+            body = functools.partial(on_device_small, mesh.shape["seq"], mesh.shape["dp"])
+        return jax.shard_map(
+            body, mesh=mesh, in_specs=in_specs, out_specs=out_specs, check_vma=False
+        )(*arrays)
+
+    return run

time: 109 us -> 46.6 us (0.43)
  waiting for transfers between devices: 42.2 us -> 10 us
  blocking collectives: 31 us -> 13.2 us
  between operations: 14 us -> 0.68 us
  matrix products: 9.32 us -> 0 us
  starting transfers between devices: 0.12 us -> 7.52 us
  Pallas kernels: 0 us -> 6.45 us
  local copies, waits for them, and re-layouts: 8.77 us -> 6.14 us
    unnamed x6 -> x0, waiting for transfers between devices: 42.2 us -> none
    all_gather x5 -> x2, blocking collectives: 31 us -> 13.2 us  [the longest x1 7.4 us: on_device_small(): terms_all = lax.all_gather(grad_terms, 'seq', axis=0)]
    ppermute x0 -> x6, waiting for transfers between devices: none -> 10 us  [swap(): return lax.ppermute(array, axis, [(i, i ^ x) for i in range(size)])]
    dot_general x6 -> x0, matrix products: 7.78 us -> none  [the longest x1 2.16 us: absorb_block(): jnp.einsum('gcts,sgd->gctd', weights.astype(jnp.bfloat16), value_heads, p...]
    ppermute x0 -> x6, starting transfers between devices: none -> 7.52 us  [swap(): return lax.ppermute(array, axis, [(i, i ^ x) for i in range(size)])]
    pallas_call x0 -> x3, Pallas kernels: none -> 6.45 us  [the longest x1 3.75 us: on_device_small(): pl.pallas_call(functools.partial(attend_kernel, (kv_local, group_size, sl...]
    another operation x3 -> x0, local copies, waits for them, and re-layouts: 3.11 us -> none  [the longest x1 1.4 us: on_device(): cross_q = q_cross[0].reshape(tok_rows, kv_local, group_size, HD)]
    reduce_sum x3 -> x0, other arithmetic: 2.6 us -> none  [the longest x1 1.01 us: absorb_block(): denominator = factor * denominator + jnp.sum(weights, axis=-1)]
  transfers between devices with their start and end apart: 3 -> 6, of which waited for: 3 -> 2; matrix products, arithmetic and copies ran while one was open for 7% -> 3% of each run, Pallas kernels for 0% -> 12%
where the time goes in v1:
time: 46.6 us; the launch traced here: 46.2 us
  blocking collectives  13.2 us (28%)
  waiting for transfers between devices  10 us (21%)
  starting transfers between devices  7.52 us (16%)
  Pallas kernels  6.45 us (14%)
  local copies, waits for them, and re-layouts  6.14 us (13%)
  other arithmetic  2.21 us (5%)
  between operations  0.68 us (1%)
    ppermute x6, waiting for transfers between devices, swap(): return lax.ppermute(array, axis, [(i, i ^ x) for i in range(size)])  10 us
    ppermute x6, starting transfers between devices, swap(): return lax.ppermute(array, axis, [(i, i ^ x) for i in range(size)])  7.52 us
    all_gather x1, blocking collectives, on_device_small(): terms_all = lax.all_gather(grad_terms, 'seq', axis=0)  7.4 us
    all_gather x1, blocking collectives, on_device_small(): lax.all_gather(jnp.concatenate([img_keys[0], doc_row], axis=0), 'seq', ax...  5.78 us
    unnamed x18, local copies, waits for them, and re-layouts  5.22 us
    pallas_call x1, Pallas kernels, on_device_small(): pl.pallas_call(functools.partial(attend_kernel, (kv_local, group_size, sl...  3.75 us
    pallas_call x1, Pallas kernels, on_device_small(): pl.pallas_call(functools.partial(cross_kernel, (kv_local, group_size, slo...  1.75 us
    pallas_call x1, Pallas kernels, on_device_small(): pl.pallas_call(functools.partial(product_kernel, (slots, vision, out_rows...  0.95 us
  transfers between devices with their start and end apart: 6, of which 2 were waited for; matrix products, arithmetic and copies ran while one was open for 3% of the time, Pallas kernels for 12%

profile of v1, /device:TPU:0, one launch (start us, length us, event | category | flops | bytes accessed | tf_op | source)
XLA Modules:
  0.0 46.2 jit_solution(17542076056232487996)
XLA Ops:
  0.6 0.8 %slice_dynamic-update-slice_fusion.1 = bf16[352,512]{1,0:T(8,128)(2,1)S(1)} fusion(bf16[32,1280]{1,0:T(8,128)(2,1)} %bitcast.21), kind=kLoop, calls=%fused_computation.9 | loop fusion | bytes 65536
  1.5 0.8 %slice_dynamic-update-slice_fusion = bf16[352,512]{1,0:T(8,128)(2,1)S(1)} fusion(bf16[352,512]{1,0:T(8,128)(2,1)S(1)} %slice_dynamic-update-slice_fusion.1, bf16[32,1280]{1,0:T(8,128)(2,1)} %bitcast.22), kind=kLoop, calls=%fused_computation.8 | loop fusion | bytes 65536
  2.3 0.7 %fusion.2 = bf16[352,512]{1,0:T(8,128)(2,1)S(1)} fusion(bf16[352,512]{1,0:T(8,128)(2,1)S(1)} %slice_dynamic-update-slice_fusion, bf16[32,1280]{1,0:T(8,128)(2,1)} %bitcast.23), kind=kLoop, calls=%fused_computation.7 | loop fusion | bytes 114688
  3.0 0.9 %bitcast_dynamic-update-slice_fusion.1 = bf16[352,512]{1,0:T(8,128)(2,1)S(1)} fusion(bf16[352,512]{1,0:T(8,128)(2,1)S(1)} %fusion.2, bf16[1,128,512]{2,1,0:T(8,128)(2,1)} %param.12), kind=kLoop, calls=%fused_computation.2 | loop fusion | bytes 262144
  3.9 0.9 %bitcast_dynamic-update-slice_fusion.rest_0_ = bf16[352,512]{1,0:T(8,128)(2,1)S(1)} fusion(bf16[352,512]{1,0:T(8,128)(2,1)S(1)} %bitcast_dynamic-update-slice_fusion.1, bf16[1,128,512]{2,1,0:T(8,128)(2,1)} %param.13), kind=kLoop, calls=%fused_computation.1 | loop fusion | bytes 262144 | tf_op jit(solution)/shard_map/concatenate | solution.py:357
  4.8 3.1 %collective-permute-start.1 = (bf16[352,512]{1,0:T(8,128)(2,1)S(1)}, bf16[352,512]{1,0:T(8,128)(2,1)S(1)}, u32[]{:S(2)}, u32[]{:S(2)}) collective-permute-start(bf16[352,512]{1,0:T(8,128)(2,1)S(1)} %bitcast_dynamic-update-slice_fusion.rest_0_), channel_id=1, source_target_pairs={{0,4},{2,6},{4,0},{6,2},{1,5},{3,7},{5,1},{7,3},{8,12},{10,14},{12... | collective-permute-start | bytes 1081352 | tf_op jit(solution)/shard_map/ppermute | solution.py:317
  7.9 0.7 %convert_element_type.16 = bf16[1,128]{1,0:T(2,128)(2,1)S(1)} convert(s32[1,128]{1,0:T(1,128)} %docs_ref.3) | non-fusion elementwise | flops 128 | bytes 768 | tf_op jit(solution)/shard_map/convert_element_type | solution.py:350
  8.5 0.8 %fusion.1 = bf16[48,512]{1,0:T(8,128)(2,1)S(1)} fusion(bf16[1,128]{1,0:T(2,128)(2,1)S(1)} %convert_element_type.16, bf16[32,512]{1,0:T(8,128)(2,1)} %bitcast.24), kind=kLoop, calls=%fused_computation.6 | loop fusion | flops 147456 | bytes 82176 | tf_op jit(solution)/shard_map/concatenate | solution.py:351
  9.3 7.0 %collective-permute-done.1.rest_2_ = bf16[352,512]{1,0:T(8,128)(2,1)S(1)} collective-permute-done((bf16[352,512]{1,0:T(8,128)(2,1)S(1)}, bf16[352,512]{1,0:T(8,128)(2,1)S(1)}, u32[]{:S(2)}, u32[]{:S(2)}) %collective-permute-start.1) | collective-permute-done | bytes 360480 | tf_op jit(solution)/shard_map/ppermute | solution.py:317
  16.3 0.0 collective-permute-start.2
  16.3 5.8 %all-gather = bf16[192,512]{1,0:T(8,128)(2,1)S(1)} all-gather(bf16[48,512]{1,0:T(8,128)(2,1)S(1)} %fusion.1), channel_id=2, replica_groups=mesh['dp'=4,'seq'=4,'tensor'=2] {'seq'}, dimensions={0}, use_global_device_ids=true | all-gather | bytes 245760 | tf_op jit(solution)/shard_map/all_gather | solution.py:351
  22.1 0.7 %copy-done.4 = s32[1,128]{1,0:T(1,128)S(1)} copy-done((s32[1,128]{1,0:T(1,128)S(1)}, s32[1,128]{1,0:T(1,128)}, u32[]{:S(2)}) %copy-start.4) | copy-done | bytes 536
  22.7 0.7 %copy-done.5 = s32[1,4]{1,0:T(1,128)S(1)} copy-done((s32[1,4]{1,0:T(1,128)S(1)}, s32[1,4]{1,0:T(1,128)}, u32[]{:S(2)}) %copy-start.5) | copy-done | bytes 40
  23.4 0.7 %copy-done.6 = s32[1,4]{1,0:T(1,128)S(1)} copy-done((s32[1,4]{1,0:T(1,128)S(1)}, s32[1,4]{1,0:T(1,128)}, u32[]{:S(2)}) %copy-start.6) | copy-done | bytes 40
  24.0 1.8 %cross.1 = (bf16[128,512]{1,0:T(8,128)(2,1)S(1)}, bf16[4,128,512]{2,1,0:T(8,128)(2,1)S(1)}) custom-call(s32[1,4]{1,0:T(1,128)S(1)} %copy-done.5, s32[1,4]{1,0:T(1,128)S(1)} %copy-done.6, s32[1,128]{1,0:T(1,128)S(1)} %copy-done.4, bf16[4,48,512]{2,1,0:T(8,128)(2,1)S(1)} %bitcast.15, bf16[128,2048]{1,0:T(8,128)(2,1)S(1)} %bitcast.18, ...), custom_call_target="tpu_custom_call" | custom-call | tf_op jit(solution)/shard_map/cross/pallas_call | solution.py:366
  25.8 0.1 pad_add_fusion.where_ref
  25.9 7.4 %all-gather.1 = bf16[512,512]{1,0:T(8,128)(2,1)S(1)} all-gather(bf16[128,512]{1,0:T(8,128)(2,1)S(1)} %get-tuple-element.9), channel_id=3, replica_groups=mesh['dp'=4,'seq'=4,'tensor'=2] {'seq'}, dimensions={0}, use_global_device_ids=true | all-gather | bytes 655360 | tf_op jit(solution)/shard_map/all_gather | solution.py:380
  33.3 1.0 %product.1 = (f32[80,512]{1,0:T(8,128)S(1)}, bf16[80,512]{1,0:T(8,128)(2,1)S(1)}, bf16[80,512]{1,0:T(8,128)(2,1)S(1)}, bf16[80,512]{1,0:T(8,128)(2,1)S(1)}) custom-call(s32[2]{0:T(128)S(1)} %pad_add_fusion.where_ref, bf16[4,128,512]{2,1,0:T(8,128)(2,1)S(1)} %bitcast.14, bf16[352,512]{1,0:T(8,128)(2,1)S(1)} %bitcast_dynamic-update-slice_fusion.rest_0_, ...), custom_call_target="tpu_custom_call" | custom-call | tf_op jit(solution)/shard_map/product/pallas_call | solution.py:381
  34.3 1.7 %collective-permute-start.3 = (bf16[80,512]{1,0:T(8,128)(2,1)S(1)}, bf16[80,512]{1,0:T(8,128)(2,1)S(1)}, u32[]{:S(2)}, u32[]{:S(2)}) collective-permute-start(bf16[80,512]{1,0:T(8,128)(2,1)S(1)} %get-tuple-element.11), channel_id=1, source_target_pairs={{0,8},{8,0},{16,24},{24,16},{1,9},{9,1},{17,25},{25,17},{2,10},{10... | collective-permute-start | bytes 245768 | tf_op jit(solution)/shard_map/ppermute | solution.py:317
  36.0 2.6 %collective-permute-start.4 = (bf16[80,512]{1,0:T(8,128)(2,1)S(1)}, bf16[80,512]{1,0:T(8,128)(2,1)S(1)}, u32[]{:S(2)}, u32[]{:S(2)}) collective-permute-start(bf16[80,512]{1,0:T(8,128)(2,1)S(1)} %get-tuple-element.12), channel_id=1, source_target_pairs={{0,16},{8,24},{16,0},{24,8},{1,17},{9,25},{17,1},{25,9},{2,18},{10... | collective-permute-start | bytes 245768 | tf_op jit(solution)/shard_map/ppermute | solution.py:317
  38.6 0.1 collective-permute-start.5
  38.7 3.7 %attend.1 = bf16[128,2048]{1,0:T(8,128)(2,1)} custom-call(s32[2]{0:T(128)S(1)} %pad_add_fusion.where_ref, s32[1,128]{1,0:T(1,128)S(1)} %copy-done.4, bf16[4,48,512]{2,1,0:T(8,128)(2,1)S(1)} %bitcast.16, bf16[128,2048]{1,0:T(8,128)(2,1)S(1)} %bitcast.17, bf16[1280,512]{1,0:T(8,128)(2,1)S(1)} %copy-done, ...), custom_call_target="tpu_custom_call" | custom-call | tf_op jit(solution)/shard_map/attend/pallas_call | solution.py:400
  42.5 3.0 %collective-permute-done.4 = bf16[80,512]{1,0:T(8,128)(2,1)S(1)} collective-permute-done((bf16[80,512]{1,0:T(8,128)(2,1)S(1)}, bf16[80,512]{1,0:T(8,128)(2,1)S(1)}, u32[]{:S(2)}, u32[]{:S(2)}) %collective-permute-start.4) | collective-permute-done | bytes 81952 | tf_op jit(solution)/shard_map/ppermute | solution.py:317
  45.5 0.7 %convert_add_fusion = f32[80,512]{1,0:T(8,128)} fusion(bf16[80,512]{1,0:T(8,128)(2,1)S(1)} %collective-permute-done.5, bf16[80,512]{1,0:T(8,128)(2,1)S(1)} %collective-permute-done.4, f32[80,512]{1,0:T(8,128)S(1)} %get-tuple-element.10, bf16[80,512]{1,0:T(8,128)(2,1)S(1)} %collective-permute-done.3), kind=kLoop, calls=%fused_computation | loop fusion | flops 245760 | bytes 573440 | tf_op jit(solution)/shard_map/add | solution.py:398
  (16 shorter events, 0.0 us)
Async XLA Ops:
  0.6 21.4 %copy-start.3 = (bf16[1,128,2048]{2,1,0:T(8,128)(2,1)S(1)}, bf16[1,128,2048]{2,1,0:T(8,128)(2,1)}, u32[]{:S(2)}) copy-start(bf16[1,128,2048]{2,1,0:T(8,128)(2,1)} %param.16) | copy-start | bytes 1572868
  0.6 21.4 %copy-start.2 = (bf16[1,128,2048]{2,1,0:T(8,128)(2,1)S(1)}, bf16[1,128,2048]{2,1,0:T(8,128)(2,1)}, u32[]{:S(2)}) copy-start(bf16[1,128,2048]{2,1,0:T(8,128)(2,1)} %param.15) | copy-start | bytes 1572868
  4.8 11.5 %collective-permute-start.1 = (bf16[352,512]{1,0:T(8,128)(2,1)S(1)}, bf16[352,512]{1,0:T(8,128)(2,1)S(1)}, u32[]{:S(2)}, u32[]{:S(2)}) collective-permute-start(bf16[352,512]{1,0:T(8,128)(2,1)S(1)} %bitcast_dynamic-update-slice_fusion.rest_0_), channel_id=1, source_target_pairs={{0,4},{2,6},{4,0},{6,2},{1,5},{3,7},{5,1},{7,3},{8,12},{10,14},{12... | collective-permute-start | bytes 1081352 | tf_op jit(solution)/shard_map/ppermute | solution.py:317
  7.9 25.4 %collective-permute-start = (bf16[352,512]{1,0:T(8,128)(2,1)S(1)}, bf16[352,512]{1,0:T(8,128)(2,1)S(1)}, u32[]{:S(2)}, u32[]{:S(2)}) collective-permute-start(bf16[352,512]{1,0:T(8,128)(2,1)S(1)} %bitcast_dynamic-update-slice_fusion.rest_0_), channel_id=1, source_target_pairs={{0,2},{2,0},{4,6},{6,4},{1,3},{3,1},{5,7},{7,5},{8,10},{10,8},{12,... | collective-permute-start | bytes 1081352 | tf_op jit(solution)/shard_map/ppermute | solution.py:317
  16.3 17.0 %collective-permute-start.2 = (bf16[352,512]{1,0:T(8,128)(2,1)S(1)}, bf16[352,512]{1,0:T(8,128)(2,1)S(1)}, u32[]{:S(2)}, u32[]{:S(2)}) collective-permute-start(bf16[352,512]{1,0:T(8,128)(2,1)S(1)} %collective-permute-done.1.rest_2_), channel_id=1, source_target_pairs={{0,2},{2,0},{4,6},{6,4},{1,3},{3,1},{5,7},{7,5},{8,10},{10,8},{12,... | collective-permute-start | bytes 1081352 | tf_op jit(solution)/shard_map/ppermute | solution.py:317
  22.1 0.7 %copy-start.4 = (s32[1,128]{1,0:T(1,128)S(1)}, s32[1,128]{1,0:T(1,128)}, u32[]{:S(2)}) copy-start(s32[1,128]{1,0:T(1,128)} %docs_ref.3) | copy-start | bytes 1540
  22.7 0.7 %copy-start.5 = (s32[1,4]{1,0:T(1,128)S(1)}, s32[1,4]{1,0:T(1,128)}, u32[]{:S(2)}) copy-start(s32[1,4]{1,0:T(1,128)} %tiles_ref.1) | copy-start | bytes 52
  23.4 0.7 %copy-start.6 = (s32[1,4]{1,0:T(1,128)S(1)}, s32[1,4]{1,0:T(1,128)}, u32[]{:S(2)}) copy-start(s32[1,4]{1,0:T(1,128)} %cite_ref.1) | copy-start | bytes 52
  25.9 12.8 %copy-start = (bf16[1280,512]{1,0:T(8,128)(2,1)S(1)}, bf16[1280,512]{1,0:T(8,128)(2,1)}, u32[]{:S(2)}) copy-start(bf16[1280,512]{1,0:T(8,128)(2,1)} %w_ref.1) | copy-start | bytes 3932164
  25.9 12.8 %copy-start.1 = (bf16[1,128,2048]{2,1,0:T(8,128)(2,1)S(1)}, bf16[1,128,2048]{2,1,0:T(8,128)(2,1)}, u32[]{:S(2)}) copy-start(bf16[1,128,2048]{2,1,0:T(8,128)(2,1)} %param.11) | copy-start | bytes 1572868
  34.3 8.2 %collective-permute-start.3 = (bf16[80,512]{1,0:T(8,128)(2,1)S(1)}, bf16[80,512]{1,0:T(8,128)(2,1)S(1)}, u32[]{:S(2)}, u32[]{:S(2)}) collective-permute-start(bf16[80,512]{1,0:T(8,128)(2,1)S(1)} %get-tuple-element.11), channel_id=1, source_target_pairs={{0,8},{8,0},{16,24},{24,16},{1,9},{9,1},{17,25},{25,17},{2,10},{10... | collective-permute-start | bytes 245768 | tf_op jit(solution)/shard_map/ppermute | solution.py:317
  36.0 9.5 %collective-permute-start.4 = (bf16[80,512]{1,0:T(8,128)(2,1)S(1)}, bf16[80,512]{1,0:T(8,128)(2,1)S(1)}, u32[]{:S(2)}, u32[]{:S(2)}) collective-permute-start(bf16[80,512]{1,0:T(8,128)(2,1)S(1)} %get-tuple-element.12), channel_id=1, source_target_pairs={{0,16},{8,24},{16,0},{24,8},{1,17},{9,25},{17,1},{25,9},{2,18},{10... | collective-permute-start | bytes 245768 | tf_op jit(solution)/shard_map/ppermute | solution.py:317
  38.6 6.9 %collective-permute-start.5 = (bf16[80,512]{1,0:T(8,128)(2,1)S(1)}, bf16[80,512]{1,0:T(8,128)(2,1)S(1)}, u32[]{:S(2)}, u32[]{:S(2)}) collective-permute-start(bf16[80,512]{1,0:T(8,128)(2,1)S(1)} %get-tuple-element.13), channel_id=1, source_target_pairs={{0,24},{8,16},{16,8},{24,0},{1,25},{9,17},{17,9},{25,1},{2,26},{10... | collective-permute-start | bytes 245768 | tf_op jit(solution)/shard_map/ppermute | solution.py:317

commit v2 on v1

--- a/solution.py
+++ b/solution.py
@@ -7,6 +7,7 @@
 from jax.experimental import pallas as pl
 from jax.experimental.pallas import tpu as pltpu
 from jax.sharding import PartitionSpec as P
+
 
 HD = 128
 TILE_TOK = 8
@@ -88,7 +89,7 @@
             None,
         )
 
-    running_max, denominator, numerator = lax.scan(
+    _, denominator, numerator = lax.scan(
         absorb_step, start_state, (key_blocks, value_blocks, doc_blocks, pos_blocks)
     )[0]
     self_out = numerator / denominator[..., None]
@@ -185,23 +186,86 @@
     )
 
 
-def cross_kernel(
-    sizes, tiles_ref, cite_ref, docs_ref, head_ref, q_ref, cot_ref, grad_ref, weights_ref
+def pack_kernel(
+    sizes,
+    docs_hbm,
+    tiles_hbm,
+    cite_hbm,
+    img_hbm,
+    features_hbm,
+    k_hbm,
+    v_hbm,
+    head_ref,
+    pack_ref,
+    meta_ref,
+    docs_ref,
+    tiles_ref,
+    cite_ref,
+    sems,
 ):
-    kv_local, group_size, slots, images, slot_count = sizes
-    blocks = head_ref.shape[0]
-    key_count = blocks * slots
+    slots, parts, slot_count = sizes
+    tok_rows = docs_ref.shape[1]
+    width = pack_ref.shape[1]
+    vision = features_hbm.shape[2]
+    feature_rows = parts * slots
+    pairs = [
+        (docs_hbm, docs_ref),
+        (tiles_hbm, tiles_ref),
+        (cite_hbm, cite_ref),
+        (img_hbm.at[0], head_ref.at[pl.ds(0, slots), :]),
+        (k_hbm.at[0], pack_ref.at[pl.ds(feature_rows, tok_rows), :]),
+        (v_hbm.at[0], pack_ref.at[pl.ds(feature_rows + tok_rows, tok_rows), :]),
+    ]
+    for part in range(parts):
+        cut = min(width, vision - part * width)
+        pairs.append(
+            (
+                features_hbm.at[0, :, pl.ds(part * width, cut)],
+                pack_ref.at[pl.ds(part * slots, slots), pl.ds(0, cut)],
+            )
+        )
+    copies = [
+        pltpu.make_async_copy(source, target, sems.at[n])
+        for n, (source, target) in enumerate(pairs)
+    ]
+    for copy in copies:
+        copy.start()
+    for copy in copies[:3]:
+        copy.wait()
     docs = docs_ref[...]
-    tok_rows = docs.shape[1]
     image_of = jnp.zeros_like(docs)
     for doc in range(cite_ref.shape[1]):
         image_of = jnp.where(docs == doc, cite_ref[0, doc], image_of)
+    count = jnp.zeros_like(docs)
+    for image in range(tiles_ref.shape[1]):
+        count = jnp.where(image_of == image, tiles_ref[0, image] * TILE_TOK, count)
+    first = image_of * slot_count
+    row = lax.broadcasted_iota(jnp.int32, meta_ref.shape, 0)
+    meta_ref[...] = jnp.where(
+        row == 0, docs, jnp.where(row == 1, first, jnp.where(row == 2, first + count, 0))
+    )
+    extra = head_ref.shape[0] - slots
+    doc_rows = jnp.broadcast_to(docs.astype(jnp.float32), (extra, tok_rows))
+    head_ref[slots:, :tok_rows] = doc_rows.astype(jnp.bfloat16)
+    if width > tok_rows:
+        head_ref[slots:, tok_rows:] = jnp.zeros((extra, width - tok_rows), jnp.bfloat16)
+    for copy in copies[3:]:
+        copy.wait()
+    last = vision - (parts - 1) * width
+    if last < width:
+        pack_ref[(parts - 1) * slots : feature_rows, last:] = jnp.zeros(
+            (slots, width - last), jnp.bfloat16
+        )
+
+
+def cross_kernel(sizes, meta_ref, head_ref, q_ref, cot_ref, grad_ref, weights_ref):
+    kv_local, group_size, slots = sizes
+    blocks = head_ref.shape[0]
+    key_count = blocks * slots
+    tok_rows = q_ref.shape[0]
     slot_ids = lax.broadcasted_iota(jnp.int32, (key_count, tok_rows), 0)
-    bias = jnp.full((key_count, tok_rows), MASK_FILL, jnp.float32)
-    for image in range(images):
-        first = image * slot_count
-        usable = (slot_ids >= first) & (slot_ids < first + tiles_ref[0, image] * TILE_TOK)
-        bias = jnp.where(usable & (image_of == image), 0.0, bias)
+    kept = (slot_ids >= meta_ref[1:2, :]) & (slot_ids < meta_ref[2:3, :])
+    bias = jnp.where(kept, 0.0, MASK_FILL)
     bias = jnp.concatenate([bias] * group_size, axis=1)
     scale = HD ** (-0.5) * LOG2E
     for group in range(kv_local):
@@ -217,7 +281,7 @@
         )
 
 
-def attend_kernel(sizes, where_ref, docs_ref, head_ref, q_ref, w_ref, weights_ref, *rest):
+def attend_kernel(sizes, where_ref, meta_ref, head_ref, q_ref, w_ref, weights_ref, *rest):
     kv_local, group_size, slots, feature_rows = sizes
     blocks = head_ref.shape[0]
     packs, out_ref, values_ref = rest[:blocks], rest[blocks], rest[blocks + 1]
@@ -239,7 +303,7 @@
     for x in range(blocks):
         owner = pl.multiple_of((seq_at ^ x) * slots, slots)
         values_ref[pl.ds(owner, slots), :] = values[x * slots : (x + 1) * slots]
-    docs = docs_ref[...].astype(jnp.float32)
+    docs = meta_ref[0:1, :].astype(jnp.float32)
     start = jnp.zeros((1, tok_rows), jnp.float32)
     for b in range(blocks):
         row = head_ref[b, slots : slots + 16, :tok_rows].astype(jnp.float32)[0:1]
@@ -343,20 +407,33 @@
     out_rows = vision // (seq_size * dp_size)
     key_count = slots * seq_size
     smem = pl.BlockSpec(memory_space=pltpu.SMEM)
-    seq_at = lax.axis_index("seq")
-    dp_at = lax.axis_index("dp")
-    where_at = jnp.stack([seq_at, dp_at]).astype(jnp.int32)
-
-    doc_row = jnp.pad(docs.astype(jnp.bfloat16), ((0, 15), (0, width - tok_rows)))
-    heads_all = lax.all_gather(jnp.concatenate([img_keys[0], doc_row], axis=0), "seq", axis=0)
-
+    hbm = pl.BlockSpec(memory_space=pltpu.HBM)
+    where_at = jnp.stack([lax.axis_index("seq"), lax.axis_index("dp")]).astype(jnp.int32)
     parts = -(-vision // width)
     feature_rows = parts * slots
-    padded = jnp.pad(features[0], ((0, 0), (0, parts * width - vision)))
-    pieces = [padded[:, p * width : (p + 1) * width] for p in range(parts)]
-    packs = [jnp.concatenate(pieces + [k_self[0], v_self[0]], axis=0)]
+
+    head, own, meta = pl.pallas_call(
+        functools.partial(pack_kernel, (slots, parts, key_count // images)),
+        out_shape=(
+            jax.ShapeDtypeStruct((slots + 16, width), jnp.bfloat16),
+            jax.ShapeDtypeStruct((feature_rows + 2 * tok_rows, width), jnp.bfloat16),
+            jax.ShapeDtypeStruct((8, tok_rows), jnp.int32),
+        ),
+        in_specs=[hbm] * 7,
+        out_specs=tuple(vmem_specs(3)),
+        scratch_shapes=[
+            pltpu.VMEM(docs.shape, jnp.int32),
+            pltpu.SMEM(tiles.shape, jnp.int32),
+            pltpu.SMEM(cite.shape, jnp.int32),
+            pltpu.SemaphoreType.DMA((6 + parts,)),
+        ],
+        compiler_params=pltpu.CompilerParams(vmem_limit_bytes=8 << 20),
+        cost_estimate=pl.CostEstimate(flops=4 << 30, bytes_accessed=16 << 20, transcendentals=0),
+        name="pack",
+    )(*[pltpu.with_memory_space_constraint(a, pltpu.HBM) for a in (docs, tiles, cite, img_keys, features, k_self, v_self)])
+    heads_all = lax.all_gather(head, "seq", axis=0)
     bit = seq_size // 2
-    order = {0: packs[0]}
+    order = {0: own}
     while bit:
         for x in list(order):
             order[x ^ bit] = swap(order[x], "seq", seq_size, bit)
@@ -364,19 +441,16 @@
     packs = [order[x] for x in range(seq_size)]
 
     grad_terms, weights = pl.pallas_call(
-        functools.partial(
-            cross_kernel, (kv_local, group_size, slots, images, key_count // images)
-        ),
+        functools.partial(cross_kernel, (kv_local, group_size, slots)),
         out_shape=(
             jax.ShapeDtypeStruct((key_count, width), jnp.bfloat16),
             jax.ShapeDtypeStruct((kv_local, key_count, group_size * tok_rows), jnp.bfloat16),
         ),
-        in_specs=[smem, smem] + vmem_specs(4),
+        in_specs=vmem_specs(4),
         out_specs=tuple(vmem_specs(2)),
         compiler_params=pltpu.CompilerParams(vmem_limit_bytes=24 << 20),
         name="cross",
-    )(tiles, cite, docs, heads_all, q_cross[0], cotangent[0])
-
+    )(meta, heads_all, q_cross[0], cotangent[0])
     terms_all = lax.all_gather(grad_terms, "seq", axis=0)
     blocks_out = pl.pallas_call(
         functools.partial(product_kernel, (slots, vision, out_rows, dp_size)),
@@ -393,9 +467,12 @@
         compiler_params=pltpu.CompilerParams(vmem_limit_bytes=16 << 20),
         name="product",
     )(where_at, terms_all, *packs)
+    arrived = []
+    for x in range(dp_size - 1, 0, -1):
+        arrived.append(swap(blocks_out[x], "dp", dp_size, x))
     weight_grad = blocks_out[0]
-    for x in range(1, dp_size):
-        weight_grad = weight_grad + swap(blocks_out[x], "dp", dp_size, x).astype(jnp.float32)
+    for block in arrived:
+        weight_grad = weight_grad + block.astype(jnp.float32)
 
     merged = pl.pallas_call(
         functools.partial(attend_kernel, (kv_local, group_size, slots, feature_rows)),
@@ -405,13 +482,13 @@
         scratch_shapes=[pltpu.VMEM((key_count, width), jnp.bfloat16)],
         compiler_params=pltpu.CompilerParams(vmem_limit_bytes=32 << 20),
         name="attend",
-    )(where_at, docs, heads_all, q_self[0], w_value, weights, *packs)
+    )(where_at, meta, heads_all, q_self[0], w_value, weights, *packs)
     return (merged[None], weight_grad)
 
 
 def fits_small(mesh, shapes):
     seq_size, dp_size = mesh.shape["seq"], mesh.shape["dp"]
-    q_self, k_self, img_keys, features, w_value, cite = shapes
+    q_self, k_self, img_keys, features, _, cite = shapes
     tensor = mesh.shape["tensor"]
     powers = all(n & (n - 1) == 0 for n in (seq_size, dp_size))
     tok_rows, width = q_self[1] // seq_size, k_self[2] // tensor

time: 46.6 us -> 40.8 us (0.88)
  local copies, waits for them, and re-layouts: 6.14 us -> 0.02 us
  other arithmetic: 2.21 us -> 0.79 us
  waiting for transfers between devices: 10 us -> 11.3 us
  Pallas kernels: 6.45 us -> 7.07 us
    unnamed x18 -> x8, local copies, waits for them, and re-layouts: 5.22 us -> 0.02 us
    ppermute x6, waiting for transfers between devices: 10 us -> 11.3 us  [swap(): return lax.ppermute(array, axis, [(i, i ^ x) for i in range(size)])]
    pallas_call x0 -> x1, Pallas kernels: none -> 1.17 us  [on_device_small(): pl.pallas_call(functools.partial(pack_kernel, (slots, parts, key_count //...]
    concatenate x1 -> x0, local copies, waits for them, and re-layouts: 0.92 us -> none  [on_device_small(): packs = [jnp.concatenate(pieces + [k_self[0], v_self[0]], axis=0)]]
    concatenate x1 -> x0, other arithmetic: 0.76 us -> none  [on_device_small(): jnp.concatenate([img_keys[0], doc_row], axis=0)]
    convert_element_type x1 -> x0, other arithmetic: 0.66 us -> none  [on_device_small(): docs.astype(jnp.bfloat16)]
    pallas_call x1, Pallas kernels: 1.75 us -> 1.21 us  [on_device_small(): pl.pallas_call(functools.partial(cross_kernel, (kv_local, group_size, slo...]
  transfers between devices with their start and end apart: 6 -> 6, of which waited for: 2 -> 2; matrix products, arithmetic and copies ran while one was open for 3% -> 0% of each run, Pallas kernels for 12% -> 12%
where the time goes in v2:
time: 40.8 us; the launch traced here: 40.6 us
  blocking collectives  13.2 us (32%)
  waiting for transfers between devices  11.3 us (28%)
  starting transfers between devices  7.52 us (18%)
  Pallas kernels  7.07 us (17%)
  other arithmetic  0.79 us (2%)
  between operations  0.68 us (2%)
    ppermute x6, waiting for transfers between devices, swap(): return lax.ppermute(array, axis, [(i, i ^ x) for i in range(size)])  11.3 us
    ppermute x6, starting transfers between devices, swap(): return lax.ppermute(array, axis, [(i, i ^ x) for i in range(size)])  7.52 us
    all_gather x1, blocking collectives, on_device_small(): terms_all = lax.all_gather(grad_terms, 'seq', axis=0)  7.4 us
    all_gather x1, blocking collectives, on_device_small(): heads_all = lax.all_gather(head, 'seq', axis=0)  5.78 us
    pallas_call x1, Pallas kernels, on_device_small(): pl.pallas_call(functools.partial(attend_kernel, (kv_local, group_size, sl...  3.74 us
    pallas_call x1, Pallas kernels, on_device_small(): pl.pallas_call(functools.partial(cross_kernel, (kv_local, group_size, slo...  1.21 us
    pallas_call x1, Pallas kernels, on_device_small(): pl.pallas_call(functools.partial(pack_kernel, (slots, parts, key_count //...  1.17 us
    pallas_call x1, Pallas kernels, on_device_small(): pl.pallas_call(functools.partial(product_kernel, (slots, vision, out_rows...  0.95 us
  transfers between devices with their start and end apart: 6, of which 2 were waited for; matrix products, arithmetic and copies ran while one was open for 0% of the time, Pallas kernels for 12%

profile of v2, /device:TPU:0, one launch (start us, length us, event | category | flops | bytes accessed | tf_op | source)
XLA Modules:
  0.0 40.6 jit_solution(1137259969634162287)
XLA Ops:
  0.6 0.0 copy-start.2
  0.6 0.0 copy-start.1
  0.7 1.2 %pack.1 = (bf16[48,512]{1,0:T(8,128)(2,1)S(1)}, bf16[352,512]{1,0:T(8,128)(2,1)S(1)}, s32[8,128]{1,0:T(8,128)S(1)}) custom-call(s32[1,128]{1,0:T(1,128)} %docs_hbm.1, s32[1,4]{1,0:T(1,128)} %tiles_hbm.1, s32[1,4]{1,0:T(1,128)} %cite_hbm.1, bf16[1,32,512]{2,1,0:T(8,128)(2,1)} %img_hbm.1, bf16[1,32,1280]{2,1,0:T(8,128)(2,1)} %features_hbm.1, ...), custom_call_target="tpu_custom_call" | custom-call | flops 4294967296 | bytes 16777216 | tf_op jit(solution)/shard_map/pack/pallas_call | solution.py:415
  1.8 3.1 %collective-permute-start.1 = (bf16[352,512]{1,0:T(8,128)(2,1)S(1)}, bf16[352,512]{1,0:T(8,128)(2,1)S(1)}, u32[]{:S(2)}, u32[]{:S(2)}) collective-permute-start(bf16[352,512]{1,0:T(8,128)(2,1)S(1)} %get-tuple-element.14.rest_0_), channel_id=1, source_target_pairs={{0,4},{2,6},{4,0},{6,2},{1,5},{3,7},{5,1},{7,3},{8,12},{10,14},{12... | collective-permute-start | bytes 1081352 | tf_op jit(solution)/shard_map/ppermute | solution.py:381
  4.9 0.0 collective-permute-start
  4.9 8.4 %collective-permute-done.1.rest_2_ = bf16[352,512]{1,0:T(8,128)(2,1)S(1)} collective-permute-done((bf16[352,512]{1,0:T(8,128)(2,1)S(1)}, bf16[352,512]{1,0:T(8,128)(2,1)S(1)}, u32[]{:S(2)}, u32[]{:S(2)}) %collective-permute-start.1) | collective-permute-done | bytes 360480 | tf_op jit(solution)/shard_map/ppermute | solution.py:381
  13.3 0.0 collective-permute-start.2
  13.3 5.8 %all-gather = bf16[192,512]{1,0:T(8,128)(2,1)S(1)} all-gather(bf16[48,512]{1,0:T(8,128)(2,1)S(1)} %get-tuple-element.12), channel_id=2, replica_groups=mesh['dp'=4,'seq'=4,'tensor'=2] {'seq'}, dimensions={0}, use_global_device_ids=true | all-gather | bytes 245760 | tf_op jit(solution)/shard_map/all_gather | solution.py:434
  19.1 0.0 copy-done.2
  19.1 0.0 copy-done.1
  19.1 1.2 %cross.1 = (bf16[128,512]{1,0:T(8,128)(2,1)S(1)}, bf16[4,128,512]{2,1,0:T(8,128)(2,1)S(1)}) custom-call(s32[8,128]{1,0:T(8,128)S(1)} %get-tuple-element.11.meta_ref, bf16[4,48,512]{2,1,0:T(8,128)(2,1)S(1)} %bitcast.9, bf16[128,2048]{1,0:T(8,128)(2,1)S(1)} %bitcast.11, bf16[128,2048]{1,0:T(8,128)(2,1)S(1)} %bitcast.12), custom_call_target="tpu_custom_call" | custom-call | tf_op jit(solution)/shard_map/cross/pallas_call | solution.py:443
  20.3 0.1 pad_add_fusion.where_ref
  20.4 7.4 %all-gather.1 = bf16[512,512]{1,0:T(8,128)(2,1)S(1)} all-gather(bf16[128,512]{1,0:T(8,128)(2,1)S(1)} %get-tuple-element.15), channel_id=3, replica_groups=mesh['dp'=4,'seq'=4,'tensor'=2] {'seq'}, dimensions={0}, use_global_device_ids=true | all-gather | bytes 655360 | tf_op jit(solution)/shard_map/all_gather | solution.py:454
  27.8 0.0 collective-permute-done.rest_1_
  27.8 0.0 collective-permute-done.2.rest_3_
  27.8 1.0 %product.1 = (f32[80,512]{1,0:T(8,128)S(1)}, bf16[80,512]{1,0:T(8,128)(2,1)S(1)}, bf16[80,512]{1,0:T(8,128)(2,1)S(1)}, bf16[80,512]{1,0:T(8,128)(2,1)S(1)}) custom-call(s32[2]{0:T(128)S(1)} %pad_add_fusion.where_ref, bf16[4,128,512]{2,1,0:T(8,128)(2,1)S(1)} %bitcast.8, bf16[352,512]{1,0:T(8,128)(2,1)S(1)} %get-tuple-element.14.rest_0_, ...), custom_call_target="tpu_custom_call" | custom-call | tf_op jit(solution)/shard_map/product/pallas_call | solution.py:455
  28.8 3.7 %collective-permute-start.3 = (bf16[80,512]{1,0:T(8,128)(2,1)S(1)}, bf16[80,512]{1,0:T(8,128)(2,1)S(1)}, u32[]{:S(2)}, u32[]{:S(2)}) collective-permute-start(bf16[80,512]{1,0:T(8,128)(2,1)S(1)} %get-tuple-element.17), channel_id=1, source_target_pairs={{0,24},{8,16},{16,8},{24,0},{1,25},{9,17},{17,9},{25,1},{2,26},{10... | collective-permute-start | bytes 245768 | tf_op jit(solution)/shard_map/ppermute | solution.py:381
  32.5 0.0 collective-permute-start.4
  32.5 0.7 %collective-permute-start.5 = (bf16[80,512]{1,0:T(8,128)(2,1)S(1)}, bf16[80,512]{1,0:T(8,128)(2,1)S(1)}, u32[]{:S(2)}, u32[]{:S(2)}) collective-permute-start(bf16[80,512]{1,0:T(8,128)(2,1)S(1)} %get-tuple-element.19), channel_id=1, source_target_pairs={{0,8},{8,0},{16,24},{24,16},{1,9},{9,1},{17,25},{25,17},{2,10},{10... | collective-permute-start | bytes 245768 | tf_op jit(solution)/shard_map/ppermute | solution.py:381
  33.2 3.7 %attend.1 = bf16[128,2048]{1,0:T(8,128)(2,1)} custom-call(s32[2]{0:T(128)S(1)} %pad_add_fusion.where_ref, s32[8,128]{1,0:T(8,128)S(1)} %get-tuple-element.11.meta_ref, bf16[4,48,512]{2,1,0:T(8,128)(2,1)S(1)} %bitcast.10, bf16[128,2048]{1,0:T(8,128)(2,1)S(1)} %bitcast.13, bf16[1280,512]{1,0:T(8,128)(2,1)S(1)} %copy-done, ...), custom_call_target="tpu_custom_call" | custom-call | tf_op jit(solution)/shard_map/attend/pallas_call | solution.py:477
  37.0 0.0 collective-permute-done.3
  37.0 2.9 %collective-permute-done.4 = bf16[80,512]{1,0:T(8,128)(2,1)S(1)} collective-permute-done((bf16[80,512]{1,0:T(8,128)(2,1)S(1)}, bf16[80,512]{1,0:T(8,128)(2,1)S(1)}, u32[]{:S(2)}, u32[]{:S(2)}) %collective-permute-start.4) | collective-permute-done | bytes 81952 | tf_op jit(solution)/shard_map/ppermute | solution.py:381
  39.9 0.0 collective-permute-done.5
  39.9 0.7 %convert_add_fusion = f32[80,512]{1,0:T(8,128)} fusion(bf16[80,512]{1,0:T(8,128)(2,1)S(1)} %collective-permute-done.5, bf16[80,512]{1,0:T(8,128)(2,1)S(1)} %collective-permute-done.4, f32[80,512]{1,0:T(8,128)S(1)} %get-tuple-element.16, bf16[80,512]{1,0:T(8,128)(2,1)S(1)} %collective-permute-done.3), kind=kLoop, calls=%fused_computation | loop fusion | flops 245760 | bytes 573440 | tf_op jit(solution)/shard_map/add | solution.py:475
  (4 shorter events, 0.0 us)
Async XLA Ops:
  0.6 18.5 %copy-start.2 = (bf16[1,128,2048]{2,1,0:T(8,128)(2,1)S(1)}, bf16[1,128,2048]{2,1,0:T(8,128)(2,1)}, u32[]{:S(2)}) copy-start(bf16[1,128,2048]{2,1,0:T(8,128)(2,1)} %param.16) | copy-start | bytes 1572868
  0.6 18.5 %copy-start.1 = (bf16[1,128,2048]{2,1,0:T(8,128)(2,1)S(1)}, bf16[1,128,2048]{2,1,0:T(8,128)(2,1)}, u32[]{:S(2)}) copy-start(bf16[1,128,2048]{2,1,0:T(8,128)(2,1)} %param.15) | copy-start | bytes 1572868
  1.8 11.5 %collective-permute-start.1 = (bf16[352,512]{1,0:T(8,128)(2,1)S(1)}, bf16[352,512]{1,0:T(8,128)(2,1)S(1)}, u32[]{:S(2)}, u32[]{:S(2)}) collective-permute-start(bf16[352,512]{1,0:T(8,128)(2,1)S(1)} %get-tuple-element.14.rest_0_), channel_id=1, source_target_pairs={{0,4},{2,6},{4,0},{6,2},{1,5},{3,7},{5,1},{7,3},{8,12},{10,14},{12... | collective-permute-start | bytes 1081352 | tf_op jit(solution)/shard_map/ppermute | solution.py:381
  4.9 22.9 %collective-permute-start = (bf16[352,512]{1,0:T(8,128)(2,1)S(1)}, bf16[352,512]{1,0:T(8,128)(2,1)S(1)}, u32[]{:S(2)}, u32[]{:S(2)}) collective-permute-start(bf16[352,512]{1,0:T(8,128)(2,1)S(1)} %get-tuple-element.14.rest_0_), channel_id=1, source_target_pairs={{0,2},{2,0},{4,6},{6,4},{1,3},{3,1},{5,7},{7,5},{8,10},{10,8},{12,... | collective-permute-start | bytes 1081352 | tf_op jit(solution)/shard_map/ppermute | solution.py:381
  13.3 14.5 %collective-permute-start.2 = (bf16[352,512]{1,0:T(8,128)(2,1)S(1)}, bf16[352,512]{1,0:T(8,128)(2,1)S(1)}, u32[]{:S(2)}, u32[]{:S(2)}) collective-permute-start(bf16[352,512]{1,0:T(8,128)(2,1)S(1)} %collective-permute-done.1.rest_2_), channel_id=1, source_target_pairs={{0,2},{2,0},{4,6},{6,4},{1,3},{3,1},{5,7},{7,5},{8,10},{10,8},{12,... | collective-permute-start | bytes 1081352 | tf_op jit(solution)/shard_map/ppermute | solution.py:381
  20.4 12.8 %copy-start = (bf16[1280,512]{1,0:T(8,128)(2,1)S(1)}, bf16[1280,512]{1,0:T(8,128)(2,1)}, u32[]{:S(2)}) copy-start(bf16[1280,512]{1,0:T(8,128)(2,1)} %w_ref.1) | copy-start | bytes 3932164
  20.4 12.8 %copy-start.3 = (bf16[1,128,2048]{2,1,0:T(8,128)(2,1)S(1)}, bf16[1,128,2048]{2,1,0:T(8,128)(2,1)}, u32[]{:S(2)}) copy-start(bf16[1,128,2048]{2,1,0:T(8,128)(2,1)} %param.11) | copy-start | bytes 1572868
  28.8 8.2 %collective-permute-start.3 = (bf16[80,512]{1,0:T(8,128)(2,1)S(1)}, bf16[80,512]{1,0:T(8,128)(2,1)S(1)}, u32[]{:S(2)}, u32[]{:S(2)}) collective-permute-start(bf16[80,512]{1,0:T(8,128)(2,1)S(1)} %get-tuple-element.17), channel_id=1, source_target_pairs={{0,24},{8,16},{16,8},{24,0},{1,25},{9,17},{17,9},{25,1},{2,26},{10... | collective-permute-start | bytes 245768 | tf_op jit(solution)/shard_map/ppermute | solution.py:381
  32.5 7.4 %collective-permute-start.4 = (bf16[80,512]{1,0:T(8,128)(2,1)S(1)}, bf16[80,512]{1,0:T(8,128)(2,1)S(1)}, u32[]{:S(2)}, u32[]{:S(2)}) collective-permute-start(bf16[80,512]{1,0:T(8,128)(2,1)S(1)} %get-tuple-element.18), channel_id=1, source_target_pairs={{0,16},{8,24},{16,0},{24,8},{1,17},{9,25},{17,1},{25,9},{2,18},{10... | collective-permute-start | bytes 245768 | tf_op jit(solution)/shard_map/ppermute | solution.py:381
  32.5 7.4 %collective-permute-start.5 = (bf16[80,512]{1,0:T(8,128)(2,1)S(1)}, bf16[80,512]{1,0:T(8,128)(2,1)S(1)}, u32[]{:S(2)}, u32[]{:S(2)}) collective-permute-start(bf16[80,512]{1,0:T(8,128)(2,1)S(1)} %get-tuple-element.19), channel_id=1, source_target_pairs={{0,8},{8,0},{16,24},{24,16},{1,9},{9,1},{17,25},{25,17},{2,10},{10... | collective-permute-start | bytes 245768 | tf_op jit(solution)/shard_map/ppermute | solution.py:381

commit v3 on v2

--- a/solution.py
+++ b/solution.py
@@ -195,8 +195,10 @@
     features_hbm,
     k_hbm,
     v_hbm,
-    head_ref,
-    pack_ref,
+    keys_ref,
+    rows_ref,
+    kv_ref,
+    all_ref,
     meta_ref,
     docs_ref,
     tiles_ref,
@@ -205,25 +207,24 @@
 ):
     slots, parts, slot_count = sizes
     tok_rows = docs_ref.shape[1]
-    width = pack_ref.shape[1]
+    width = keys_ref.shape[1]
     vision = features_hbm.shape[2]
     feature_rows = parts * slots
-    pairs = [
-        (docs_hbm, docs_ref),
-        (tiles_hbm, tiles_ref),
-        (cite_hbm, cite_ref),
-        (img_hbm.at[0], head_ref.at[pl.ds(0, slots), :]),
-        (k_hbm.at[0], pack_ref.at[pl.ds(feature_rows, tok_rows), :]),
-        (v_hbm.at[0], pack_ref.at[pl.ds(feature_rows + tok_rows, tok_rows), :]),
-    ]
-    for part in range(parts):
-        cut = min(width, vision - part * width)
-        pairs.append(
-            (
-                features_hbm.at[0, :, pl.ds(part * width, cut)],
-                pack_ref.at[pl.ds(part * slots, slots), pl.ds(0, cut)],
+    pairs = [(docs_hbm, docs_ref), (tiles_hbm, tiles_ref), (cite_hbm, cite_ref)]
+    places = ((keys_ref, rows_ref, kv_ref, 0, 0, 0),)
+    places += ((all_ref, all_ref, all_ref, 0, slots, slots + feature_rows),)
+    for keys_to, rows_to, kv_to, keys_at, rows_at, kv_at in places:
+        pairs.append((img_hbm.at[0], keys_to.at[pl.ds(keys_at, slots), :]))
+        for part in range(parts):
+            cut = min(width, vision - part * width)
+            pairs.append(
+                (
+                    features_hbm.at[0, :, pl.ds(part * width, cut)],
+                    rows_to.at[pl.ds(rows_at + part * slots, slots), pl.ds(0, cut)],
+                )
             )
-        )
+        pairs.append((k_hbm.at[0], kv_to.at[pl.ds(kv_at, tok_rows), :]))
+        pairs.append((v_hbm.at[0], kv_to.at[pl.ds(kv_at + tok_rows, tok_rows), :]))
     copies = [
         pltpu.make_async_copy(source, target, sems.at[n])
         for n, (source, target) in enumerate(pairs)
@@ -244,97 +245,100 @@
     meta_ref[...] = jnp.where(
         row == 0, docs, jnp.where(row == 1, first, jnp.where(row == 2, first + count, 0))
     )
-    extra = head_ref.shape[0] - slots
-    doc_rows = jnp.broadcast_to(docs.astype(jnp.float32), (extra, tok_rows))
-    head_ref[slots:, :tok_rows] = doc_rows.astype(jnp.bfloat16)
-    if width > tok_rows:
-        head_ref[slots:, tok_rows:] = jnp.zeros((extra, width - tok_rows), jnp.bfloat16)
+    doc_rows = jnp.broadcast_to(docs.astype(jnp.float32), (slots, tok_rows))
+    spare = jnp.zeros((slots, parts * width - vision - tok_rows), jnp.float32)
+    tail = jnp.concatenate([doc_rows, spare], axis=1).astype(jnp.bfloat16)
     for copy in copies[3:]:
         copy.wait()
     last = vision - (parts - 1) * width
-    if last < width:
-        pack_ref[(parts - 1) * slots : feature_rows, last:] = jnp.zeros(
-            (slots, width - last), jnp.bfloat16
-        )
-
-
-def cross_kernel(sizes, meta_ref, head_ref, q_ref, cot_ref, grad_ref, weights_ref):
-    kv_local, group_size, slots = sizes
-    blocks = head_ref.shape[0]
-    key_count = blocks * slots
+    rows_ref[feature_rows - slots : feature_rows, last:] = tail
+    all_ref[feature_rows : feature_rows + slots, last:] = tail
+
+
+def cross_kernel(sizes, meta_ref, q_ref, cot_ref, *rest):
+    kv_local, group_size, slots, blocks = sizes
+    key_refs = rest[:blocks]
+    grad_ref, weights_ref = rest[blocks:]
+    seq_at = lax.axis_index("seq")
     tok_rows = q_ref.shape[0]
-    slot_ids = lax.broadcasted_iota(jnp.int32, (key_count, tok_rows), 0)
-    kept = (slot_ids >= meta_ref[1:2, :]) & (slot_ids < meta_ref[2:3, :])
-    bias = jnp.where(kept, 0.0, MASK_FILL)
+    bias = []
+    for x in range(blocks):
+        slot_ids = (seq_at ^ x) * slots + lax.broadcasted_iota(jnp.int32, (slots, tok_rows), 0)
+        kept = (slot_ids >= meta_ref[1:2, :]) & (slot_ids < meta_ref[2:3, :])
+        bias.append(jnp.where(kept, 0.0, MASK_FILL))
+    bias = jnp.concatenate(bias, axis=0)
     bias = jnp.concatenate([bias] * group_size, axis=1)
     scale = HD ** (-0.5) * LOG2E
     for group in range(kv_local):
         columns = slice(group * HD, (group + 1) * HD)
-        keys = jnp.concatenate([head_ref[b, :slots, columns] for b in range(blocks)], axis=0)
+        keys = jnp.concatenate([ref[:slots, columns] for ref in key_refs], axis=0)
         scores = dot_nt(keys, stacked_heads(q_ref, group, group_size)) * scale + bias
         exps = jnp.exp2(scores - jnp.max(scores, axis=0, keepdims=True))
         inverse = 1.0 / jnp.sum(exps, axis=0, keepdims=True)
         weights = (exps * inverse).astype(jnp.bfloat16)
         weights_ref[group] = weights
-        grad_ref[:, columns] = dot_nn(weights, stacked_heads(cot_ref, group, group_size)).astype(
-            jnp.bfloat16
-        )
-
-
-def attend_kernel(sizes, where_ref, meta_ref, head_ref, q_ref, w_ref, weights_ref, *rest):
-    kv_local, group_size, slots, feature_rows = sizes
-    blocks = head_ref.shape[0]
-    packs, out_ref, values_ref = rest[:blocks], rest[blocks], rest[blocks + 1]
-    seq_at = where_ref[0]
+        grads = dot_nn(weights, stacked_heads(cot_ref, group, group_size)).astype(jnp.bfloat16)
+        for x in range(blocks):
+            at = pl.multiple_of((seq_at ^ x) * slots, slots)
+            grad_ref[pl.ds(at, slots), columns] = grads[x * slots : (x + 1) * slots]
+
+
+def stacked_features(rows, part, slots, cut):
+    return jnp.concatenate(
+        [ref[first + part * slots : first + (part + 1) * slots, :cut] for ref, first in rows],
+        axis=0,
+    )
+
+
+def attend_kernel(sizes, meta_ref, q_ref, w_ref, weights_ref, *rest):
+    kv_local, group_size, slots, parts, row_firsts, kv_firsts = sizes
+    blocks = len(row_firsts)
+    out_ref = rest[-1]
+    rows = list(zip(rest[:blocks], row_firsts))
+    pairs = list(zip(rest[blocks : 2 * blocks], kv_firsts))
+    seq_at = lax.axis_index("seq")
     tok_rows = q_ref.shape[0]
-    key_rows = (packs[0].shape[0] - feature_rows) // 2
-    width = packs[0].shape[1]
+    width = pairs[0][0].shape[1]
     vision = w_ref.shape[0]
-    parts = feature_rows // slots
     total = None
     for part in range(parts):
         cut = min(width, vision - part * width)
-        rows = jnp.concatenate(
-            [pack[part * slots : (part + 1) * slots, :cut] for pack in packs], axis=0
-        )
-        term = dot_nn(rows, w_ref[part * width : part * width + cut, :])
+        term = dot_nn(
+            stacked_features(rows, part, slots, cut), w_ref[part * width : part * width + cut, :]
+        )
         total = term if total is None else total + term
     values = total.astype(jnp.bfloat16)
-    for x in range(blocks):
-        owner = pl.multiple_of((seq_at ^ x) * slots, slots)
-        values_ref[pl.ds(owner, slots), :] = values[x * slots : (x + 1) * slots]
+    last = vision - (parts - 1) * width
     docs = meta_ref[0:1, :].astype(jnp.float32)
     start = jnp.zeros((1, tok_rows), jnp.float32)
-    for b in range(blocks):
-        row = head_ref[b, slots : slots + 16, :tok_rows].astype(jnp.float32)[0:1]
+    for ref, first in rows:
+        at = first + (parts - 1) * slots
+        row = ref[at : at + 16, last : last + tok_rows].astype(jnp.float32)[0:1]
         column = jnp.transpose(jnp.broadcast_to(row, (tok_rows, tok_rows)))
         start = start + jnp.sum(jnp.where(column < docs, 1.0, 0.0), axis=0, keepdims=True)
     start = start.astype(jnp.int32)
     query_pos = seq_at * tok_rows + lax.broadcasted_iota(jnp.int32, (1, tok_rows), 1)
     bias = []
     for x in range(blocks):
-        key_pos = (seq_at ^ x) * key_rows + lax.broadcasted_iota(
-            jnp.int32, (key_rows, tok_rows), 0
+        key_pos = (seq_at ^ x) * tok_rows + lax.broadcasted_iota(
+            jnp.int32, (tok_rows, tok_rows), 0
         )
         kept = (key_pos >= start) & (key_pos <= query_pos)
         bias.append(jnp.where(kept, 0.0, MASK_FILL))
     bias = jnp.concatenate(bias, axis=0)
     bias = jnp.concatenate([bias] * group_size, axis=1)
     scale = HD ** (-0.5) * LOG2E
-    first_key, first_value = feature_rows, feature_rows + key_rows
     for group in range(kv_local):
         columns = slice(group * HD, (group + 1) * HD)
-        keys = jnp.concatenate(
-            [pack[first_key : first_key + key_rows, columns] for pack in packs], axis=0
-        )
+        keys = jnp.concatenate([r[f : f + tok_rows, columns] for r, f in pairs], axis=0)
         vals = jnp.concatenate(
-            [pack[first_value : first_value + key_rows, columns] for pack in packs], axis=0
+            [r[f + tok_rows : f + 2 * tok_rows, columns] for r, f in pairs], axis=0
         )
         scores = dot_nt(keys, stacked_heads(q_ref, group, group_size)) * scale + bias
         exps = jnp.exp2(scores - jnp.max(scores, axis=0, keepdims=True))
         inverse = 1.0 / jnp.sum(exps, axis=0, keepdims=True)
         self_out = dot_tn(vals, exps.astype(jnp.bfloat16)) * inverse
-        cross_out = dot_tn(values_ref[:, columns], weights_ref[group])
+        cross_out = dot_tn(values[:, columns], weights_ref[group])
         merged = (self_out + cross_out).astype(jnp.bfloat16)
         for c in range(group_size):
             head = group * group_size + c
@@ -343,13 +347,13 @@
             )
 
 
-def product_kernel(sizes, where_ref, terms_ref, *rest):
-    slots, vision, out_rows, steps = sizes
-    blocks = terms_ref.shape[0]
-    packs, outs = rest[:blocks], rest[blocks : blocks + steps]
+def product_kernel(sizes, terms_ref, *rest):
+    slots, vision, out_rows, steps, parts, row_firsts = sizes
+    blocks = len(row_firsts)
+    rows, outs = list(zip(rest[:blocks], row_firsts)), rest[blocks : blocks + steps]
     sum_ref, turned_ref = rest[blocks + steps :]
-    seq_at, dp_at = where_ref[0], where_ref[1]
-    width = packs[0].shape[1]
+    seq_at, dp_at = lax.axis_index("seq"), lax.axis_index("dp")
+    width = terms_ref.shape[2]
     total = terms_ref[0].astype(jnp.float32)
     for b in range(1, blocks):
         total = total + terms_ref[b].astype(jnp.float32)
@@ -361,12 +365,11 @@
         ],
         axis=0,
     )
-    for part in range(-(-vision // width)):
+    for part in range(parts):
         cut = min(width, vision - part * width)
-        rows = jnp.concatenate(
-            [pack[part * slots : (part + 1) * slots, :cut] for pack in packs], axis=0
-        )
-        turned_ref[part * width : part * width + cut, :] = jnp.transpose(rows)
+        turned_ref[part * width : part * width + cut, :] = jnp.transpose(
+            stacked_features(rows, part, slots, cut)
+        )
     for x in range(steps):
         row = pl.multiple_of(((dp_at ^ x) * blocks + seq_at) * out_rows, out_rows)
         block = dot_nn(turned_ref[pl.ds(row, out_rows), :], grads)
@@ -406,59 +409,71 @@
     images = tiles.shape[1]
     out_rows = vision // (seq_size * dp_size)
     key_count = slots * seq_size
-    smem = pl.BlockSpec(memory_space=pltpu.SMEM)
     hbm = pl.BlockSpec(memory_space=pltpu.HBM)
-    where_at = jnp.stack([lax.axis_index("seq"), lax.axis_index("dp")]).astype(jnp.int32)
     parts = -(-vision // width)
     feature_rows = parts * slots
-
-    head, own, meta = pl.pallas_call(
+    kv_rows = 2 * tok_rows
+    all_rows = slots + feature_rows + kv_rows
+
+    keys_own, rows_own, kv_own, all_own, meta = pl.pallas_call(
         functools.partial(pack_kernel, (slots, parts, key_count // images)),
-        out_shape=(
-            jax.ShapeDtypeStruct((slots + 16, width), jnp.bfloat16),
-            jax.ShapeDtypeStruct((feature_rows + 2 * tok_rows, width), jnp.bfloat16),
-            jax.ShapeDtypeStruct((8, tok_rows), jnp.int32),
-        ),
+        out_shape=tuple(
+            jax.ShapeDtypeStruct((rows, width), jnp.bfloat16)
+            for rows in (slots, feature_rows, kv_rows, all_rows)
+        )
+        + (jax.ShapeDtypeStruct((8, tok_rows), jnp.int32),),
         in_specs=[hbm] * 7,
-        out_specs=tuple(vmem_specs(3)),
+        out_specs=tuple(vmem_specs(5)),
         scratch_shapes=[
             pltpu.VMEM(docs.shape, jnp.int32),
             pltpu.SMEM(tiles.shape, jnp.int32),
             pltpu.SMEM(cite.shape, jnp.int32),
-            pltpu.SemaphoreType.DMA((6 + parts,)),
+            pltpu.SemaphoreType.DMA((9 + 2 * parts,)),
         ],
         compiler_params=pltpu.CompilerParams(vmem_limit_bytes=8 << 20),
         cost_estimate=pl.CostEstimate(flops=4 << 30, bytes_accessed=16 << 20, transcendentals=0),
         name="pack",
-    )(*[pltpu.with_memory_space_constraint(a, pltpu.HBM) for a in (docs, tiles, cite, img_keys, features, k_self, v_self)])
-    heads_all = lax.all_gather(head, "seq", axis=0)
-    bit = seq_size // 2
-    order = {0: own}
-    while bit:
-        for x in list(order):
-            order[x ^ bit] = swap(order[x], "seq", seq_size, bit)
-        bit //= 2
-    packs = [order[x] for x in range(seq_size)]
+    )(
+        *[
+            pltpu.with_memory_space_constraint(array, pltpu.HBM)
+            for array in (docs, tiles, cite, img_keys, features, k_self, v_self)
+        ]
+    )
+    far, near = seq_size // 2, 1
+
+    def far_and_across(array):
+        there = swap(array, "seq", seq_size, far)
+        return there, swap(there, "seq", seq_size, near)
+
+    keys_far, keys_across = far_and_across(keys_own)
+    rows_far, rows_across = far_and_across(rows_own)
+    kv_far, kv_across = far_and_across(kv_own)
+    all_near = swap(all_own, "seq", seq_size, near)
+    key_blocks = (all_own, all_near, keys_far, keys_across)
+    row_blocks = (all_own, all_near, rows_far, rows_across)
+    kv_blocks = (all_own, all_near, kv_far, kv_across)
+    row_firsts = (slots, slots, 0, 0)
+    kv_firsts = (slots + feature_rows, slots + feature_rows, 0, 0)
 
     grad_terms, weights = pl.pallas_call(
-        functools.partial(cross_kernel, (kv_local, group_size, slots)),
+        functools.partial(cross_kernel, (kv_local, group_size, slots, seq_size)),
         out_shape=(
             jax.ShapeDtypeStruct((key_count, width), jnp.bfloat16),
             jax.ShapeDtypeStruct((kv_local, key_count, group_size * tok_rows), jnp.bfloat16),
         ),
-        in_specs=vmem_specs(4),
+        in_specs=vmem_specs(3 + seq_size),
         out_specs=tuple(vmem_specs(2)),
         compiler_params=pltpu.CompilerParams(vmem_limit_bytes=24 << 20),
         name="cross",
-    )(meta, heads_all, q_cross[0], cotangent[0])
+    )(meta, q_cross[0], cotangent[0], *key_blocks)
     terms_all = lax.all_gather(grad_terms, "seq", axis=0)
     blocks_out = pl.pallas_call(
-        functools.partial(product_kernel, (slots, vision, out_rows, dp_size)),
+        functools.partial(product_kernel, (slots, vision, out_rows, dp_size, parts, row_firsts)),
         out_shape=tuple(
             jax.ShapeDtypeStruct((out_rows, width), jnp.bfloat16 if x else jnp.float32)
             for x in range(dp_size)
         ),
-        in_specs=[smem] + vmem_specs(1 + seq_size),
+        in_specs=vmem_specs(1 + seq_size),
         out_specs=tuple(vmem_specs(dp_size)),
         scratch_shapes=[
             pltpu.VMEM((key_count, width), jnp.bfloat16),
@@ -466,7 +481,7 @@
         ],
         compiler_params=pltpu.CompilerParams(vmem_limit_bytes=16 << 20),
         name="product",
-    )(where_at, terms_all, *packs)
+    )(terms_all, *row_blocks)
     arrived = []
     for x in range(dp_size - 1, 0, -1):
         arrived.append(swap(blocks_out[x], "dp", dp_size, x))
@@ -475,14 +490,15 @@
         weight_grad = weight_grad + block.astype(jnp.float32)
 
     merged = pl.pallas_call(
-        functools.partial(attend_kernel, (kv_local, group_size, slots, feature_rows)),
+        functools.partial(
+            attend_kernel, (kv_local, group_size, slots, parts, row_firsts, kv_firsts)
+        ),
         out_shape=jax.ShapeDtypeStruct((tok_rows, heads_local * HD), jnp.bfloat16),
-        in_specs=[smem] + vmem_specs(5 + seq_size),
+        in_specs=vmem_specs(4 + 2 * seq_size),
         out_specs=vmem_specs(1)[0],
-        scratch_shapes=[pltpu.VMEM((key_count, width), jnp.bfloat16)],
         compiler_params=pltpu.CompilerParams(vmem_limit_bytes=32 << 20),
         name="attend",
-    )(where_at, meta, heads_all, q_self[0], w_value, weights, *packs)
+    )(meta, q_self[0], w_value, weights, *row_blocks, *kv_blocks)
     return (merged[None], weight_grad)
 
 
@@ -496,7 +512,7 @@
     rows, left = divmod(features[2], seq_size * dp_size)
     return (
         powers
-        and seq_size <= 4
+        and seq_size == 4
         and dp_size <= 8
         and tok_rows == HD
         and tok_rows <= width
@@ -506,6 +522,7 @@
         and rows % 16 == 0
         and features[2] % HD == 0
         and width % HD == 0
+        and -features[2] % width >= tok_rows
         and cite[1] <= 256
     )
 

time: 40.8 us -> 37.5 us (0.919)
  blocking collectives: 13.2 us -> 9.13 us
  starting transfers between devices: 7.52 us -> 9.73 us
  Pallas kernels: 7.07 us -> 6.27 us
  waiting for transfers between devices: 11.3 us -> 10.8 us
    all_gather x1 -> x0, blocking collectives: 5.78 us -> none  [on_device_small(): heads_all = lax.all_gather(head, 'seq', axis=0)]
    ppermute x6 -> x10, starting transfers between devices: 7.52 us -> 9.73 us  [swap(): return lax.ppermute(array, axis, [(i, i ^ x) for i in range(size)])]
    all_gather x1, blocking collectives: 7.4 us -> 9.13 us  [on_device_small(): terms_all = lax.all_gather(grad_terms, 'seq', axis=0)]
    pallas_call x1, Pallas kernels: 0.95 us -> 0.37 us  [on_device_small(): pl.pallas_call(functools.partial(product_kernel, (slots, vision, out_rows...]
    ppermute x6 -> x10, waiting for transfers between devices: 11.3 us -> 10.8 us  [swap(): return lax.ppermute(array, axis, [(i, i ^ x) for i in range(size)])]
    pallas_call x1, Pallas kernels: 3.74 us -> 3.22 us  [on_device_small(): pl.pallas_call(functools.partial(attend_kernel, (kv_local, group_size, sl...]
  transfers between devices with their start and end apart: 6 -> 10, of which waited for: 2 -> 3; matrix products, arithmetic and copies ran while one was open for 0% -> 2% of each run, Pallas kernels for 12% -> 4%
where the time goes in v3:
time: 37.5 us; the launch traced here: 37.3 us
  waiting for transfers between devices  10.8 us (29%)
  starting transfers between devices  9.73 us (26%)
  blocking collectives  9.13 us (24%)
  Pallas kernels  6.27 us (17%)
  other arithmetic  0.71 us (2%)
  between operations  0.71 us (2%)
    ppermute x10, waiting for transfers between devices, swap(): return lax.ppermute(array, axis, [(i, i ^ x) for i in range(size)])  10.8 us
    ppermute x10, starting transfers between devices, swap(): return lax.ppermute(array, axis, [(i, i ^ x) for i in range(size)])  9.73 us
    all_gather x1, blocking collectives, on_device_small(): terms_all = lax.all_gather(grad_terms, 'seq', axis=0)  9.13 us
    pallas_call x1, Pallas kernels, on_device_small(): pl.pallas_call(functools.partial(attend_kernel, (kv_local, group_size, sl...  3.22 us
    pallas_call x1, Pallas kernels, on_device_small(): pl.pallas_call(functools.partial(pack_kernel, (slots, parts, key_count //...  1.46 us
    pallas_call x1, Pallas kernels, on_device_small(): pl.pallas_call(functools.partial(cross_kernel, (kv_local, group_size, slo...  1.23 us
  transfers between devices with their start and end apart: 10, of which 3 were waited for; matrix products, arithmetic and copies ran while one was open for 2% of the time, Pallas kernels for 4%

profile of v3, /device:TPU:0, one launch (start us, length us, event | category | flops | bytes accessed | tf_op | source)
XLA Modules:
  0.0 37.3 jit_solution(5187718323115538135)
XLA Ops:
  0.7 1.5 %pack.1 = (bf16[32,512]{1,0:T(8,128)(2,1)S(1)}, bf16[96,512]{1,0:T(8,128)(2,1)S(1)}, bf16[256,512]{1,0:T(8,128)(2,1)S(1)}, bf16[384,512]{1,0:T(8,128)(2,1)S(1)}, s32[8,128]{1,0:T(8,128)S(1)}) custom-call(s32[1,128]{1,0:T(1,128)} %docs_hbm.1, s32[1,4]{1,0:T(1,128)} %tiles_hbm.1, s32[1,4]{1,0:T(1,128)} %cite_hbm.1, bf16[1,32,512]{2,1,0:T(8,128)(2,1)} %img_hbm.1, ...), custom_call_target="tpu_custom_call" | custom-call | flops 4294967296 | bytes 16777216 | tf_op jit(solution)/shard_map/pack/pallas_call | solution.py:418
  2.1 0.6 %collective-permute-start = (bf16[384,512]{1,0:T(8,128)(2,1)S(1)}, bf16[384,512]{1,0:T(8,128)(2,1)S(1)}, u32[]{:S(2)}, u32[]{:S(2)}) collective-permute-start(bf16[384,512]{1,0:T(8,128)(2,1)S(1)} %get-tuple-element.14.rest_0_.rest_4_), channel_id=1, source_target_pairs={{0,2},{2,0},{4,6},{6,4},{1,3},{3,1},{5,7},{7,5},{8,10},{10,8},{12,... | collective-permute-start | bytes 1179656 | tf_op jit(solution)/shard_map/ppermute | solution.py:384
  2.7 2.6 %collective-permute-start.3 = (bf16[96,512]{1,0:T(8,128)(2,1)S(1)}, bf16[96,512]{1,0:T(8,128)(2,1)S(1)}, u32[]{:S(2)}, u32[]{:S(2)}) collective-permute-start(bf16[96,512]{1,0:T(8,128)(2,1)S(1)} %get-tuple-element.17), channel_id=1, source_target_pairs={{0,4},{2,6},{4,0},{6,2},{1,5},{3,7},{5,1},{7,3},{8,12},{10,14},{12... | collective-permute-start | bytes 294920 | tf_op jit(solution)/shard_map/ppermute | solution.py:384
  5.3 0.1 collective-permute-start.1
  5.3 4.0 %collective-permute-done.1.rest_2_ = bf16[32,512]{1,0:T(8,128)(2,1)S(1)} collective-permute-done((bf16[32,512]{1,0:T(8,128)(2,1)S(1)}, bf16[32,512]{1,0:T(8,128)(2,1)S(1)}, u32[]{:S(2)}, u32[]{:S(2)}) %collective-permute-start.1) | collective-permute-done | bytes 32800 | tf_op jit(solution)/shard_map/ppermute | solution.py:384
  9.4 1.7 %collective-permute-start.5 = (bf16[256,512]{1,0:T(8,128)(2,1)S(1)}, bf16[256,512]{1,0:T(8,128)(2,1)S(1)}, u32[]{:S(2)}, u32[]{:S(2)}) collective-permute-start(bf16[256,512]{1,0:T(8,128)(2,1)S(1)} %get-tuple-element.18), channel_id=1, source_target_pairs={{0,4},{2,6},{4,0},{6,2},{1,5},{3,7},{5,1},{7,3},{8,12},{10,14},{12... | collective-permute-start | bytes 786440 | tf_op jit(solution)/shard_map/ppermute | solution.py:384
  11.1 0.0 collective-permute-done.3.rest_2_
  11.1 0.2 collective-permute-start.4
  11.3 0.0 collective-permute-done.rest_1_.rest_5_
  11.3 1.2 %cross.1 = (bf16[128,512]{1,0:T(8,128)(2,1)S(1)}, bf16[4,128,512]{2,1,0:T(8,128)(2,1)S(1)}) custom-call(s32[8,128]{1,0:T(8,128)S(1)} %get-tuple-element.13.meta_ref, bf16[128,2048]{1,0:T(8,128)(2,1)S(1)} %bitcast.7, bf16[128,2048]{1,0:T(8,128)(2,1)S(1)} %bitcast.8, bf16[384,512]{1,0:T(8,128)(2,1)S(1)} %get-tuple-element.14.rest_0_.rest_4_, ...), custom_call_target="tpu_custom_call" | custom-call | tf_op jit(solution)/shard_map/cross/pallas_call | solution.py:458
  12.6 0.0 copy-start
  12.6 0.0 copy-start.1
  12.6 9.1 %all-gather = bf16[512,512]{1,0:T(8,128)(2,1)S(1)} all-gather(bf16[128,512]{1,0:T(8,128)(2,1)S(1)} %get-tuple-element.19), channel_id=2, replica_groups=mesh['dp'=4,'seq'=4,'tensor'=2] {'seq'}, dimensions={0}, use_global_device_ids=true | all-gather | bytes 655360 | tf_op jit(solution)/shard_map/all_gather | solution.py:469
  21.7 0.0 collective-permute-done.4.rest_3_
  21.7 0.4 product.1
  22.1 3.9 %collective-permute-start.7 = (bf16[80,512]{1,0:T(8,128)(2,1)S(1)}, bf16[80,512]{1,0:T(8,128)(2,1)S(1)}, u32[]{:S(2)}, u32[]{:S(2)}) collective-permute-start(bf16[80,512]{1,0:T(8,128)(2,1)S(1)} %get-tuple-element.21), channel_id=1, source_target_pairs={{0,24},{8,16},{16,8},{24,0},{1,25},{9,17},{17,9},{25,1},{2,26},{10... | collective-permute-start | bytes 245768 | tf_op jit(solution)/shard_map/ppermute | solution.py:384
  26.0 0.0 collective-permute-start.8
  26.0 0.6 %collective-permute-start.9 = (bf16[80,512]{1,0:T(8,128)(2,1)S(1)}, bf16[80,512]{1,0:T(8,128)(2,1)S(1)}, u32[]{:S(2)}, u32[]{:S(2)}) collective-permute-start(bf16[80,512]{1,0:T(8,128)(2,1)S(1)} %get-tuple-element.23), channel_id=1, source_target_pairs={{0,8},{8,0},{16,24},{24,16},{1,9},{9,1},{17,25},{25,17},{2,10},{10... | collective-permute-start | bytes 245768 | tf_op jit(solution)/shard_map/ppermute | solution.py:384
  26.7 0.0 collective-permute-done.5.rest_6_
  26.7 2.7 %collective-permute-done.7 = bf16[80,512]{1,0:T(8,128)(2,1)S(1)} collective-permute-done((bf16[80,512]{1,0:T(8,128)(2,1)S(1)}, bf16[80,512]{1,0:T(8,128)(2,1)S(1)}, u32[]{:S(2)}, u32[]{:S(2)}) %collective-permute-start.7) | collective-permute-done | bytes 81952 | tf_op jit(solution)/shard_map/ppermute | solution.py:384
  29.4 4.0 %collective-permute-done.8 = bf16[80,512]{1,0:T(8,128)(2,1)S(1)} collective-permute-done((bf16[80,512]{1,0:T(8,128)(2,1)S(1)}, bf16[80,512]{1,0:T(8,128)(2,1)S(1)}, u32[]{:S(2)}, u32[]{:S(2)}) %collective-permute-start.8) | collective-permute-done | bytes 81952 | tf_op jit(solution)/shard_map/ppermute | solution.py:384
  33.4 0.7 %convert_add_fusion = f32[80,512]{1,0:T(8,128)} fusion(bf16[80,512]{1,0:T(8,128)(2,1)S(1)} %collective-permute-done.9, bf16[80,512]{1,0:T(8,128)(2,1)S(1)} %collective-permute-done.8, f32[80,512]{1,0:T(8,128)S(1)} %get-tuple-element.20, bf16[80,512]{1,0:T(8,128)(2,1)S(1)} %collective-permute-done.7), kind=kLoop, calls=%fused_computation | loop fusion | flops 245760 | bytes 573440 | tf_op jit(solution)/shard_map/add | solution.py:490
  34.1 0.0 collective-permute-done.6.rest_7_
  34.1 3.2 %attend.1 = bf16[128,2048]{1,0:T(8,128)(2,1)} custom-call(s32[8,128]{1,0:T(8,128)S(1)} %get-tuple-element.13.meta_ref, bf16[128,2048]{1,0:T(8,128)(2,1)S(1)} %bitcast.6, bf16[1280,512]{1,0:T(8,128)(2,1)S(1)} %copy-done, bf16[4,128,512]{2,1,0:T(8,128)(2,1)S(1)} %get-tuple-element.16.weights_ref, bf16[384,512]{1,0:T(8,128)(2,1)S(1)} %get-tuple-element.14.rest_0_.rest_4_, ...), custom_call_target="tpu_custom_call" | custom-call | tf_op jit(solution)/shard_map/attend/pallas_call | solution.py:492
  (10 shorter events, 0.0 us)
Async XLA Ops:
  0.6 10.7 %copy-start.3 = (bf16[1,128,2048]{2,1,0:T(8,128)(2,1)S(1)}, bf16[1,128,2048]{2,1,0:T(8,128)(2,1)}, u32[]{:S(2)}) copy-start(bf16[1,128,2048]{2,1,0:T(8,128)(2,1)} %param.16) | copy-start | bytes 1572868
  0.6 10.7 %copy-start.2 = (bf16[1,128,2048]{2,1,0:T(8,128)(2,1)S(1)}, bf16[1,128,2048]{2,1,0:T(8,128)(2,1)}, u32[]{:S(2)}) copy-start(bf16[1,128,2048]{2,1,0:T(8,128)(2,1)} %param.15) | copy-start | bytes 1572868
  2.1 9.2 %collective-permute-start = (bf16[384,512]{1,0:T(8,128)(2,1)S(1)}, bf16[384,512]{1,0:T(8,128)(2,1)S(1)}, u32[]{:S(2)}, u32[]{:S(2)}) collective-permute-start(bf16[384,512]{1,0:T(8,128)(2,1)S(1)} %get-tuple-element.14.rest_0_.rest_4_), channel_id=1, source_target_pairs={{0,2},{2,0},{4,6},{6,4},{1,3},{3,1},{5,7},{7,5},{8,10},{10,8},{12,... | collective-permute-start | bytes 1179656 | tf_op jit(solution)/shard_map/ppermute | solution.py:384
  2.7 8.4 %collective-permute-start.3 = (bf16[96,512]{1,0:T(8,128)(2,1)S(1)}, bf16[96,512]{1,0:T(8,128)(2,1)S(1)}, u32[]{:S(2)}, u32[]{:S(2)}) collective-permute-start(bf16[96,512]{1,0:T(8,128)(2,1)S(1)} %get-tuple-element.17), channel_id=1, source_target_pairs={{0,4},{2,6},{4,0},{6,2},{1,5},{3,7},{5,1},{7,3},{8,12},{10,14},{12... | collective-permute-start | bytes 294920 | tf_op jit(solution)/shard_map/ppermute | solution.py:384
  5.3 4.1 %collective-permute-start.1 = (bf16[32,512]{1,0:T(8,128)(2,1)S(1)}, bf16[32,512]{1,0:T(8,128)(2,1)S(1)}, u32[]{:S(2)}, u32[]{:S(2)}) collective-permute-start(bf16[32,512]{1,0:T(8,128)(2,1)S(1)} %get-tuple-element.15), channel_id=1, source_target_pairs={{0,4},{2,6},{4,0},{6,2},{1,5},{3,7},{5,1},{7,3},{8,12},{10,14},{12... | collective-permute-start | bytes 98312 | tf_op jit(solution)/shard_map/ppermute | solution.py:384
  9.3 2.0 %collective-permute-start.2 = (bf16[32,512]{1,0:T(8,128)(2,1)S(1)}, bf16[32,512]{1,0:T(8,128)(2,1)S(1)}, u32[]{:S(2)}, u32[]{:S(2)}) collective-permute-start(bf16[32,512]{1,0:T(8,128)(2,1)S(1)} %collective-permute-done.1.rest_2_), channel_id=1, source_target_pairs={{0,2},{2,0},{4,6},{6,4},{1,3},{3,1},{5,7},{7,5},{8,10},{10,8},{12,... | collective-permute-start | bytes 98312 | tf_op jit(solution)/shard_map/ppermute | solution.py:384
  9.4 17.3 %collective-permute-start.5 = (bf16[256,512]{1,0:T(8,128)(2,1)S(1)}, bf16[256,512]{1,0:T(8,128)(2,1)S(1)}, u32[]{:S(2)}, u32[]{:S(2)}) collective-permute-start(bf16[256,512]{1,0:T(8,128)(2,1)S(1)} %get-tuple-element.18), channel_id=1, source_target_pairs={{0,4},{2,6},{4,0},{6,2},{1,5},{3,7},{5,1},{7,3},{8,12},{10,14},{12... | collective-permute-start | bytes 786440 | tf_op jit(solution)/shard_map/ppermute | solution.py:384
  11.1 10.6 %collective-permute-start.4 = (bf16[96,512]{1,0:T(8,128)(2,1)S(1)}, bf16[96,512]{1,0:T(8,128)(2,1)S(1)}, u32[]{:S(2)}, u32[]{:S(2)}) collective-permute-start(bf16[96,512]{1,0:T(8,128)(2,1)S(1)} %collective-permute-done.3.rest_2_), channel_id=1, source_target_pairs={{0,2},{2,0},{4,6},{6,4},{1,3},{3,1},{5,7},{7,5},{8,10},{10,8},{12,... | collective-permute-start | bytes 294920 | tf_op jit(solution)/shard_map/ppermute | solution.py:384
  12.6 21.5 %copy-start = (bf16[1280,512]{1,0:T(8,128)(2,1)S(1)}, bf16[1280,512]{1,0:T(8,128)(2,1)}, u32[]{:S(2)}) copy-start(bf16[1280,512]{1,0:T(8,128)(2,1)} %w_ref.1) | copy-start | bytes 3932164
  12.6 21.5 %copy-start.1 = (bf16[1,128,2048]{2,1,0:T(8,128)(2,1)S(1)}, bf16[1,128,2048]{2,1,0:T(8,128)(2,1)}, u32[]{:S(2)}) copy-start(bf16[1,128,2048]{2,1,0:T(8,128)(2,1)} %param.11) | copy-start | bytes 1572868
  22.1 7.3 %collective-permute-start.7 = (bf16[80,512]{1,0:T(8,128)(2,1)S(1)}, bf16[80,512]{1,0:T(8,128)(2,1)S(1)}, u32[]{:S(2)}, u32[]{:S(2)}) collective-permute-start(bf16[80,512]{1,0:T(8,128)(2,1)S(1)} %get-tuple-element.21), channel_id=1, source_target_pairs={{0,24},{8,16},{16,8},{24,0},{1,25},{9,17},{17,9},{25,1},{2,26},{10... | collective-permute-start | bytes 245768 | tf_op jit(solution)/shard_map/ppermute | solution.py:384
  26.0 7.4 %collective-permute-start.8 = (bf16[80,512]{1,0:T(8,128)(2,1)S(1)}, bf16[80,512]{1,0:T(8,128)(2,1)S(1)}, u32[]{:S(2)}, u32[]{:S(2)}) collective-permute-start(bf16[80,512]{1,0:T(8,128)(2,1)S(1)} %get-tuple-element.22), channel_id=1, source_target_pairs={{0,16},{8,24},{16,0},{24,8},{1,17},{9,25},{17,1},{25,9},{2,18},{10... | collective-permute-start | bytes 245768 | tf_op jit(solution)/shard_map/ppermute | solution.py:384
  26.0 7.4 %collective-permute-start.9 = (bf16[80,512]{1,0:T(8,128)(2,1)S(1)}, bf16[80,512]{1,0:T(8,128)(2,1)S(1)}, u32[]{:S(2)}, u32[]{:S(2)}) collective-permute-start(bf16[80,512]{1,0:T(8,128)(2,1)S(1)} %get-tuple-element.23), channel_id=1, source_target_pairs={{0,8},{8,0},{16,24},{24,16},{1,9},{9,1},{17,25},{25,17},{2,10},{10... | collective-permute-start | bytes 245768 | tf_op jit(solution)/shard_map/ppermute | solution.py:384
  26.7 7.4 %collective-permute-start.6 = (bf16[256,512]{1,0:T(8,128)(2,1)S(1)}, bf16[256,512]{1,0:T(8,128)(2,1)S(1)}, u32[]{:S(2)}, u32[]{:S(2)}) collective-permute-start(bf16[256,512]{1,0:T(8,128)(2,1)S(1)} %collective-permute-done.5.rest_6_), channel_id=1, source_target_pairs={{0,2},{2,0},{4,6},{6,4},{1,3},{3,1},{5,7},{7,5},{8,10},{10,8},{12,... | collective-permute-start | bytes 786440 | tf_op jit(solution)/shard_map/ppermute | solution.py:384

commit v4 on v3

--- a/solution.py
+++ b/solution.py
@@ -191,14 +191,11 @@
     docs_hbm,
     tiles_hbm,
     cite_hbm,
-    img_hbm,
     features_hbm,
     k_hbm,
     v_hbm,
-    keys_ref,
     rows_ref,
     kv_ref,
-    all_ref,
     meta_ref,
     docs_ref,
     tiles_ref,
@@ -207,24 +204,20 @@
 ):
     slots, parts, slot_count = sizes
     tok_rows = docs_ref.shape[1]
-    width = keys_ref.shape[1]
+    width = kv_ref.shape[1]
     vision = features_hbm.shape[2]
     feature_rows = parts * slots
     pairs = [(docs_hbm, docs_ref), (tiles_hbm, tiles_ref), (cite_hbm, cite_ref)]
-    places = ((keys_ref, rows_ref, kv_ref, 0, 0, 0),)
-    places += ((all_ref, all_ref, all_ref, 0, slots, slots + feature_rows),)
-    for keys_to, rows_to, kv_to, keys_at, rows_at, kv_at in places:
-        pairs.append((img_hbm.at[0], keys_to.at[pl.ds(keys_at, slots), :]))
-        for part in range(parts):
-            cut = min(width, vision - part * width)
-            pairs.append(
-                (
-                    features_hbm.at[0, :, pl.ds(part * width, cut)],
-                    rows_to.at[pl.ds(rows_at + part * slots, slots), pl.ds(0, cut)],
-                )
+    for part in range(parts):
+        cut = min(width, vision - part * width)
+        pairs.append(
+            (
+                features_hbm.at[0, :, pl.ds(part * width, cut)],
+                rows_ref.at[pl.ds(part * slots, slots), pl.ds(0, cut)],
             )
-        pairs.append((k_hbm.at[0], kv_to.at[pl.ds(kv_at, tok_rows), :]))
-        pairs.append((v_hbm.at[0], kv_to.at[pl.ds(kv_at + tok_rows, tok_rows), :]))
+        )
+    pairs.append((k_hbm.at[0], kv_ref.at[pl.ds(0, tok_rows), :]))
+    pairs.append((v_hbm.at[0], kv_ref.at[pl.ds(tok_rows, tok_rows), :]))
     copies = [
         pltpu.make_async_copy(source, target, sems.at[n])
         for n, (source, target) in enumerate(pairs)
@@ -252,7 +245,6 @@
         copy.wait()
     last = vision - (parts - 1) * width
     rows_ref[feature_rows - slots : feature_rows, last:] = tail
-    all_ref[feature_rows : feature_rows + slots, last:] = tail
 
 
 def cross_kernel(sizes, meta_ref, q_ref, cot_ref, *rest):
@@ -269,15 +261,23 @@
     bias = jnp.concatenate(bias, axis=0)
     bias = jnp.concatenate([bias] * group_size, axis=1)
     scale = HD ** (-0.5) * LOG2E
+    spans = [slice(group * HD, (group + 1) * HD) for group in range(kv_local)]
+    scores = [
+        dot_nt(
+            jnp.concatenate([ref[:, columns] for ref in key_refs], axis=0),
+            stacked_heads(q_ref, group, group_size),
+        )
+        for group, columns in enumerate(spans)
+    ]
     for group in range(kv_local):
-        columns = slice(group * HD, (group + 1) * HD)
-        keys = jnp.concatenate([ref[:slots, columns] for ref in key_refs], axis=0)
-        scores = dot_nt(keys, stacked_heads(q_ref, group, group_size)) * scale + bias
-        exps = jnp.exp2(scores - jnp.max(scores, axis=0, keepdims=True))
+        scaled = scores[group] * scale + bias
+        exps = jnp.exp2(scaled - jnp.max(scaled, axis=0, keepdims=True))
         inverse = 1.0 / jnp.sum(exps, axis=0, keepdims=True)
-        weights = (exps * inverse).astype(jnp.bfloat16)
-        weights_ref[group] = weights
-        grads = dot_nn(weights, stacked_heads(cot_ref, group, group_size)).astype(jnp.bfloat16)
+        weights_ref[group] = (exps * inverse).astype(jnp.bfloat16)
+    for group, columns in enumerate(spans):
+        grads = dot_nn(weights_ref[group], stacked_heads(cot_ref, group, group_size)).astype(
+            jnp.bfloat16
+        )
         for x in range(blocks):
             at = pl.multiple_of((seq_at ^ x) * slots, slots)
             grad_ref[pl.ds(at, slots), columns] = grads[x * slots : (x + 1) * slots]
@@ -285,21 +285,72 @@
 
 def stacked_features(rows, part, slots, cut):
     return jnp.concatenate(
-        [ref[first + part * slots : first + (part + 1) * slots, :cut] for ref, first in rows],
-        axis=0,
-    )
-
-
-def attend_kernel(sizes, meta_ref, q_ref, w_ref, weights_ref, *rest):
-    kv_local, group_size, slots, parts, row_firsts, kv_firsts = sizes
-    blocks = len(row_firsts)
-    out_ref = rest[-1]
-    rows = list(zip(rest[:blocks], row_firsts))
-    pairs = list(zip(rest[blocks : 2 * blocks], kv_firsts))
+        [ref[part * slots : (part + 1) * slots, :cut] for ref in rows], axis=0
+    )
+
+
+def first_positions(sizes, meta_ref, rows):
+    slots, parts, last = sizes
+    docs = meta_ref[0:1, :].astype(jnp.float32)
+    tok_rows = docs.shape[1]
+    start = jnp.zeros((1, tok_rows), jnp.float32)
+    at = (parts - 1) * slots
+    for ref in rows:
+        row = ref[at : at + 16, last : last + tok_rows].astype(jnp.float32)[0:1]
+        column = jnp.transpose(jnp.broadcast_to(row, (tok_rows, tok_rows)))
+        start = start + jnp.sum(jnp.where(column < docs, 1.0, 0.0), axis=0, keepdims=True)
+    return start
+
+
+def kept_bias(seq_at, first, blocks, start, group_size):
+    tok_rows = start.shape[1]
+    query_pos = seq_at * tok_rows + lax.broadcasted_iota(jnp.int32, (1, tok_rows), 1)
+    bias = []
+    for x in range(first, first + blocks):
+        key_pos = (seq_at ^ x) * tok_rows + lax.broadcasted_iota(
+            jnp.int32, (tok_rows, tok_rows), 0
+        )
+        kept = (key_pos >= start) & (key_pos <= query_pos)
+        bias.append(jnp.where(kept, 0.0, MASK_FILL))
+    return jnp.concatenate([jnp.concatenate(bias, axis=0)] * group_size, axis=1)
+
+
+def scaled_scores(pairs, columns, queries, bias):
+    tok_rows = pairs[0].shape[0] // 2
+    keys = jnp.concatenate([ref[:tok_rows, columns] for ref in pairs], axis=0)
+    return dot_nt(keys, queries) * (HD ** (-0.5) * LOG2E) + bias
+
+
+def weighted_values(pairs, columns, exps):
+    tok_rows = pairs[0].shape[0] // 2
+    vals = jnp.concatenate([ref[tok_rows:, columns] for ref in pairs], axis=0)
+    return dot_tn(vals, exps)
+
+
+def early_kernel(sizes, meta_ref, q_ref, w_ref, weights_ref, *rest):
+    kv_local, group_size, slots, parts, blocks, count = sizes
+    rows, pairs = rest[:blocks], rest[blocks : blocks + count]
+    cross_ref, self_ref, stats_ref = rest[blocks + count :]
+    width = pairs[0].shape[1]
+    vision = w_ref.shape[0]
     seq_at = lax.axis_index("seq")
-    tok_rows = q_ref.shape[0]
-    width = pairs[0][0].shape[1]
-    vision = w_ref.shape[0]
+    start = first_positions((slots, parts, vision - (parts - 1) * width), meta_ref, rows)
+    stats_ref[kv_local, 0:1, :] = jnp.concatenate([start] * group_size, axis=1)
+    bias = kept_bias(seq_at, 0, count, start.astype(jnp.int32), group_size)
+    spans = [slice(group * HD, (group + 1) * HD) for group in range(kv_local)]
+    scores = [
+        scaled_scores(pairs, columns, stacked_heads(q_ref, group, group_size), bias)
+        for group, columns in enumerate(spans)
+    ]
+    weighted = []
+    for group in range(kv_local):
+        top = jnp.max(scores[group], axis=0, keepdims=True)
+        exps = jnp.exp2(scores[group] - top)
+        stats_ref[group, 0:1, :] = top
+        stats_ref[group, 1:2, :] = jnp.sum(exps, axis=0, keepdims=True)
+        weighted.append(exps.astype(jnp.bfloat16))
+    for group, columns in enumerate(spans):
+        self_ref[group] = weighted_values(pairs, columns, weighted[group])
     total = None
     for part in range(parts):
         cut = min(width, vision - part * width)
@@ -308,55 +359,81 @@
         )
         total = term if total is None else total + term
     values = total.astype(jnp.bfloat16)
-    last = vision - (parts - 1) * width
-    docs = meta_ref[0:1, :].astype(jnp.float32)
-    start = jnp.zeros((1, tok_rows), jnp.float32)
-    for ref, first in rows:
-        at = first + (parts - 1) * slots
-        row = ref[at : at + 16, last : last + tok_rows].astype(jnp.float32)[0:1]
-        column = jnp.transpose(jnp.broadcast_to(row, (tok_rows, tok_rows)))
-        start = start + jnp.sum(jnp.where(column < docs, 1.0, 0.0), axis=0, keepdims=True)
-    start = start.astype(jnp.int32)
-    query_pos = seq_at * tok_rows + lax.broadcasted_iota(jnp.int32, (1, tok_rows), 1)
-    bias = []
-    for x in range(blocks):
-        key_pos = (seq_at ^ x) * tok_rows + lax.broadcasted_iota(
-            jnp.int32, (tok_rows, tok_rows), 0
-        )
-        kept = (key_pos >= start) & (key_pos <= query_pos)
-        bias.append(jnp.where(kept, 0.0, MASK_FILL))
-    bias = jnp.concatenate(bias, axis=0)
-    bias = jnp.concatenate([bias] * group_size, axis=1)
-    scale = HD ** (-0.5) * LOG2E
     for group in range(kv_local):
         columns = slice(group * HD, (group + 1) * HD)
-        keys = jnp.concatenate([r[f : f + tok_rows, columns] for r, f in pairs], axis=0)
-        vals = jnp.concatenate(
-            [r[f + tok_rows : f + 2 * tok_rows, columns] for r, f in pairs], axis=0
-        )
-        scores = dot_nt(keys, stacked_heads(q_ref, group, group_size)) * scale + bias
-        exps = jnp.exp2(scores - jnp.max(scores, axis=0, keepdims=True))
-        inverse = 1.0 / jnp.sum(exps, axis=0, keepdims=True)
-        self_out = dot_tn(vals, exps.astype(jnp.bfloat16)) * inverse
-        cross_out = dot_tn(values[:, columns], weights_ref[group])
-        merged = (self_out + cross_out).astype(jnp.bfloat16)
+        cross_ref[group] = dot_tn(values[:, columns], weights_ref[group])
+
+
+def absorbed(sizes, first, pair_ref, q_ref, stats_ref):
+    kv_local, group_size = sizes
+    seq_at = lax.axis_index("seq")
+    start = stats_ref[kv_local, 0:1, : q_ref.shape[0]]
+    bias = kept_bias(seq_at, first, 1, start.astype(jnp.int32), group_size)
+    spans = [slice(group * HD, (group + 1) * HD) for group in range(kv_local)]
+    pairs = (pair_ref,)
+    scores = [
+        scaled_scores(pairs, columns, stacked_heads(q_ref, group, group_size), bias)
+        for group, columns in enumerate(spans)
+    ]
+    found = []
+    for group in range(kv_local):
+        before = stats_ref[group, 0:1, :]
+        top = jnp.maximum(before, jnp.max(scores[group], axis=0, keepdims=True))
+        exps = jnp.exp2(scores[group] - top)
+        factor = jnp.exp2(before - top)
+        total = factor * stats_ref[group, 1:2, :] + jnp.sum(exps, axis=0, keepdims=True)
+        found.append((top, factor, total, exps.astype(jnp.bfloat16)))
+    return [
+        (top, factor, total, weighted_values(pairs, columns, exps))
+        for columns, (top, factor, total, exps) in zip(spans, found)
+    ]
+
+
+def middle_kernel(sizes, q_ref, self_ref, stats_ref, pair_ref, out_ref, stats_out_ref):
+    kv_local, group_size, first = sizes
+    stats_out_ref[kv_local, 0:1, :] = stats_ref[kv_local, 0:1, :]
+    found = absorbed((kv_local, group_size), first, pair_ref, q_ref, stats_ref)
+    for group, (top, factor, total, added) in enumerate(found):
+        out_ref[group] = self_ref[group] * factor + added
+        stats_out_ref[group, 0:1, :] = top
+        stats_out_ref[group, 1:2, :] = total
+
+
+def late_kernel(
+    sizes, q_ref, cross_ref, self_ref, stats_ref, pair_ref, out_hbm, out_ref, sems
+):
+    kv_local, group_size, first = sizes
+    tok_rows = q_ref.shape[0]
+    found = absorbed((kv_local, group_size), first, pair_ref, q_ref, stats_ref)
+    copies = []
+    for group, (_, factor, total, added) in enumerate(found):
+        inverse = 1.0 / total
+        self_out = self_ref[group] * (factor * inverse) + added * inverse
+        merged = (self_out + cross_ref[group]).astype(jnp.bfloat16)
         for c in range(group_size):
-            head = group * group_size + c
-            out_ref[:, head * HD : (head + 1) * HD] = jnp.transpose(
+            out_ref[group, :, c * HD : (c + 1) * HD] = jnp.transpose(
                 merged[:, c * tok_rows : (c + 1) * tok_rows]
             )
-
-
-def product_kernel(sizes, terms_ref, *rest):
-    slots, vision, out_rows, steps, parts, row_firsts = sizes
-    blocks = len(row_firsts)
-    rows, outs = list(zip(rest[:blocks], row_firsts)), rest[blocks : blocks + steps]
-    sum_ref, turned_ref = rest[blocks + steps :]
+        span = group_size * HD
+        copies.append(
+            pltpu.make_async_copy(
+                out_ref.at[group], out_hbm.at[:, pl.ds(group * span, span)], sems.at[group]
+            )
+        )
+        copies[-1].start()
+    for copy in copies:
+        copy.wait()
+
+
+def product_kernel(sizes, *rest):
+    slots, vision, out_rows, steps, parts, blocks = sizes
+    terms, rows, outs = rest[:blocks], rest[blocks : 2 * blocks], rest[2 * blocks : -2]
+    sum_ref, turned_ref = rest[-2:]
     seq_at, dp_at = lax.axis_index("seq"), lax.axis_index("dp")
-    width = terms_ref.shape[2]
-    total = terms_ref[0].astype(jnp.float32)
-    for b in range(1, blocks):
-        total = total + terms_ref[b].astype(jnp.float32)
+    width = sum_ref.shape[1]
+    total = terms[0][...].astype(jnp.float32)
+    for ref in terms[1:]:
+        total = total + ref[...].astype(jnp.float32)
     sum_ref[...] = total.astype(jnp.bfloat16)
     grads = jnp.concatenate(
         [
@@ -380,8 +457,8 @@
     return [pl.BlockSpec(memory_space=pltpu.VMEM)] * count
 
 
-def swap(array, axis, size, x):
-    return lax.ppermute(array, axis, [(i, i ^ x) for i in range(size)])
+def dp_order(size):
+    return sorted(range(1, size), key=lambda x: (x == 1, x))
 
 
 def on_device_small(
@@ -412,23 +489,33 @@
     hbm = pl.BlockSpec(memory_space=pltpu.HBM)
     parts = -(-vision // width)
     feature_rows = parts * slots
-    kv_rows = 2 * tok_rows
-    all_rows = slots + feature_rows + kv_rows
-
-    keys_own, rows_own, kv_own, all_own, meta = pl.pallas_call(
+    far, near = seq_size // 2, 1
+
+    def swapped(array, axis, size, x):
+        return lax.ppermute(array, axis, [(i, i ^ x) for i in range(size)])
+
+    def gathered(array):
+        there = swapped(array, "seq", seq_size, far)
+        beside = swapped(array, "seq", seq_size, near)
+        across = swapped(there, "seq", seq_size, near)
+        return (array, beside, there, across)
+
+    key_blocks = gathered(img_keys[0])
+
+    rows_own, kv_own, meta = pl.pallas_call(
         functools.partial(pack_kernel, (slots, parts, key_count // images)),
-        out_shape=tuple(
-            jax.ShapeDtypeStruct((rows, width), jnp.bfloat16)
-            for rows in (slots, feature_rows, kv_rows, all_rows)
-        )
-        + (jax.ShapeDtypeStruct((8, tok_rows), jnp.int32),),
-        in_specs=[hbm] * 7,
-        out_specs=tuple(vmem_specs(5)),
+        out_shape=(
+            jax.ShapeDtypeStruct((feature_rows, width), jnp.bfloat16),
+            jax.ShapeDtypeStruct((2 * tok_rows, width), jnp.bfloat16),
+            jax.ShapeDtypeStruct((8, tok_rows), jnp.int32),
+        ),
+        in_specs=[hbm] * 6,
+        out_specs=tuple(vmem_specs(3)),
         scratch_shapes=[
             pltpu.VMEM(docs.shape, jnp.int32),
             pltpu.SMEM(tiles.shape, jnp.int32),
             pltpu.SMEM(cite.shape, jnp.int32),
-            pltpu.SemaphoreType.DMA((9 + 2 * parts,)),
+            pltpu.SemaphoreType.DMA((5 + parts,)),
         ],
         compiler_params=pltpu.CompilerParams(vmem_limit_bytes=8 << 20),
         cost_estimate=pl.CostEstimate(flops=4 << 30, bytes_accessed=16 << 20, transcendentals=0),
@@ -436,24 +523,10 @@
     )(
         *[
             pltpu.with_memory_space_constraint(array, pltpu.HBM)
-            for array in (docs, tiles, cite, img_keys, features, k_self, v_self)
+            for array in (docs, tiles, cite, features, k_self, v_self)
         ]
     )
-    far, near = seq_size // 2, 1
-
-    def far_and_across(array):
-        there = swap(array, "seq", seq_size, far)
-        return there, swap(there, "seq", seq_size, near)
-
-    keys_far, keys_across = far_and_across(keys_own)
-    rows_far, rows_across = far_and_across(rows_own)
-    kv_far, kv_across = far_and_across(kv_own)
-    all_near = swap(all_own, "seq", seq_size, near)
-    key_blocks = (all_own, all_near, keys_far, keys_across)
-    row_blocks = (all_own, all_near, rows_far, rows_across)
-    kv_blocks = (all_own, all_near, kv_far, kv_across)
-    row_firsts = (slots, slots, 0, 0)
-    kv_firsts = (slots + feature_rows, slots + feature_rows, 0, 0)
+    row_blocks = gathered(rows_own)
 
     grad_terms, weights = pl.pallas_call(
         functools.partial(cross_kernel, (kv_local, group_size, slots, seq_size)),
@@ -466,14 +539,17 @@
         compiler_params=pltpu.CompilerParams(vmem_limit_bytes=24 << 20),
         name="cross",
     )(meta, q_cross[0], cotangent[0], *key_blocks)
-    terms_all = lax.all_gather(grad_terms, "seq", axis=0)
+    term_blocks = gathered(grad_terms)
+    kv_blocks = gathered(kv_own)
     blocks_out = pl.pallas_call(
-        functools.partial(product_kernel, (slots, vision, out_rows, dp_size, parts, row_firsts)),
+        functools.partial(
+            product_kernel, (slots, vision, out_rows, dp_size, parts, seq_size)
+        ),
         out_shape=tuple(
             jax.ShapeDtypeStruct((out_rows, width), jnp.bfloat16 if x else jnp.float32)
             for x in range(dp_size)
         ),
-        in_specs=vmem_specs(1 + seq_size),
+        in_specs=vmem_specs(2 * seq_size),
         out_specs=tuple(vmem_specs(dp_size)),
         scratch_shapes=[
             pltpu.VMEM((key_count, width), jnp.bfloat16),
@@ -481,24 +557,44 @@
         ],
         compiler_params=pltpu.CompilerParams(vmem_limit_bytes=16 << 20),
         name="product",
-    )(terms_all, *row_blocks)
-    arrived = []
-    for x in range(dp_size - 1, 0, -1):
-        arrived.append(swap(blocks_out[x], "dp", dp_size, x))
+    )(*term_blocks, *row_blocks)
     weight_grad = blocks_out[0]
-    for block in arrived:
-        weight_grad = weight_grad + block.astype(jnp.float32)
-
+    for x in dp_order(dp_size):
+        arrived = swapped(blocks_out[x], "dp", dp_size, x)
+        weight_grad = weight_grad + arrived.astype(jnp.float32)
+
+    chip = seq_size // 2
+    columns = group_size * tok_rows
+    partial_shape = jax.ShapeDtypeStruct((kv_local, HD, columns), jnp.float32)
+    stats_shape = jax.ShapeDtypeStruct((kv_local + 1, 8, columns), jnp.float32)
+    cross_out, partial, stats = pl.pallas_call(
+        functools.partial(early_kernel, (kv_local, group_size, slots, parts, seq_size, chip)),
+        out_shape=(partial_shape, partial_shape, stats_shape),
+        in_specs=vmem_specs(4 + seq_size + chip),
+        out_specs=tuple(vmem_specs(3)),
+        compiler_params=pltpu.CompilerParams(vmem_limit_bytes=24 << 20),
+        name="early",
+    )(meta, q_self[0], w_value, weights, *row_blocks, *kv_blocks[:chip])
+    partial, stats = pl.pallas_call(
+        functools.partial(middle_kernel, (kv_local, group_size, chip)),
+        out_shape=(partial_shape, stats_shape),
+        in_specs=vmem_specs(4),
+        out_specs=tuple(vmem_specs(2)),
+        compiler_params=pltpu.CompilerParams(vmem_limit_bytes=16 << 20),
+        name="middle",
+    )(q_self[0], partial, stats, kv_blocks[chip])
     merged = pl.pallas_call(
-        functools.partial(
-            attend_kernel, (kv_local, group_size, slots, parts, row_firsts, kv_firsts)
-        ),
+        functools.partial(late_kernel, (kv_local, group_size, chip + 1)),
         out_shape=jax.ShapeDtypeStruct((tok_rows, heads_local * HD), jnp.bfloat16),
-        in_specs=vmem_specs(4 + 2 * seq_size),
-        out_specs=vmem_specs(1)[0],
-        compiler_params=pltpu.CompilerParams(vmem_limit_bytes=32 << 20),
-        name="attend",
-    )(meta, q_self[0], w_value, weights, *row_blocks, *kv_blocks)
+        in_specs=vmem_specs(5),
+        out_specs=hbm,
+        scratch_shapes=[
+            pltpu.VMEM((kv_local, tok_rows, group_size * HD), jnp.bfloat16),
+            pltpu.SemaphoreType.DMA((kv_local,)),
+        ],
+        compiler_params=pltpu.CompilerParams(vmem_limit_bytes=16 << 20),
+        name="late",
+    )(q_self[0], cross_out, partial, stats, kv_blocks[chip + 1])
     return (merged[None], weight_grad)
 
 

time: 37.5 us -> 31.8 us (0.85)
  blocking collectives: 9.13 us -> 0 us
  starting transfers between devices: 9.73 us -> 13 us
  waiting for transfers between devices: 10.8 us -> 11.2 us
  Pallas kernels: 6.27 us -> 5.88 us
    all_gather x1 -> x0, blocking collectives: 9.13 us -> none  [on_device_small(): terms_all = lax.all_gather(grad_terms, 'seq', axis=0)]
    ppermute x10 -> x15, starting transfers between devices: 9.73 us -> 13 us  [swapped(): return lax.ppermute(array, axis, [(i, i ^ x) for i in range(size)])]
    pallas_call x1, Pallas kernels: 1.23 us -> 0.7 us  [on_device_small(): pl.pallas_call(functools.partial(cross_kernel, (kv_local, group_size, slo...]
    ppermute x10 -> x15, waiting for transfers between devices: 10.8 us -> 11.2 us  [swapped(): return lax.ppermute(array, axis, [(i, i ^ x) for i in range(size)])]
    pallas_call x1 -> x3, Pallas kernels: 3.22 us -> 3.69 us  [the longest x1 1.55 us: on_device_small(): pl.pallas_call(functools.partial(late_kernel, (kv_local, group_size, chip...]
  transfers between devices with their start and end apart: 10 -> 15, of which waited for: 3 -> 8; matrix products, arithmetic and copies ran while one was open for 2% -> 2% of each run, Pallas kernels for 4% -> 11%
where the time goes in v4:
time: 31.8 us; the launch traced here: 31.6 us
  starting transfers between devices  13 us (41%)
  waiting for transfers between devices  11.2 us (35%)
  Pallas kernels  5.88 us (18%)
  between operations  0.75 us (2%)
  other arithmetic  0.7 us (2%)
    ppermute x15, starting transfers between devices, swapped(): return lax.ppermute(array, axis, [(i, i ^ x) for i in range(size)])  13 us
    ppermute x15, waiting for transfers between devices, swapped(): return lax.ppermute(array, axis, [(i, i ^ x) for i in range(size)])  11.2 us
    pallas_call x1, Pallas kernels, on_device_small(): pl.pallas_call(functools.partial(late_kernel, (kv_local, group_size, chip...  1.55 us
    pallas_call x1, Pallas kernels, on_device_small(): pl.pallas_call(functools.partial(early_kernel, (kv_local, group_size, slo...  1.47 us
    pallas_call x1, Pallas kernels, on_device_small(): pl.pallas_call(functools.partial(pack_kernel, (slots, parts, key_count //...  1.11 us
    pallas_call x1, Pallas kernels, on_device_small(): pl.pallas_call(functools.partial(cross_kernel, (kv_local, group_size, slo...  0.7 us
    add x1, other arithmetic, on_device_small(): weight_grad = weight_grad + arrived.astype(jnp.float32)  0.7 us
    pallas_call x1, Pallas kernels, on_device_small(): pl.pallas_call(functools.partial(middle_kernel, (kv_local, group_size, ch...  0.67 us
  transfers between devices with their start and end apart: 15, of which 8 were waited for; matrix products, arithmetic and copies ran while one was open for 2% of the time, Pallas kernels for 11%

profile of v4, /device:TPU:0, one launch (start us, length us, event | category | flops | bytes accessed | tf_op | source)
XLA Modules:
  0.0 31.6 jit_solution(4643689098434989333)
XLA Ops:
  0.7 3.1 %collective-permute-start.1 = (bf16[32,512]{1,0:T(8,128)(2,1)}, bf16[32,512]{1,0:T(8,128)(2,1)S(1)}, u32[]{:S(2)}, u32[]{:S(2)}) collective-permute-start(bf16[32,512]{1,0:T(8,128)(2,1)} %bitcast.10), channel_id=1, source_target_pairs={{0,4},{2,6},{4,0},{6,2},{1,5},{3,7},{5,1},{7,3},{8,12},{10,14},{12... | collective-permute-start | bytes 98312 | tf_op jit(solution)/shard_map/ppermute | solution.py:495
  3.7 2.1 %collective-permute-done.1.rest_2_ = bf16[32,512]{1,0:T(8,128)(2,1)S(1)} collective-permute-done((bf16[32,512]{1,0:T(8,128)(2,1)}, bf16[32,512]{1,0:T(8,128)(2,1)S(1)}, u32[]{:S(2)}, u32[]{:S(2)}) %collective-permute-start.1) | collective-permute-done | bytes 32800 | tf_op jit(solution)/shard_map/ppermute | solution.py:495
  5.8 1.1 %pack.1 = (bf16[96,512]{1,0:T(8,128)(2,1)S(1)}, bf16[256,512]{1,0:T(8,128)(2,1)S(1)}, s32[8,128]{1,0:T(8,128)S(1)}) custom-call(s32[1,128]{1,0:T(1,128)} %docs_hbm.1, s32[1,4]{1,0:T(1,128)} %tiles_hbm.1, s32[1,4]{1,0:T(1,128)} %cite_hbm.1, bf16[1,32,1280]{2,1,0:T(8,128)(2,1)} %features_hbm.1, bf16[1,128,512]{2,1,0:T(8,128)(2,1)} %k_hbm.1, ...), custom_call_target="tpu_custom_call" | custom-call | flops 4294967296 | bytes 16777216 | tf_op jit(solution)/shard_map/pack/pallas_call | solution.py:505
  7.0 0.7 %cross.1 = (bf16[128,512]{1,0:T(8,128)(2,1)S(1)}, bf16[4,128,512]{2,1,0:T(8,128)(2,1)S(1)}) custom-call(s32[8,128]{1,0:T(8,128)S(1)} %get-tuple-element.16.meta_ref, bf16[128,2048]{1,0:T(8,128)(2,1)S(1)} %bitcast.8, bf16[128,2048]{1,0:T(8,128)(2,1)S(1)} %bitcast.9, bf16[32,512]{1,0:T(8,128)(2,1)S(1)} %bitcast.12, ...), custom_call_target="tpu_custom_call" | custom-call | tf_op jit(solution)/shard_map/cross/pallas_call | solution.py:531
  7.8 2.1 %collective-permute-start.10 = (bf16[128,512]{1,0:T(8,128)(2,1)S(1)}, bf16[128,512]{1,0:T(8,128)(2,1)S(1)}, u32[]{:S(2)}, u32[]{:S(2)}) collective-permute-start(bf16[128,512]{1,0:T(8,128)(2,1)S(1)} %get-tuple-element.25.rest_0_), channel_id=1, source_target_pairs={{0,4},{2,6},{4,0},{6,2},{1,5},{3,7},{5,1},{7,3},{8,12},{10,14},{12... | collective-permute-start | bytes 393224 | tf_op jit(solution)/shard_map/ppermute | solution.py:495
  9.8 0.1 collective-permute-start.4
  9.9 1.9 %collective-permute-start.7 = (bf16[256,512]{1,0:T(8,128)(2,1)S(1)}, bf16[256,512]{1,0:T(8,128)(2,1)S(1)}, u32[]{:S(2)}, u32[]{:S(2)}) collective-permute-start(bf16[256,512]{1,0:T(8,128)(2,1)S(1)} %get-tuple-element.19.rest_4_), channel_id=1, source_target_pairs={{0,4},{2,6},{4,0},{6,2},{1,5},{3,7},{5,1},{7,3},{8,12},{10,14},{12... | collective-permute-start | bytes 786440 | tf_op jit(solution)/shard_map/ppermute | solution.py:495
  11.9 0.5 %collective-permute-start.6 = (bf16[256,512]{1,0:T(8,128)(2,1)S(1)}, bf16[256,512]{1,0:T(8,128)(2,1)S(1)}, u32[]{:S(2)}, u32[]{:S(2)}) collective-permute-start(bf16[256,512]{1,0:T(8,128)(2,1)S(1)} %get-tuple-element.19.rest_4_), channel_id=1, source_target_pairs={{0,2},{2,0},{4,6},{6,4},{1,3},{3,1},{5,7},{7,5},{8,10},{10,8},{12,... | collective-permute-start | bytes 786440 | tf_op jit(solution)/shard_map/ppermute | solution.py:495
  12.4 3.9 %collective-permute-done.4.rest_2_.rest_6_ = bf16[96,512]{1,0:T(8,128)(2,1)S(1)} collective-permute-done((bf16[96,512]{1,0:T(8,128)(2,1)S(1)}, bf16[96,512]{1,0:T(8,128)(2,1)S(1)}, u32[]{:S(2)}, u32[]{:S(2)}) %collective-permute-start.4) | collective-permute-done | bytes 98336 | tf_op jit(solution)/shard_map/ppermute | solution.py:495
  16.3 0.5 %collective-permute-start.11 = (bf16[128,512]{1,0:T(8,128)(2,1)S(1)}, bf16[128,512]{1,0:T(8,128)(2,1)S(1)}, u32[]{:S(2)}, u32[]{:S(2)}) collective-permute-start(bf16[128,512]{1,0:T(8,128)(2,1)S(1)} %collective-permute-done.10.rest_2_), channel_id=1, source_target_pairs={{0,2},{2,0},{4,6},{6,4},{1,3},{3,1},{5,7},{7,5},{8,10},{10,8},{12,... | collective-permute-start | bytes 393224 | tf_op jit(solution)/shard_map/ppermute | solution.py:495
  16.8 0.1 collective-permute-start.5
  16.9 0.8 %collective-permute-done.9.rest_1_ = bf16[128,512]{1,0:T(8,128)(2,1)S(1)} collective-permute-done((bf16[128,512]{1,0:T(8,128)(2,1)S(1)}, bf16[128,512]{1,0:T(8,128)(2,1)S(1)}, u32[]{:S(2)}, u32[]{:S(2)}) %collective-permute-start.9) | collective-permute-done | bytes 131104 | tf_op jit(solution)/shard_map/ppermute | solution.py:495
  17.7 0.5 %collective-permute-done.5.rest_3_.rest_7_ = bf16[96,512]{1,0:T(8,128)(2,1)S(1)} collective-permute-done((bf16[96,512]{1,0:T(8,128)(2,1)S(1)}, bf16[96,512]{1,0:T(8,128)(2,1)S(1)}, u32[]{:S(2)}, u32[]{:S(2)}) %collective-permute-start.5) | collective-permute-done | bytes 98336 | tf_op jit(solution)/shard_map/ppermute | solution.py:495
  18.1 0.4 %product.1 = (f32[80,512]{1,0:T(8,128)S(1)}, bf16[80,512]{1,0:T(8,128)(2,1)S(1)}, bf16[80,512]{1,0:T(8,128)(2,1)S(1)}, bf16[80,512]{1,0:T(8,128)(2,1)S(1)}) custom-call(bf16[128,512]{1,0:T(8,128)(2,1)S(1)} %get-tuple-element.25.rest_0_, bf16[128,512]{1,0:T(8,128)(2,1)S(1)} %collective-permute-done.9.rest_1_, ...), custom_call_target="tpu_custom_call" | custom-call | tf_op jit(solution)/shard_map/product/pallas_call | solution.py:544
  18.5 3.2 %collective-permute-start.12 = (bf16[80,512]{1,0:T(8,128)(2,1)S(1)}, bf16[80,512]{1,0:T(8,128)(2,1)S(1)}, u32[]{:S(2)}, u32[]{:S(2)}) collective-permute-start(bf16[80,512]{1,0:T(8,128)(2,1)S(1)} %get-tuple-element.27), channel_id=1, source_target_pairs={{0,16},{8,24},{16,0},{24,8},{1,17},{9,25},{17,1},{25,9},{2,18},{10... | collective-permute-start | bytes 245768 | tf_op jit(solution)/shard_map/ppermute | solution.py:495
  21.7 1.3 %collective-permute-start.13 = (bf16[80,512]{1,0:T(8,128)(2,1)S(1)}, bf16[80,512]{1,0:T(8,128)(2,1)S(1)}, u32[]{:S(2)}, u32[]{:S(2)}) collective-permute-start(bf16[80,512]{1,0:T(8,128)(2,1)S(1)} %get-tuple-element.28), channel_id=1, source_target_pairs={{0,24},{8,16},{16,8},{24,0},{1,25},{9,17},{17,9},{25,1},{2,26},{10... | collective-permute-start | bytes 245768 | tf_op jit(solution)/shard_map/ppermute | solution.py:495
  23.0 0.2 collective-permute-start.14
  23.3 1.5 %early.1 = (f32[4,128,512]{2,1,0:T(8,128)S(1)}, f32[4,128,512]{2,1,0:T(8,128)S(1)}, f32[5,8,512]{2,1,0:T(8,128)S(1)}) custom-call(s32[8,128]{1,0:T(8,128)S(1)} %get-tuple-element.16.meta_ref, bf16[128,2048]{1,0:T(8,128)(2,1)S(1)} %bitcast.5, bf16[1280,512]{1,0:T(8,128)(2,1)S(1)} %copy-done.1, bf16[4,128,512]{2,1,0:T(8,128)(2,1)S(1)} %get-tuple-element.17.weights_ref, ...), custom_call_target="tpu_custom_call" | custom-call | tf_op jit(solution)/shard_map/early/pallas_call | solution.py:570
  24.7 0.7 %middle.1 = (f32[4,128,512]{2,1,0:T(8,128)S(1)}, f32[5,8,512]{2,1,0:T(8,128)S(1)}) custom-call(bf16[128,2048]{1,0:T(8,128)(2,1)S(1)} %bitcast.6, f32[4,128,512]{2,1,0:T(8,128)S(1)} %get-tuple-element.21.self_ref, f32[5,8,512]{2,1,0:T(8,128)S(1)} %get-tuple-element.22.stats_ref, bf16[256,512]{1,0:T(8,128)(2,1)S(1)} %collective-permute-done.7.pair_ref), custom_call_target="tpu_custom_call" | custom-call | tf_op jit(solution)/shard_map/middle/pallas_call | solution.py:578
  25.4 2.7 %collective-permute-done.12 = bf16[80,512]{1,0:T(8,128)(2,1)S(1)} collective-permute-done((bf16[80,512]{1,0:T(8,128)(2,1)S(1)}, bf16[80,512]{1,0:T(8,128)(2,1)S(1)}, u32[]{:S(2)}, u32[]{:S(2)}) %collective-permute-start.12) | collective-permute-done | bytes 81952 | tf_op jit(solution)/shard_map/ppermute | solution.py:495
  28.2 0.4 %collective-permute-done.13 = bf16[80,512]{1,0:T(8,128)(2,1)S(1)} collective-permute-done((bf16[80,512]{1,0:T(8,128)(2,1)S(1)}, bf16[80,512]{1,0:T(8,128)(2,1)S(1)}, u32[]{:S(2)}, u32[]{:S(2)}) %collective-permute-start.13) | collective-permute-done | bytes 81952 | tf_op jit(solution)/shard_map/ppermute | solution.py:495
  28.6 0.8 %collective-permute-done.14 = bf16[80,512]{1,0:T(8,128)(2,1)S(1)} collective-permute-done((bf16[80,512]{1,0:T(8,128)(2,1)S(1)}, bf16[80,512]{1,0:T(8,128)(2,1)S(1)}, u32[]{:S(2)}, u32[]{:S(2)}) %collective-permute-start.14) | collective-permute-done | bytes 81952 | tf_op jit(solution)/shard_map/ppermute | solution.py:495
  29.3 0.7 %convert_add_fusion = f32[80,512]{1,0:T(8,128)} fusion(bf16[80,512]{1,0:T(8,128)(2,1)S(1)} %collective-permute-done.14, bf16[80,512]{1,0:T(8,128)(2,1)S(1)} %collective-permute-done.13, f32[80,512]{1,0:T(8,128)S(1)} %get-tuple-element.26, bf16[80,512]{1,0:T(8,128)(2,1)S(1)} %collective-permute-done.12), kind=kLoop, calls=%fused_computation | loop fusion | flops 245760 | bytes 573440 | tf_op jit(solution)/shard_map/add | solution.py:564
  30.0 1.5 %late.1 = bf16[128,2048]{1,0:T(8,128)(2,1)} custom-call(bf16[128,2048]{1,0:T(8,128)(2,1)S(1)} %bitcast.7, f32[4,128,512]{2,1,0:T(8,128)S(1)} %get-tuple-element.20.cross_ref, f32[4,128,512]{2,1,0:T(8,128)S(1)} %get-tuple-element.23.self_ref, f32[5,8,512]{2,1,0:T(8,128)S(1)} %get-tuple-element.24.stats_ref, bf16[256,512]{1,0:T(8,128)(2,1)S(1)} %collective-permute-done.8.pair_ref), custom_call_target="tpu_custom_call" | custom-call | tf_op jit(solution)/shard_map/late/pallas_call | solution.py:586
  (23 shorter events, 0.1 us)
Async XLA Ops:
  0.6 6.4 %copy-start.2 = (bf16[1,128,2048]{2,1,0:T(8,128)(2,1)S(1)}, bf16[1,128,2048]{2,1,0:T(8,128)(2,1)}, u32[]{:S(2)}) copy-start(bf16[1,128,2048]{2,1,0:T(8,128)(2,1)} %param.15) | copy-start | bytes 1572868
  0.6 6.4 %copy-start.3 = (bf16[1,128,2048]{2,1,0:T(8,128)(2,1)S(1)}, bf16[1,128,2048]{2,1,0:T(8,128)(2,1)}, u32[]{:S(2)}) copy-start(bf16[1,128,2048]{2,1,0:T(8,128)(2,1)} %param.16) | copy-start | bytes 1572868
  0.7 6.4 %copy-start.4 = (bf16[1,32,512]{2,1,0:T(8,128)(2,1)S(1)}, bf16[1,32,512]{2,1,0:T(8,128)(2,1)}, u32[]{:S(2)}) copy-start(bf16[1,32,512]{2,1,0:T(8,128)(2,1)} %param.17) | copy-start | bytes 98308
  0.7 5.2 %collective-permute-start.1 = (bf16[32,512]{1,0:T(8,128)(2,1)}, bf16[32,512]{1,0:T(8,128)(2,1)S(1)}, u32[]{:S(2)}, u32[]{:S(2)}) collective-permute-start(bf16[32,512]{1,0:T(8,128)(2,1)} %bitcast.10), channel_id=1, source_target_pairs={{0,4},{2,6},{4,0},{6,2},{1,5},{3,7},{5,1},{7,3},{8,12},{10,14},{12... | collective-permute-start | bytes 98312 | tf_op jit(solution)/shard_map/ppermute | solution.py:495
  3.7 3.3 %collective-permute-start = (bf16[32,512]{1,0:T(8,128)(2,1)}, bf16[32,512]{1,0:T(8,128)(2,1)S(1)}, u32[]{:S(2)}, u32[]{:S(2)}) collective-permute-start(bf16[32,512]{1,0:T(8,128)(2,1)} %bitcast.11), channel_id=1, source_target_pairs={{0,2},{2,0},{4,6},{6,4},{1,3},{3,1},{5,7},{7,5},{8,10},{10,8},{12,... | collective-permute-start | bytes 98312 | tf_op jit(solution)/shard_map/ppermute | solution.py:495
  5.8 1.2 %collective-permute-start.2 = (bf16[32,512]{1,0:T(8,128)(2,1)S(1)}, bf16[32,512]{1,0:T(8,128)(2,1)S(1)}, u32[]{:S(2)}, u32[]{:S(2)}) collective-permute-start(bf16[32,512]{1,0:T(8,128)(2,1)S(1)} %collective-permute-done.1.rest_2_), channel_id=1, source_target_pairs={{0,2},{2,0},{4,6},{6,4},{1,3},{3,1},{5,7},{7,5},{8,10},{10,8},{12,... | collective-permute-start | bytes 98312 | tf_op jit(solution)/shard_map/ppermute | solution.py:495
  7.0 16.3 %copy-start = (bf16[1,128,2048]{2,1,0:T(8,128)(2,1)S(1)}, bf16[1,128,2048]{2,1,0:T(8,128)(2,1)}, u32[]{:S(2)}) copy-start(bf16[1,128,2048]{2,1,0:T(8,128)(2,1)} %param.11) | copy-start | bytes 1572868
  7.0 16.3 %copy-start.1 = (bf16[1280,512]{1,0:T(8,128)(2,1)S(1)}, bf16[1280,512]{1,0:T(8,128)(2,1)}, u32[]{:S(2)}) copy-start(bf16[1280,512]{1,0:T(8,128)(2,1)} %w_ref.1) | copy-start | bytes 3932164
  7.8 8.5 %collective-permute-start.10 = (bf16[128,512]{1,0:T(8,128)(2,1)S(1)}, bf16[128,512]{1,0:T(8,128)(2,1)S(1)}, u32[]{:S(2)}, u32[]{:S(2)}) collective-permute-start(bf16[128,512]{1,0:T(8,128)(2,1)S(1)} %get-tuple-element.25.rest_0_), channel_id=1, source_target_pairs={{0,4},{2,6},{4,0},{6,2},{1,5},{3,7},{5,1},{7,3},{8,12},{10,14},{12... | collective-permute-start | bytes 393224 | tf_op jit(solution)/shard_map/ppermute | solution.py:495
  9.8 6.5 %collective-permute-start.4 = (bf16[96,512]{1,0:T(8,128)(2,1)S(1)}, bf16[96,512]{1,0:T(8,128)(2,1)S(1)}, u32[]{:S(2)}, u32[]{:S(2)}) collective-permute-start(bf16[96,512]{1,0:T(8,128)(2,1)S(1)} %get-tuple-element.18.rest_0_.rest_4_), channel_id=1, source_target_pairs={{0,4},{2,6},{4,0},{6,2},{1,5},{3,7},{5,1},{7,3},{8,12},{10,14},{12... | collective-permute-start | bytes 294920 | tf_op jit(solution)/shard_map/ppermute | solution.py:495
  9.9 13.3 %collective-permute-start.7 = (bf16[256,512]{1,0:T(8,128)(2,1)S(1)}, bf16[256,512]{1,0:T(8,128)(2,1)S(1)}, u32[]{:S(2)}, u32[]{:S(2)}) collective-permute-start(bf16[256,512]{1,0:T(8,128)(2,1)S(1)} %get-tuple-element.19.rest_4_), channel_id=1, source_target_pairs={{0,4},{2,6},{4,0},{6,2},{1,5},{3,7},{5,1},{7,3},{8,12},{10,14},{12... | collective-permute-start | bytes 786440 | tf_op jit(solution)/shard_map/ppermute | solution.py:495
  11.9 5.0 %collective-permute-start.3 = (bf16[96,512]{1,0:T(8,128)(2,1)S(1)}, bf16[96,512]{1,0:T(8,128)(2,1)S(1)}, u32[]{:S(2)}, u32[]{:S(2)}) collective-permute-start(bf16[96,512]{1,0:T(8,128)(2,1)S(1)} %get-tuple-element.18.rest_0_.rest_4_), channel_id=1, source_target_pairs={{0,2},{2,0},{4,6},{6,4},{1,3},{3,1},{5,7},{7,5},{8,10},{10,8},{12,... | collective-permute-start | bytes 294920 | tf_op jit(solution)/shard_map/ppermute | solution.py:495
  11.9 11.4 %collective-permute-start.6 = (bf16[256,512]{1,0:T(8,128)(2,1)S(1)}, bf16[256,512]{1,0:T(8,128)(2,1)S(1)}, u32[]{:S(2)}, u32[]{:S(2)}) collective-permute-start(bf16[256,512]{1,0:T(8,128)(2,1)S(1)} %get-tuple-element.19.rest_4_), channel_id=1, source_target_pairs={{0,2},{2,0},{4,6},{6,4},{1,3},{3,1},{5,7},{7,5},{8,10},{10,8},{12,... | collective-permute-start | bytes 786440 | tf_op jit(solution)/shard_map/ppermute | solution.py:495
  16.3 1.3 %collective-permute-start.9 = (bf16[128,512]{1,0:T(8,128)(2,1)S(1)}, bf16[128,512]{1,0:T(8,128)(2,1)S(1)}, u32[]{:S(2)}, u32[]{:S(2)}) collective-permute-start(bf16[128,512]{1,0:T(8,128)(2,1)S(1)} %get-tuple-element.25.rest_0_), channel_id=1, source_target_pairs={{0,2},{2,0},{4,6},{6,4},{1,3},{3,1},{5,7},{7,5},{8,10},{10,8},{12,... | collective-permute-start | bytes 393224 | tf_op jit(solution)/shard_map/ppermute | solution.py:495
  16.3 1.8 %collective-permute-start.11 = (bf16[128,512]{1,0:T(8,128)(2,1)S(1)}, bf16[128,512]{1,0:T(8,128)(2,1)S(1)}, u32[]{:S(2)}, u32[]{:S(2)}) collective-permute-start(bf16[128,512]{1,0:T(8,128)(2,1)S(1)} %collective-permute-done.10.rest_2_), channel_id=1, source_target_pairs={{0,2},{2,0},{4,6},{6,4},{1,3},{3,1},{5,7},{7,5},{8,10},{10,8},{12,... | collective-permute-start | bytes 393224 | tf_op jit(solution)/shard_map/ppermute | solution.py:495
  16.8 1.3 %collective-permute-start.5 = (bf16[96,512]{1,0:T(8,128)(2,1)S(1)}, bf16[96,512]{1,0:T(8,128)(2,1)S(1)}, u32[]{:S(2)}, u32[]{:S(2)}) collective-permute-start(bf16[96,512]{1,0:T(8,128)(2,1)S(1)} %collective-permute-done.4.rest_2_.rest_6_), channel_id=1, source_target_pairs={{0,2},{2,0},{4,6},{6,4},{1,3},{3,1},{5,7},{7,5},{8,10},{10,8},{12,... | collective-permute-start | bytes 294920 | tf_op jit(solution)/shard_map/ppermute | solution.py:495
  18.5 9.7 %collective-permute-start.12 = (bf16[80,512]{1,0:T(8,128)(2,1)S(1)}, bf16[80,512]{1,0:T(8,128)(2,1)S(1)}, u32[]{:S(2)}, u32[]{:S(2)}) collective-permute-start(bf16[80,512]{1,0:T(8,128)(2,1)S(1)} %get-tuple-element.27), channel_id=1, source_target_pairs={{0,16},{8,24},{16,0},{24,8},{1,17},{9,25},{17,1},{25,9},{2,18},{10... | collective-permute-start | bytes 245768 | tf_op jit(solution)/shard_map/ppermute | solution.py:495
  21.7 6.9 %collective-permute-start.13 = (bf16[80,512]{1,0:T(8,128)(2,1)S(1)}, bf16[80,512]{1,0:T(8,128)(2,1)S(1)}, u32[]{:S(2)}, u32[]{:S(2)}) collective-permute-start(bf16[80,512]{1,0:T(8,128)(2,1)S(1)} %get-tuple-element.28), channel_id=1, source_target_pairs={{0,24},{8,16},{16,8},{24,0},{1,25},{9,17},{17,9},{25,1},{2,26},{10... | collective-permute-start | bytes 245768 | tf_op jit(solution)/shard_map/ppermute | solution.py:495
  23.0 6.3 %collective-permute-start.14 = (bf16[80,512]{1,0:T(8,128)(2,1)S(1)}, bf16[80,512]{1,0:T(8,128)(2,1)S(1)}, u32[]{:S(2)}, u32[]{:S(2)}) collective-permute-start(bf16[80,512]{1,0:T(8,128)(2,1)S(1)} %get-tuple-element.29), channel_id=1, source_target_pairs={{0,8},{8,0},{16,24},{24,16},{1,9},{9,1},{17,25},{25,17},{2,10},{10... | collective-permute-start | bytes 245768 | tf_op jit(solution)/shard_map/ppermute | solution.py:495
  23.2 6.8 %collective-permute-start.8 = (bf16[256,512]{1,0:T(8,128)(2,1)S(1)}, bf16[256,512]{1,0:T(8,128)(2,1)S(1)}, u32[]{:S(2)}, u32[]{:S(2)}) collective-permute-start(bf16[256,512]{1,0:T(8,128)(2,1)S(1)} %collective-permute-done.7.pair_ref), channel_id=1, source_target_pairs={{0,2},{2,0},{4,6},{6,4},{1,3},{3,1},{5,7},{7,5},{8,10},{10,8},{12,... | collective-permute-start | bytes 786440 | tf_op jit(solution)/shard_map/ppermute | solution.py:495

commit v5 on v4

--- a/solution.py
+++ b/solution.py
@@ -249,8 +249,8 @@
 
 def cross_kernel(sizes, meta_ref, q_ref, cot_ref, *rest):
     kv_local, group_size, slots, blocks = sizes
-    key_refs = rest[:blocks]
-    grad_ref, weights_ref = rest[blocks:]
+    key_refs, weights_ref, grad_refs = rest[:blocks], rest[blocks], rest[blocks + 1 :]
+    share = kv_local // len(grad_refs)
     seq_at = lax.axis_index("seq")
     tok_rows = q_ref.shape[0]
     bias = []
@@ -280,7 +280,9 @@
         )
         for x in range(blocks):
             at = pl.multiple_of((seq_at ^ x) * slots, slots)
-            grad_ref[pl.ds(at, slots), columns] = grads[x * slots : (x + 1) * slots]
+            grad_refs[group // share][pl.ds(at, slots), spans[group % share]] = grads[
+                x * slots : (x + 1) * slots
+            ]
 
 
 def stacked_features(rows, part, slots, cut):
@@ -330,7 +332,7 @@
 def early_kernel(sizes, meta_ref, q_ref, w_ref, weights_ref, *rest):
     kv_local, group_size, slots, parts, blocks, count = sizes
     rows, pairs = rest[:blocks], rest[blocks : blocks + count]
-    cross_ref, self_ref, stats_ref = rest[blocks + count :]
+    cross_ref, self_ref, stats_ref, turned_ref = rest[blocks + count :]
     width = pairs[0].shape[1]
     vision = w_ref.shape[0]
     seq_at = lax.axis_index("seq")
@@ -354,9 +356,9 @@
     total = None
     for part in range(parts):
         cut = min(width, vision - part * width)
-        term = dot_nn(
-            stacked_features(rows, part, slots, cut), w_ref[part * width : part * width + cut, :]
-        )
+        stacked = stacked_features(rows, part, slots, cut)
+        turned_ref[part * width : part * width + cut, :] = jnp.transpose(stacked)
+        term = dot_nn(stacked, w_ref[part * width : part * width + cut, :])
         total = term if total is None else total + term
     values = total.astype(jnp.bfloat16)
     for group in range(kv_local):
@@ -425,12 +427,10 @@
         copy.wait()
 
 
-def product_kernel(sizes, *rest):
-    slots, vision, out_rows, steps, parts, blocks = sizes
-    terms, rows, outs = rest[:blocks], rest[blocks : 2 * blocks], rest[2 * blocks : -2]
-    sum_ref, turned_ref = rest[-2:]
+def product_kernel(sizes, turned_ref, *rest):
+    slots, out_rows, steps, blocks = sizes
+    terms, outs, sum_ref = rest[:blocks], rest[blocks:-1], rest[-1]
     seq_at, dp_at = lax.axis_index("seq"), lax.axis_index("dp")
-    width = sum_ref.shape[1]
     total = terms[0][...].astype(jnp.float32)
     for ref in terms[1:]:
         total = total + ref[...].astype(jnp.float32)
@@ -442,11 +442,6 @@
         ],
         axis=0,
     )
-    for part in range(parts):
-        cut = min(width, vision - part * width)
-        turned_ref[part * width : part * width + cut, :] = jnp.transpose(
-            stacked_features(rows, part, slots, cut)
-        )
     for x in range(steps):
         row = pl.multiple_of(((dp_at ^ x) * blocks + seq_at) * out_rows, out_rows)
         block = dot_nn(turned_ref[pl.ds(row, out_rows), :], grads)
@@ -528,53 +523,60 @@
     )
     row_blocks = gathered(rows_own)
 
-    grad_terms, weights = pl.pallas_call(
+    halves = 1
+    half_width = width // halves
+    weights, *grad_terms = pl.pallas_call(
         functools.partial(cross_kernel, (kv_local, group_size, slots, seq_size)),
         out_shape=(
-            jax.ShapeDtypeStruct((key_count, width), jnp.bfloat16),
             jax.ShapeDtypeStruct((kv_local, key_count, group_size * tok_rows), jnp.bfloat16),
-        ),
+        )
+        + (jax.ShapeDtypeStruct((key_count, half_width), jnp.bfloat16),) * halves,
         in_specs=vmem_specs(3 + seq_size),
-        out_specs=tuple(vmem_specs(2)),
+        out_specs=tuple(vmem_specs(1 + halves)),
         compiler_params=pltpu.CompilerParams(vmem_limit_bytes=24 << 20),
         name="cross",
     )(meta, q_cross[0], cotangent[0], *key_blocks)
-    term_blocks = gathered(grad_terms)
     kv_blocks = gathered(kv_own)
-    blocks_out = pl.pallas_call(
-        functools.partial(
-            product_kernel, (slots, vision, out_rows, dp_size, parts, seq_size)
-        ),
-        out_shape=tuple(
-            jax.ShapeDtypeStruct((out_rows, width), jnp.bfloat16 if x else jnp.float32)
-            for x in range(dp_size)
-        ),
-        in_specs=vmem_specs(2 * seq_size),
-        out_specs=tuple(vmem_specs(dp_size)),
-        scratch_shapes=[
-            pltpu.VMEM((key_count, width), jnp.bfloat16),
-            pltpu.VMEM((vision, key_count), jnp.bfloat16),
-        ],
-        compiler_params=pltpu.CompilerParams(vmem_limit_bytes=16 << 20),
-        name="product",
-    )(*term_blocks, *row_blocks)
-    weight_grad = blocks_out[0]
-    for x in dp_order(dp_size):
-        arrived = swapped(blocks_out[x], "dp", dp_size, x)
-        weight_grad = weight_grad + arrived.astype(jnp.float32)
-
     chip = seq_size // 2
     columns = group_size * tok_rows
     partial_shape = jax.ShapeDtypeStruct((kv_local, HD, columns), jnp.float32)
     stats_shape = jax.ShapeDtypeStruct((kv_local + 1, 8, columns), jnp.float32)
-    cross_out, partial, stats = pl.pallas_call(
+    cross_out, partial, stats, turned = pl.pallas_call(
         functools.partial(early_kernel, (kv_local, group_size, slots, parts, seq_size, chip)),
-        out_shape=(partial_shape, partial_shape, stats_shape),
+        out_shape=(
+            partial_shape,
+            partial_shape,
+            stats_shape,
+            jax.ShapeDtypeStruct((vision, key_count), jnp.bfloat16),
+        ),
         in_specs=vmem_specs(4 + seq_size + chip),
-        out_specs=tuple(vmem_specs(3)),
+        out_specs=tuple(vmem_specs(4)),
         compiler_params=pltpu.CompilerParams(vmem_limit_bytes=24 << 20),
         name="early",
     )(meta, q_self[0], w_value, weights, *row_blocks, *kv_blocks[:chip])
+    sums = []
+    for half in range(halves):
+        term_blocks = gathered(grad_terms[half])
+        blocks_out = pl.pallas_call(
+            functools.partial(product_kernel, (slots, out_rows, dp_size, seq_size)),
+            out_shape=tuple(
+                jax.ShapeDtypeStruct(
+                    (out_rows, half_width), jnp.bfloat16 if x else jnp.float32
+                )
+                for x in range(dp_size)
+            ),
+            in_specs=vmem_specs(1 + seq_size),
+            out_specs=tuple(vmem_specs(dp_size)),
+            scratch_shapes=[pltpu.VMEM((key_count, half_width), jnp.bfloat16)],
+            compiler_params=pltpu.CompilerParams(vmem_limit_bytes=16 << 20),
+            name="product",
+        )(turned, *term_blocks)
+        total = blocks_out[0]
+        for x in dp_order(dp_size):
+            arrived = swapped(blocks_out[x], "dp", dp_size, x)
+            total = total + arrived.astype(jnp.float32)
+        sums.append(total)
+    weight_grad = jnp.concatenate(sums, axis=1)
     partial, stats = pl.pallas_call(
         functools.partial(middle_kernel, (kv_local, group_size, chip)),
         out_shape=(partial_shape, stats_shape),

time: 31.8 us -> 33.9 us (1.066)
  waiting for transfers between devices: 11.2 us -> 13.2 us
    ppermute x15, waiting for transfers between devices: 11.2 us -> 13.2 us  [swapped(): return lax.ppermute(array, axis, [(i, i ^ x) for i in range(size)])]
  transfers between devices with their start and end apart: 15 -> 15, of which waited for: 8 -> 6; matrix products, arithmetic and copies ran while one was open for 2% -> 2% of each run, Pallas kernels for 11% -> 13%
where the time goes in v5:
time: 33.9 us; the launch traced here: 33.7 us
  waiting for transfers between devices  13.2 us (39%)
  starting transfers between devices  13.1 us (39%)
  Pallas kernels  5.93 us (17%)
  between operations  0.76 us (2%)
  other arithmetic  0.71 us (2%)
    ppermute x15, waiting for transfers between devices, swapped(): return lax.ppermute(array, axis, [(i, i ^ x) for i in range(size)])  13.2 us
    ppermute x15, starting transfers between devices, swapped(): return lax.ppermute(array, axis, [(i, i ^ x) for i in range(size)])  13.1 us
    pallas_call x1, Pallas kernels, on_device_small(): pl.pallas_call(functools.partial(late_kernel, (kv_local, group_size, chip...  1.55 us
    pallas_call x1, Pallas kernels, on_device_small(): pl.pallas_call(functools.partial(early_kernel, (kv_local, group_size, slo...  1.49 us
    pallas_call x1, Pallas kernels, on_device_small(): pl.pallas_call(functools.partial(pack_kernel, (slots, parts, key_count //...  1.21 us
    add x1, other arithmetic, on_device_small(): total = total + arrived.astype(jnp.float32)  0.71 us
    pallas_call x1, Pallas kernels, on_device_small(): pl.pallas_call(functools.partial(cross_kernel, (kv_local, group_size, slo...  0.7 us
  transfers between devices with their start and end apart: 15, of which 6 were waited for; matrix products, arithmetic and copies ran while one was open for 2% of the time, Pallas kernels for 13%

profile of v5, /device:TPU:0, one launch (start us, length us, event | category | flops | bytes accessed | tf_op | source)
XLA Modules:
  0.0 33.7 jit_solution(4579626273490559087)
XLA Ops:
  0.7 3.1 %collective-permute-start.1 = (bf16[32,512]{1,0:T(8,128)(2,1)}, bf16[32,512]{1,0:T(8,128)(2,1)S(1)}, u32[]{:S(2)}, u32[]{:S(2)}) collective-permute-start(bf16[32,512]{1,0:T(8,128)(2,1)} %bitcast.10), channel_id=1, source_target_pairs={{0,4},{2,6},{4,0},{6,2},{1,5},{3,7},{5,1},{7,3},{8,12},{10,14},{12... | collective-permute-start | bytes 98312 | tf_op jit(solution)/shard_map/ppermute | solution.py:490
  3.7 2.1 %collective-permute-done.1.rest_2_ = bf16[32,512]{1,0:T(8,128)(2,1)S(1)} collective-permute-done((bf16[32,512]{1,0:T(8,128)(2,1)}, bf16[32,512]{1,0:T(8,128)(2,1)S(1)}, u32[]{:S(2)}, u32[]{:S(2)}) %collective-permute-start.1) | collective-permute-done | bytes 32800 | tf_op jit(solution)/shard_map/ppermute | solution.py:490
  5.8 1.2 %pack.1 = (bf16[96,512]{1,0:T(8,128)(2,1)S(1)}, bf16[256,512]{1,0:T(8,128)(2,1)S(1)}, s32[8,128]{1,0:T(8,128)S(1)}) custom-call(s32[1,128]{1,0:T(1,128)} %docs_hbm.1, s32[1,4]{1,0:T(1,128)} %tiles_hbm.1, s32[1,4]{1,0:T(1,128)} %cite_hbm.1, bf16[1,32,1280]{2,1,0:T(8,128)(2,1)} %features_hbm.1, bf16[1,128,512]{2,1,0:T(8,128)(2,1)} %k_hbm.1, ...), custom_call_target="tpu_custom_call" | custom-call | flops 4294967296 | bytes 16777216 | tf_op jit(solution)/shard_map/pack/pallas_call | solution.py:500
  7.0 0.0 copy-start
  7.1 0.6 %collective-permute-start.6 = (bf16[256,512]{1,0:T(8,128)(2,1)S(1)}, bf16[256,512]{1,0:T(8,128)(2,1)S(1)}, u32[]{:S(2)}, u32[]{:S(2)}) collective-permute-start(bf16[256,512]{1,0:T(8,128)(2,1)S(1)} %get-tuple-element.20.rest_4_), channel_id=1, source_target_pairs={{0,2},{2,0},{4,6},{6,4},{1,3},{3,1},{5,7},{7,5},{8,10},{10,8},{12,... | collective-permute-start | bytes 786440 | tf_op jit(solution)/shard_map/ppermute | solution.py:490
  7.7 0.7 %cross.1 = (bf16[4,128,512]{2,1,0:T(8,128)(2,1)S(1)}, bf16[128,512]{1,0:T(8,128)(2,1)S(1)}) custom-call(s32[8,128]{1,0:T(8,128)S(1)} %get-tuple-element.17.meta_ref, bf16[128,2048]{1,0:T(8,128)(2,1)S(1)} %bitcast.8, bf16[128,2048]{1,0:T(8,128)(2,1)S(1)} %bitcast.9, bf16[32,512]{1,0:T(8,128)(2,1)S(1)} %bitcast.12, ...), custom_call_target="tpu_custom_call" | custom-call | tf_op jit(solution)/shard_map/cross/pallas_call | solution.py:528
  8.4 2.1 %collective-permute-start.10 = (bf16[128,512]{1,0:T(8,128)(2,1)S(1)}, bf16[128,512]{1,0:T(8,128)(2,1)S(1)}, u32[]{:S(2)}, u32[]{:S(2)}) collective-permute-start(bf16[128,512]{1,0:T(8,128)(2,1)S(1)} %get-tuple-element.27.rest_0_), channel_id=1, source_target_pairs={{0,4},{2,6},{4,0},{6,2},{1,5},{3,7},{5,1},{7,3},{8,12},{10,14},{12... | collective-permute-start | bytes 393224 | tf_op jit(solution)/shard_map/ppermute | solution.py:490
  10.5 0.1 collective-permute-start.4
  10.5 1.9 %collective-permute-start.7 = (bf16[256,512]{1,0:T(8,128)(2,1)S(1)}, bf16[256,512]{1,0:T(8,128)(2,1)S(1)}, u32[]{:S(2)}, u32[]{:S(2)}) collective-permute-start(bf16[256,512]{1,0:T(8,128)(2,1)S(1)} %get-tuple-element.20.rest_4_), channel_id=1, source_target_pairs={{0,4},{2,6},{4,0},{6,2},{1,5},{3,7},{5,1},{7,3},{8,12},{10,14},{12... | collective-permute-start | bytes 786440 | tf_op jit(solution)/shard_map/ppermute | solution.py:490
  12.5 4.4 %collective-permute-done.4.rest_2_ = bf16[96,512]{1,0:T(8,128)(2,1)S(1)} collective-permute-done((bf16[96,512]{1,0:T(8,128)(2,1)S(1)}, bf16[96,512]{1,0:T(8,128)(2,1)S(1)}, u32[]{:S(2)}, u32[]{:S(2)}) %collective-permute-start.4) | collective-permute-done | bytes 98336 | tf_op jit(solution)/shard_map/ppermute | solution.py:490
  16.9 0.5 %collective-permute-start.11 = (bf16[128,512]{1,0:T(8,128)(2,1)S(1)}, bf16[128,512]{1,0:T(8,128)(2,1)S(1)}, u32[]{:S(2)}, u32[]{:S(2)}) collective-permute-start(bf16[128,512]{1,0:T(8,128)(2,1)S(1)} %collective-permute-done.10.rest_2_), channel_id=1, source_target_pairs={{0,2},{2,0},{4,6},{6,4},{1,3},{3,1},{5,7},{7,5},{8,10},{10,8},{12,... | collective-permute-start | bytes 393224 | tf_op jit(solution)/shard_map/ppermute | solution.py:490
  17.4 0.1 collective-permute-start.5
  17.5 1.2 %collective-permute-done.5.rest_3_ = bf16[96,512]{1,0:T(8,128)(2,1)S(1)} collective-permute-done((bf16[96,512]{1,0:T(8,128)(2,1)S(1)}, bf16[96,512]{1,0:T(8,128)(2,1)S(1)}, u32[]{:S(2)}, u32[]{:S(2)}) %collective-permute-start.5) | collective-permute-done | bytes 98336 | tf_op jit(solution)/shard_map/ppermute | solution.py:490
  18.8 1.5 %early.1 = (f32[4,128,512]{2,1,0:T(8,128)S(1)}, f32[4,128,512]{2,1,0:T(8,128)S(1)}, f32[5,8,512]{2,1,0:T(8,128)S(1)}, bf16[1280,128]{1,0:T(8,128)(2,1)S(1)}) custom-call(s32[8,128]{1,0:T(8,128)S(1)} %get-tuple-element.17.meta_ref, bf16[128,2048]{1,0:T(8,128)(2,1)S(1)} %bitcast.5, bf16[1280,512]{1,0:T(8,128)(2,1)S(1)} %copy-done.1, ...), custom_call_target="tpu_custom_call" | custom-call | tf_op jit(solution)/shard_map/early/pallas_call | solution.py:544
  20.3 0.3 product.1
  20.6 3.2 %collective-permute-start.12 = (bf16[80,512]{1,0:T(8,128)(2,1)S(1)}, bf16[80,512]{1,0:T(8,128)(2,1)S(1)}, u32[]{:S(2)}, u32[]{:S(2)}) collective-permute-start(bf16[80,512]{1,0:T(8,128)(2,1)S(1)} %get-tuple-element.29), channel_id=1, source_target_pairs={{0,16},{8,24},{16,0},{24,8},{1,17},{9,25},{17,1},{25,9},{2,18},{10... | collective-permute-start | bytes 245768 | tf_op jit(solution)/shard_map/ppermute | solution.py:490
  23.8 1.3 %collective-permute-start.13 = (bf16[80,512]{1,0:T(8,128)(2,1)S(1)}, bf16[80,512]{1,0:T(8,128)(2,1)S(1)}, u32[]{:S(2)}, u32[]{:S(2)}) collective-permute-start(bf16[80,512]{1,0:T(8,128)(2,1)S(1)} %get-tuple-element.30), channel_id=1, source_target_pairs={{0,24},{8,16},{16,8},{24,0},{1,25},{9,17},{17,9},{25,1},{2,26},{10... | collective-permute-start | bytes 245768 | tf_op jit(solution)/shard_map/ppermute | solution.py:490
  25.1 0.2 collective-permute-start.14
  25.3 0.7 %middle.1 = (f32[4,128,512]{2,1,0:T(8,128)S(1)}, f32[5,8,512]{2,1,0:T(8,128)S(1)}) custom-call(bf16[128,2048]{1,0:T(8,128)(2,1)S(1)} %bitcast.6, f32[4,128,512]{2,1,0:T(8,128)S(1)} %get-tuple-element.22.self_ref, f32[5,8,512]{2,1,0:T(8,128)S(1)} %get-tuple-element.23.stats_ref, bf16[256,512]{1,0:T(8,128)(2,1)S(1)} %collective-permute-done.7.pair_ref), custom_call_target="tpu_custom_call" | custom-call | tf_op jit(solution)/shard_map/middle/pallas_call | solution.py:580
  26.0 4.2 %collective-permute-done.12 = bf16[80,512]{1,0:T(8,128)(2,1)S(1)} collective-permute-done((bf16[80,512]{1,0:T(8,128)(2,1)S(1)}, bf16[80,512]{1,0:T(8,128)(2,1)S(1)}, u32[]{:S(2)}, u32[]{:S(2)}) %collective-permute-start.12) | collective-permute-done | bytes 81952 | tf_op jit(solution)/shard_map/ppermute | solution.py:490
  30.3 0.4 %collective-permute-done.13 = bf16[80,512]{1,0:T(8,128)(2,1)S(1)} collective-permute-done((bf16[80,512]{1,0:T(8,128)(2,1)S(1)}, bf16[80,512]{1,0:T(8,128)(2,1)S(1)}, u32[]{:S(2)}, u32[]{:S(2)}) %collective-permute-start.13) | collective-permute-done | bytes 81952 | tf_op jit(solution)/shard_map/ppermute | solution.py:490
  30.7 0.8 %collective-permute-done.14 = bf16[80,512]{1,0:T(8,128)(2,1)S(1)} collective-permute-done((bf16[80,512]{1,0:T(8,128)(2,1)S(1)}, bf16[80,512]{1,0:T(8,128)(2,1)S(1)}, u32[]{:S(2)}, u32[]{:S(2)}) %collective-permute-start.14) | collective-permute-done | bytes 81952 | tf_op jit(solution)/shard_map/ppermute | solution.py:490
  31.4 0.7 %convert_add_fusion = f32[80,512]{1,0:T(8,128)} fusion(bf16[80,512]{1,0:T(8,128)(2,1)S(1)} %collective-permute-done.14, bf16[80,512]{1,0:T(8,128)(2,1)S(1)} %collective-permute-done.13, f32[80,512]{1,0:T(8,128)S(1)} %get-tuple-element.28, bf16[80,512]{1,0:T(8,128)(2,1)S(1)} %collective-permute-done.12), kind=kLoop, calls=%fused_computation | loop fusion | flops 245760 | bytes 573440 | tf_op jit(solution)/shard_map/add | solution.py:577
  32.2 1.6 %late.1 = bf16[128,2048]{1,0:T(8,128)(2,1)} custom-call(bf16[128,2048]{1,0:T(8,128)(2,1)S(1)} %bitcast.7, f32[4,128,512]{2,1,0:T(8,128)S(1)} %get-tuple-element.21.cross_ref, f32[4,128,512]{2,1,0:T(8,128)S(1)} %get-tuple-element.24.self_ref, f32[5,8,512]{2,1,0:T(8,128)S(1)} %get-tuple-element.25.stats_ref, bf16[256,512]{1,0:T(8,128)(2,1)S(1)} %collective-permute-done.8.pair_ref), custom_call_target="tpu_custom_call" | custom-call | tf_op jit(solution)/shard_map/late/pallas_call | solution.py:588
  (23 shorter events, 0.1 us)
Async XLA Ops:
  0.6 7.0 %copy-start.2 = (bf16[1,128,2048]{2,1,0:T(8,128)(2,1)S(1)}, bf16[1,128,2048]{2,1,0:T(8,128)(2,1)}, u32[]{:S(2)}) copy-start(bf16[1,128,2048]{2,1,0:T(8,128)(2,1)} %param.15) | copy-start | bytes 1572868
  0.6 7.0 %copy-start.3 = (bf16[1,128,2048]{2,1,0:T(8,128)(2,1)S(1)}, bf16[1,128,2048]{2,1,0:T(8,128)(2,1)}, u32[]{:S(2)}) copy-start(bf16[1,128,2048]{2,1,0:T(8,128)(2,1)} %param.16) | copy-start | bytes 1572868
  0.7 7.0 %copy-start.4 = (bf16[1,32,512]{2,1,0:T(8,128)(2,1)S(1)}, bf16[1,32,512]{2,1,0:T(8,128)(2,1)}, u32[]{:S(2)}) copy-start(bf16[1,32,512]{2,1,0:T(8,128)(2,1)} %param.17) | copy-start | bytes 98308
  0.7 5.2 %collective-permute-start.1 = (bf16[32,512]{1,0:T(8,128)(2,1)}, bf16[32,512]{1,0:T(8,128)(2,1)S(1)}, u32[]{:S(2)}, u32[]{:S(2)}) collective-permute-start(bf16[32,512]{1,0:T(8,128)(2,1)} %bitcast.10), channel_id=1, source_target_pairs={{0,4},{2,6},{4,0},{6,2},{1,5},{3,7},{5,1},{7,3},{8,12},{10,14},{12... | collective-permute-start | bytes 98312 | tf_op jit(solution)/shard_map/ppermute | solution.py:490
  3.7 3.9 %collective-permute-start = (bf16[32,512]{1,0:T(8,128)(2,1)}, bf16[32,512]{1,0:T(8,128)(2,1)S(1)}, u32[]{:S(2)}, u32[]{:S(2)}) collective-permute-start(bf16[32,512]{1,0:T(8,128)(2,1)} %bitcast.11), channel_id=1, source_target_pairs={{0,2},{2,0},{4,6},{6,4},{1,3},{3,1},{5,7},{7,5},{8,10},{10,8},{12,... | collective-permute-start | bytes 98312 | tf_op jit(solution)/shard_map/ppermute | solution.py:490
  5.8 1.8 %collective-permute-start.2 = (bf16[32,512]{1,0:T(8,128)(2,1)S(1)}, bf16[32,512]{1,0:T(8,128)(2,1)S(1)}, u32[]{:S(2)}, u32[]{:S(2)}) collective-permute-start(bf16[32,512]{1,0:T(8,128)(2,1)S(1)} %collective-permute-done.1.rest_2_), channel_id=1, source_target_pairs={{0,2},{2,0},{4,6},{6,4},{1,3},{3,1},{5,7},{7,5},{8,10},{10,8},{12,... | collective-permute-start | bytes 98312 | tf_op jit(solution)/shard_map/ppermute | solution.py:490
  5.8 12.9 %copy-start.1 = (bf16[1280,512]{1,0:T(8,128)(2,1)S(1)}, bf16[1280,512]{1,0:T(8,128)(2,1)}, u32[]{:S(2)}) copy-start(bf16[1280,512]{1,0:T(8,128)(2,1)} %w_ref.1) | copy-start | bytes 3932164
  7.0 11.7 %copy-start = (bf16[1,128,2048]{2,1,0:T(8,128)(2,1)S(1)}, bf16[1,128,2048]{2,1,0:T(8,128)(2,1)}, u32[]{:S(2)}) copy-start(bf16[1,128,2048]{2,1,0:T(8,128)(2,1)} %param.11) | copy-start | bytes 1572868
  7.1 11.7 %collective-permute-start.6 = (bf16[256,512]{1,0:T(8,128)(2,1)S(1)}, bf16[256,512]{1,0:T(8,128)(2,1)S(1)}, u32[]{:S(2)}, u32[]{:S(2)}) collective-permute-start(bf16[256,512]{1,0:T(8,128)(2,1)S(1)} %get-tuple-element.20.rest_4_), channel_id=1, source_target_pairs={{0,2},{2,0},{4,6},{6,4},{1,3},{3,1},{5,7},{7,5},{8,10},{10,8},{12,... | collective-permute-start | bytes 786440 | tf_op jit(solution)/shard_map/ppermute | solution.py:490
  8.4 8.6 %collective-permute-start.10 = (bf16[128,512]{1,0:T(8,128)(2,1)S(1)}, bf16[128,512]{1,0:T(8,128)(2,1)S(1)}, u32[]{:S(2)}, u32[]{:S(2)}) collective-permute-start(bf16[128,512]{1,0:T(8,128)(2,1)S(1)} %get-tuple-element.27.rest_0_), channel_id=1, source_target_pairs={{0,4},{2,6},{4,0},{6,2},{1,5},{3,7},{5,1},{7,3},{8,12},{10,14},{12... | collective-permute-start | bytes 393224 | tf_op jit(solution)/shard_map/ppermute | solution.py:490
  10.5 6.5 %collective-permute-start.4 = (bf16[96,512]{1,0:T(8,128)(2,1)S(1)}, bf16[96,512]{1,0:T(8,128)(2,1)S(1)}, u32[]{:S(2)}, u32[]{:S(2)}) collective-permute-start(bf16[96,512]{1,0:T(8,128)(2,1)S(1)} %get-tuple-element.19.rest_0_), channel_id=1, source_target_pairs={{0,4},{2,6},{4,0},{6,2},{1,5},{3,7},{5,1},{7,3},{8,12},{10,14},{12... | collective-permute-start | bytes 294920 | tf_op jit(solution)/shard_map/ppermute | solution.py:490
  10.5 14.8 %collective-permute-start.7 = (bf16[256,512]{1,0:T(8,128)(2,1)S(1)}, bf16[256,512]{1,0:T(8,128)(2,1)S(1)}, u32[]{:S(2)}, u32[]{:S(2)}) collective-permute-start(bf16[256,512]{1,0:T(8,128)(2,1)S(1)} %get-tuple-element.20.rest_4_), channel_id=1, source_target_pairs={{0,4},{2,6},{4,0},{6,2},{1,5},{3,7},{5,1},{7,3},{8,12},{10,14},{12... | collective-permute-start | bytes 786440 | tf_op jit(solution)/shard_map/ppermute | solution.py:490
  12.5 4.9 %collective-permute-start.3 = (bf16[96,512]{1,0:T(8,128)(2,1)S(1)}, bf16[96,512]{1,0:T(8,128)(2,1)S(1)}, u32[]{:S(2)}, u32[]{:S(2)}) collective-permute-start(bf16[96,512]{1,0:T(8,128)(2,1)S(1)} %get-tuple-element.19.rest_0_), channel_id=1, source_target_pairs={{0,2},{2,0},{4,6},{6,4},{1,3},{3,1},{5,7},{7,5},{8,10},{10,8},{12,... | collective-permute-start | bytes 294920 | tf_op jit(solution)/shard_map/ppermute | solution.py:490
  16.9 3.3 %collective-permute-start.9 = (bf16[128,512]{1,0:T(8,128)(2,1)S(1)}, bf16[128,512]{1,0:T(8,128)(2,1)S(1)}, u32[]{:S(2)}, u32[]{:S(2)}) collective-permute-start(bf16[128,512]{1,0:T(8,128)(2,1)S(1)} %get-tuple-element.27.rest_0_), channel_id=1, source_target_pairs={{0,2},{2,0},{4,6},{6,4},{1,3},{3,1},{5,7},{7,5},{8,10},{10,8},{12,... | collective-permute-start | bytes 393224 | tf_op jit(solution)/shard_map/ppermute | solution.py:490
  16.9 3.3 %collective-permute-start.11 = (bf16[128,512]{1,0:T(8,128)(2,1)S(1)}, bf16[128,512]{1,0:T(8,128)(2,1)S(1)}, u32[]{:S(2)}, u32[]{:S(2)}) collective-permute-start(bf16[128,512]{1,0:T(8,128)(2,1)S(1)} %collective-permute-done.10.rest_2_), channel_id=1, source_target_pairs={{0,2},{2,0},{4,6},{6,4},{1,3},{3,1},{5,7},{7,5},{8,10},{10,8},{12,... | collective-permute-start | bytes 393224 | tf_op jit(solution)/shard_map/ppermute | solution.py:490
  17.4 1.3 %collective-permute-start.5 = (bf16[96,512]{1,0:T(8,128)(2,1)S(1)}, bf16[96,512]{1,0:T(8,128)(2,1)S(1)}, u32[]{:S(2)}, u32[]{:S(2)}) collective-permute-start(bf16[96,512]{1,0:T(8,128)(2,1)S(1)} %collective-permute-done.4.rest_2_), channel_id=1, source_target_pairs={{0,2},{2,0},{4,6},{6,4},{1,3},{3,1},{5,7},{7,5},{8,10},{10,8},{12,... | collective-permute-start | bytes 294920 | tf_op jit(solution)/shard_map/ppermute | solution.py:490
  20.6 9.7 %collective-permute-start.12 = (bf16[80,512]{1,0:T(8,128)(2,1)S(1)}, bf16[80,512]{1,0:T(8,128)(2,1)S(1)}, u32[]{:S(2)}, u32[]{:S(2)}) collective-permute-start(bf16[80,512]{1,0:T(8,128)(2,1)S(1)} %get-tuple-element.29), channel_id=1, source_target_pairs={{0,16},{8,24},{16,0},{24,8},{1,17},{9,25},{17,1},{25,9},{2,18},{10... | collective-permute-start | bytes 245768 | tf_op jit(solution)/shard_map/ppermute | solution.py:490
  23.8 6.9 %collective-permute-start.13 = (bf16[80,512]{1,0:T(8,128)(2,1)S(1)}, bf16[80,512]{1,0:T(8,128)(2,1)S(1)}, u32[]{:S(2)}, u32[]{:S(2)}) collective-permute-start(bf16[80,512]{1,0:T(8,128)(2,1)S(1)} %get-tuple-element.30), channel_id=1, source_target_pairs={{0,24},{8,16},{16,8},{24,0},{1,25},{9,17},{17,9},{25,1},{2,26},{10... | collective-permute-start | bytes 245768 | tf_op jit(solution)/shard_map/ppermute | solution.py:490
  25.1 6.4 %collective-permute-start.14 = (bf16[80,512]{1,0:T(8,128)(2,1)S(1)}, bf16[80,512]{1,0:T(8,128)(2,1)S(1)}, u32[]{:S(2)}, u32[]{:S(2)}) collective-permute-start(bf16[80,512]{1,0:T(8,128)(2,1)S(1)} %get-tuple-element.31), channel_id=1, source_target_pairs={{0,8},{8,0},{16,24},{24,16},{1,9},{9,1},{17,25},{25,17},{2,10},{10... | collective-permute-start | bytes 245768 | tf_op jit(solution)/shard_map/ppermute | solution.py:490
  25.3 6.8 %collective-permute-start.8 = (bf16[256,512]{1,0:T(8,128)(2,1)S(1)}, bf16[256,512]{1,0:T(8,128)(2,1)S(1)}, u32[]{:S(2)}, u32[]{:S(2)}) collective-permute-start(bf16[256,512]{1,0:T(8,128)(2,1)S(1)} %collective-permute-done.7.pair_ref), channel_id=1, source_target_pairs={{0,2},{2,0},{4,6},{6,4},{1,3},{3,1},{5,7},{7,5},{8,10},{10,8},{12,... | collective-permute-start | bytes 786440 | tf_op jit(solution)/shard_map/ppermute | solution.py:490

commit v6 on v5

--- a/solution.py
+++ b/solution.py
@@ -253,12 +253,13 @@
     share = kv_local // len(grad_refs)
     seq_at = lax.axis_index("seq")
     tok_rows = q_ref.shape[0]
-    bias = []
-    for x in range(blocks):
-        slot_ids = (seq_at ^ x) * slots + lax.broadcasted_iota(jnp.int32, (slots, tok_rows), 0)
-        kept = (slot_ids >= meta_ref[1:2, :]) & (slot_ids < meta_ref[2:3, :])
-        bias.append(jnp.where(kept, 0.0, MASK_FILL))
-    bias = jnp.concatenate(bias, axis=0)
+    first, count = meta_ref[1:2, :], meta_ref[2:3, :] - meta_ref[1:2, :]
+    chosen = [
+        jnp.concatenate([first == (seq_at ^ x) * slots] * group_size, axis=1)
+        for x in range(blocks)
+    ]
+    slot_ids = lax.broadcasted_iota(jnp.int32, (slots, tok_rows), 0)
+    bias = jnp.where(slot_ids < count, 0.0, MASK_FILL)
     bias = jnp.concatenate([bias] * group_size, axis=1)
     scale = HD ** (-0.5) * LOG2E
     spans = [slice(group * HD, (group + 1) * HD) for group in range(kv_local)]
@@ -269,11 +270,17 @@
         )
         for group, columns in enumerate(spans)
     ]
+    flags = [jnp.where(pick, 1.0, 0.0).astype(jnp.bfloat16) for pick in chosen]
     for group in range(kv_local):
-        scaled = scores[group] * scale + bias
+        picked = scores[group][(blocks - 1) * slots :]
+        for x in range(blocks - 1):
+            picked = jnp.where(chosen[x], scores[group][x * slots : (x + 1) * slots], picked)
+        scaled = picked * scale + bias
         exps = jnp.exp2(scaled - jnp.max(scaled, axis=0, keepdims=True))
         inverse = 1.0 / jnp.sum(exps, axis=0, keepdims=True)
-        weights_ref[group] = (exps * inverse).astype(jnp.bfloat16)
+        weights = (exps * inverse).astype(jnp.bfloat16)
+        for x in range(blocks):
+            weights_ref[group, x * slots : (x + 1) * slots] = weights * flags[x]
     for group, columns in enumerate(spans):
         grads = dot_nn(weights_ref[group], stacked_heads(cot_ref, group, group_size)).astype(
             jnp.bfloat16
@@ -602,7 +609,7 @@
 
 def fits_small(mesh, shapes):
     seq_size, dp_size = mesh.shape["seq"], mesh.shape["dp"]
-    q_self, k_self, img_keys, features, _, cite = shapes
+    q_self, k_self, img_keys, features, tiles, cite = shapes
     tensor = mesh.shape["tensor"]
     powers = all(n & (n - 1) == 0 for n in (seq_size, dp_size))
     tok_rows, width = q_self[1] // seq_size, k_self[2] // tensor
@@ -616,6 +623,7 @@
         and tok_rows <= width
         and slots % 32 == 0
         and slots * seq_size == HD
+        and tiles[1] == seq_size
         and left == 0
         and rows % 16 == 0
         and features[2] % HD == 0
@@ -642,7 +650,7 @@
     out_specs = (P("dp", "seq", "tensor"), P(("dp", "seq"), "tensor"))
 
     def run(*arrays):
-        shapes = [arrays[i].shape for i in (0, 1, 6, 7, 8, 10)]
+        shapes = [arrays[i].shape for i in (0, 1, 6, 7, 9, 10)]
         body = on_device_general
         if fits_small(mesh, shapes):
             body = functools.partial(on_device_small, mesh.shape["seq"], mesh.shape["dp"])

time: 33.9 us -> 33.7 us (level)
  no operation moved by 1% of the time
where the time goes in v6:
time: 33.7 us; the launch traced here: 33.6 us
  waiting for transfers between devices  13.2 us (39%)
  starting transfers between devices  13.1 us (39%)
  Pallas kernels  5.8 us (17%)
  between operations  0.76 us (2%)
  other arithmetic  0.71 us (2%)
    ppermute x15, waiting for transfers between devices, swapped(): return lax.ppermute(array, axis, [(i, i ^ x) for i in range(size)])  13.2 us
    ppermute x15, starting transfers between devices, swapped(): return lax.ppermute(array, axis, [(i, i ^ x) for i in range(size)])  13.1 us
    pallas_call x1, Pallas kernels, on_device_small(): pl.pallas_call(functools.partial(late_kernel, (kv_local, group_size, chip...  1.55 us
    pallas_call x1, Pallas kernels, on_device_small(): pl.pallas_call(functools.partial(early_kernel, (kv_local, group_size, slo...  1.5 us
    pallas_call x1, Pallas kernels, on_device_small(): pl.pallas_call(functools.partial(pack_kernel, (slots, parts, key_count //...  1.21 us
    add x1, other arithmetic, on_device_small(): total = total + arrived.astype(jnp.float32)  0.71 us
  transfers between devices with their start and end apart: 15, of which 6 were waited for; matrix products, arithmetic and copies ran while one was open for 2% of the time, Pallas kernels for 13%

profile of v6, /device:TPU:0, one launch (start us, length us, event | category | flops | bytes accessed | tf_op | source)
XLA Modules:
  0.0 33.6 jit_solution(11379461836467008540)
XLA Ops:
  0.7 3.1 %collective-permute-start.1 = (bf16[32,512]{1,0:T(8,128)(2,1)}, bf16[32,512]{1,0:T(8,128)(2,1)S(1)}, u32[]{:S(2)}, u32[]{:S(2)}) collective-permute-start(bf16[32,512]{1,0:T(8,128)(2,1)} %bitcast.10), channel_id=1, source_target_pairs={{0,4},{2,6},{4,0},{6,2},{1,5},{3,7},{5,1},{7,3},{8,12},{10,14},{12... | collective-permute-start | bytes 98312 | tf_op jit(solution)/shard_map/ppermute | solution.py:497
  3.7 2.1 %collective-permute-done.1.rest_2_ = bf16[32,512]{1,0:T(8,128)(2,1)S(1)} collective-permute-done((bf16[32,512]{1,0:T(8,128)(2,1)}, bf16[32,512]{1,0:T(8,128)(2,1)S(1)}, u32[]{:S(2)}, u32[]{:S(2)}) %collective-permute-start.1) | collective-permute-done | bytes 32800 | tf_op jit(solution)/shard_map/ppermute | solution.py:497
  5.8 1.2 %pack.1 = (bf16[96,512]{1,0:T(8,128)(2,1)S(1)}, bf16[256,512]{1,0:T(8,128)(2,1)S(1)}, s32[8,128]{1,0:T(8,128)S(1)}) custom-call(s32[1,128]{1,0:T(1,128)} %docs_hbm.1, s32[1,4]{1,0:T(1,128)} %tiles_hbm.1, s32[1,4]{1,0:T(1,128)} %cite_hbm.1, bf16[1,32,1280]{2,1,0:T(8,128)(2,1)} %features_hbm.1, bf16[1,128,512]{2,1,0:T(8,128)(2,1)} %k_hbm.1, ...), custom_call_target="tpu_custom_call" | custom-call | flops 4294967296 | bytes 16777216 | tf_op jit(solution)/shard_map/pack/pallas_call | solution.py:507
  7.0 0.0 copy-start
  7.1 0.6 %collective-permute-start.6 = (bf16[256,512]{1,0:T(8,128)(2,1)S(1)}, bf16[256,512]{1,0:T(8,128)(2,1)S(1)}, u32[]{:S(2)}, u32[]{:S(2)}) collective-permute-start(bf16[256,512]{1,0:T(8,128)(2,1)S(1)} %get-tuple-element.20.rest_4_), channel_id=1, source_target_pairs={{0,2},{2,0},{4,6},{6,4},{1,3},{3,1},{5,7},{7,5},{8,10},{10,8},{12,... | collective-permute-start | bytes 786440 | tf_op jit(solution)/shard_map/ppermute | solution.py:497
  7.7 0.6 %cross.1 = (bf16[4,128,512]{2,1,0:T(8,128)(2,1)S(1)}, bf16[128,512]{1,0:T(8,128)(2,1)S(1)}) custom-call(s32[8,128]{1,0:T(8,128)S(1)} %get-tuple-element.17.meta_ref, bf16[128,2048]{1,0:T(8,128)(2,1)S(1)} %bitcast.8, bf16[128,2048]{1,0:T(8,128)(2,1)S(1)} %bitcast.9, bf16[32,512]{1,0:T(8,128)(2,1)S(1)} %bitcast.12, ...), custom_call_target="tpu_custom_call" | custom-call | tf_op jit(solution)/shard_map/cross/pallas_call | solution.py:535
  8.2 2.1 %collective-permute-start.10 = (bf16[128,512]{1,0:T(8,128)(2,1)S(1)}, bf16[128,512]{1,0:T(8,128)(2,1)S(1)}, u32[]{:S(2)}, u32[]{:S(2)}) collective-permute-start(bf16[128,512]{1,0:T(8,128)(2,1)S(1)} %get-tuple-element.27.rest_0_), channel_id=1, source_target_pairs={{0,4},{2,6},{4,0},{6,2},{1,5},{3,7},{5,1},{7,3},{8,12},{10,14},{12... | collective-permute-start | bytes 393224 | tf_op jit(solution)/shard_map/ppermute | solution.py:497
  10.3 0.1 collective-permute-start.4
  10.4 1.9 %collective-permute-start.7 = (bf16[256,512]{1,0:T(8,128)(2,1)S(1)}, bf16[256,512]{1,0:T(8,128)(2,1)S(1)}, u32[]{:S(2)}, u32[]{:S(2)}) collective-permute-start(bf16[256,512]{1,0:T(8,128)(2,1)S(1)} %get-tuple-element.20.rest_4_), channel_id=1, source_target_pairs={{0,4},{2,6},{4,0},{6,2},{1,5},{3,7},{5,1},{7,3},{8,12},{10,14},{12... | collective-permute-start | bytes 786440 | tf_op jit(solution)/shard_map/ppermute | solution.py:497
  12.4 4.4 %collective-permute-done.4.rest_2_ = bf16[96,512]{1,0:T(8,128)(2,1)S(1)} collective-permute-done((bf16[96,512]{1,0:T(8,128)(2,1)S(1)}, bf16[96,512]{1,0:T(8,128)(2,1)S(1)}, u32[]{:S(2)}, u32[]{:S(2)}) %collective-permute-start.4) | collective-permute-done | bytes 98336 | tf_op jit(solution)/shard_map/ppermute | solution.py:497
  16.8 0.5 %collective-permute-start.11 = (bf16[128,512]{1,0:T(8,128)(2,1)S(1)}, bf16[128,512]{1,0:T(8,128)(2,1)S(1)}, u32[]{:S(2)}, u32[]{:S(2)}) collective-permute-start(bf16[128,512]{1,0:T(8,128)(2,1)S(1)} %collective-permute-done.10.rest_2_), channel_id=1, source_target_pairs={{0,2},{2,0},{4,6},{6,4},{1,3},{3,1},{5,7},{7,5},{8,10},{10,8},{12,... | collective-permute-start | bytes 393224 | tf_op jit(solution)/shard_map/ppermute | solution.py:497
  17.3 0.1 collective-permute-start.5
  17.4 1.2 %collective-permute-done.5.rest_3_ = bf16[96,512]{1,0:T(8,128)(2,1)S(1)} collective-permute-done((bf16[96,512]{1,0:T(8,128)(2,1)S(1)}, bf16[96,512]{1,0:T(8,128)(2,1)S(1)}, u32[]{:S(2)}, u32[]{:S(2)}) %collective-permute-start.5) | collective-permute-done | bytes 98336 | tf_op jit(solution)/shard_map/ppermute | solution.py:497
  18.6 1.5 %early.1 = (f32[4,128,512]{2,1,0:T(8,128)S(1)}, f32[4,128,512]{2,1,0:T(8,128)S(1)}, f32[5,8,512]{2,1,0:T(8,128)S(1)}, bf16[1280,128]{1,0:T(8,128)(2,1)S(1)}) custom-call(s32[8,128]{1,0:T(8,128)S(1)} %get-tuple-element.17.meta_ref, bf16[128,2048]{1,0:T(8,128)(2,1)S(1)} %bitcast.5, bf16[1280,512]{1,0:T(8,128)(2,1)S(1)} %copy-done.1, ...), custom_call_target="tpu_custom_call" | custom-call | tf_op jit(solution)/shard_map/early/pallas_call | solution.py:551
  20.1 0.3 product.1
  20.5 3.2 %collective-permute-start.12 = (bf16[80,512]{1,0:T(8,128)(2,1)S(1)}, bf16[80,512]{1,0:T(8,128)(2,1)S(1)}, u32[]{:S(2)}, u32[]{:S(2)}) collective-permute-start(bf16[80,512]{1,0:T(8,128)(2,1)S(1)} %get-tuple-element.29), channel_id=1, source_target_pairs={{0,16},{8,24},{16,0},{24,8},{1,17},{9,25},{17,1},{25,9},{2,18},{10... | collective-permute-start | bytes 245768 | tf_op jit(solution)/shard_map/ppermute | solution.py:497
  23.6 1.3 %collective-permute-start.13 = (bf16[80,512]{1,0:T(8,128)(2,1)S(1)}, bf16[80,512]{1,0:T(8,128)(2,1)S(1)}, u32[]{:S(2)}, u32[]{:S(2)}) collective-permute-start(bf16[80,512]{1,0:T(8,128)(2,1)S(1)} %get-tuple-element.30), channel_id=1, source_target_pairs={{0,24},{8,16},{16,8},{24,0},{1,25},{9,17},{17,9},{25,1},{2,26},{10... | collective-permute-start | bytes 245768 | tf_op jit(solution)/shard_map/ppermute | solution.py:497
  25.0 0.2 collective-permute-start.14
  25.2 0.7 %middle.1 = (f32[4,128,512]{2,1,0:T(8,128)S(1)}, f32[5,8,512]{2,1,0:T(8,128)S(1)}) custom-call(bf16[128,2048]{1,0:T(8,128)(2,1)S(1)} %bitcast.6, f32[4,128,512]{2,1,0:T(8,128)S(1)} %get-tuple-element.22.self_ref, f32[5,8,512]{2,1,0:T(8,128)S(1)} %get-tuple-element.23.stats_ref, bf16[256,512]{1,0:T(8,128)(2,1)S(1)} %collective-permute-done.7.pair_ref), custom_call_target="tpu_custom_call" | custom-call | tf_op jit(solution)/shard_map/middle/pallas_call | solution.py:587
  25.9 4.2 %collective-permute-done.12 = bf16[80,512]{1,0:T(8,128)(2,1)S(1)} collective-permute-done((bf16[80,512]{1,0:T(8,128)(2,1)S(1)}, bf16[80,512]{1,0:T(8,128)(2,1)S(1)}, u32[]{:S(2)}, u32[]{:S(2)}) %collective-permute-start.12) | collective-permute-done | bytes 81952 | tf_op jit(solution)/shard_map/ppermute | solution.py:497
  30.1 0.4 %collective-permute-done.13 = bf16[80,512]{1,0:T(8,128)(2,1)S(1)} collective-permute-done((bf16[80,512]{1,0:T(8,128)(2,1)S(1)}, bf16[80,512]{1,0:T(8,128)(2,1)S(1)}, u32[]{:S(2)}, u32[]{:S(2)}) %collective-permute-start.13) | collective-permute-done | bytes 81952 | tf_op jit(solution)/shard_map/ppermute | solution.py:497
  30.5 0.8 %collective-permute-done.14 = bf16[80,512]{1,0:T(8,128)(2,1)S(1)} collective-permute-done((bf16[80,512]{1,0:T(8,128)(2,1)S(1)}, bf16[80,512]{1,0:T(8,128)(2,1)S(1)}, u32[]{:S(2)}, u32[]{:S(2)}) %collective-permute-start.14) | collective-permute-done | bytes 81952 | tf_op jit(solution)/shard_map/ppermute | solution.py:497
  31.3 0.7 %convert_add_fusion = f32[80,512]{1,0:T(8,128)} fusion(bf16[80,512]{1,0:T(8,128)(2,1)S(1)} %collective-permute-done.14, bf16[80,512]{1,0:T(8,128)(2,1)S(1)} %collective-permute-done.13, f32[80,512]{1,0:T(8,128)S(1)} %get-tuple-element.28, bf16[80,512]{1,0:T(8,128)(2,1)S(1)} %collective-permute-done.12), kind=kLoop, calls=%fused_computation | loop fusion | flops 245760 | bytes 573440 | tf_op jit(solution)/shard_map/add | solution.py:584
  32.0 1.6 %late.1 = bf16[128,2048]{1,0:T(8,128)(2,1)} custom-call(bf16[128,2048]{1,0:T(8,128)(2,1)S(1)} %bitcast.7, f32[4,128,512]{2,1,0:T(8,128)S(1)} %get-tuple-element.21.cross_ref, f32[4,128,512]{2,1,0:T(8,128)S(1)} %get-tuple-element.24.self_ref, f32[5,8,512]{2,1,0:T(8,128)S(1)} %get-tuple-element.25.stats_ref, bf16[256,512]{1,0:T(8,128)(2,1)S(1)} %collective-permute-done.8.pair_ref), custom_call_target="tpu_custom_call" | custom-call | tf_op jit(solution)/shard_map/late/pallas_call | solution.py:595
  (23 shorter events, 0.1 us)
Async XLA Ops:
  0.6 7.0 %copy-start.2 = (bf16[1,128,2048]{2,1,0:T(8,128)(2,1)S(1)}, bf16[1,128,2048]{2,1,0:T(8,128)(2,1)}, u32[]{:S(2)}) copy-start(bf16[1,128,2048]{2,1,0:T(8,128)(2,1)} %param.15) | copy-start | bytes 1572868
  0.6 7.0 %copy-start.3 = (bf16[1,128,2048]{2,1,0:T(8,128)(2,1)S(1)}, bf16[1,128,2048]{2,1,0:T(8,128)(2,1)}, u32[]{:S(2)}) copy-start(bf16[1,128,2048]{2,1,0:T(8,128)(2,1)} %param.16) | copy-start | bytes 1572868
  0.7 7.0 %copy-start.4 = (bf16[1,32,512]{2,1,0:T(8,128)(2,1)S(1)}, bf16[1,32,512]{2,1,0:T(8,128)(2,1)}, u32[]{:S(2)}) copy-start(bf16[1,32,512]{2,1,0:T(8,128)(2,1)} %param.17) | copy-start | bytes 98308
  0.7 5.2 %collective-permute-start.1 = (bf16[32,512]{1,0:T(8,128)(2,1)}, bf16[32,512]{1,0:T(8,128)(2,1)S(1)}, u32[]{:S(2)}, u32[]{:S(2)}) collective-permute-start(bf16[32,512]{1,0:T(8,128)(2,1)} %bitcast.10), channel_id=1, source_target_pairs={{0,4},{2,6},{4,0},{6,2},{1,5},{3,7},{5,1},{7,3},{8,12},{10,14},{12... | collective-permute-start | bytes 98312 | tf_op jit(solution)/shard_map/ppermute | solution.py:497
  3.7 3.9 %collective-permute-start = (bf16[32,512]{1,0:T(8,128)(2,1)}, bf16[32,512]{1,0:T(8,128)(2,1)S(1)}, u32[]{:S(2)}, u32[]{:S(2)}) collective-permute-start(bf16[32,512]{1,0:T(8,128)(2,1)} %bitcast.11), channel_id=1, source_target_pairs={{0,2},{2,0},{4,6},{6,4},{1,3},{3,1},{5,7},{7,5},{8,10},{10,8},{12,... | collective-permute-start | bytes 98312 | tf_op jit(solution)/shard_map/ppermute | solution.py:497
  5.8 1.8 %collective-permute-start.2 = (bf16[32,512]{1,0:T(8,128)(2,1)S(1)}, bf16[32,512]{1,0:T(8,128)(2,1)S(1)}, u32[]{:S(2)}, u32[]{:S(2)}) collective-permute-start(bf16[32,512]{1,0:T(8,128)(2,1)S(1)} %collective-permute-done.1.rest_2_), channel_id=1, source_target_pairs={{0,2},{2,0},{4,6},{6,4},{1,3},{3,1},{5,7},{7,5},{8,10},{10,8},{12,... | collective-permute-start | bytes 98312 | tf_op jit(solution)/shard_map/ppermute | solution.py:497
  5.8 12.8 %copy-start.1 = (bf16[1280,512]{1,0:T(8,128)(2,1)S(1)}, bf16[1280,512]{1,0:T(8,128)(2,1)}, u32[]{:S(2)}) copy-start(bf16[1280,512]{1,0:T(8,128)(2,1)} %w_ref.1) | copy-start | bytes 3932164
  7.0 11.6 %copy-start = (bf16[1,128,2048]{2,1,0:T(8,128)(2,1)S(1)}, bf16[1,128,2048]{2,1,0:T(8,128)(2,1)}, u32[]{:S(2)}) copy-start(bf16[1,128,2048]{2,1,0:T(8,128)(2,1)} %param.11) | copy-start | bytes 1572868
  7.1 11.5 %collective-permute-start.6 = (bf16[256,512]{1,0:T(8,128)(2,1)S(1)}, bf16[256,512]{1,0:T(8,128)(2,1)S(1)}, u32[]{:S(2)}, u32[]{:S(2)}) collective-permute-start(bf16[256,512]{1,0:T(8,128)(2,1)S(1)} %get-tuple-element.20.rest_4_), channel_id=1, source_target_pairs={{0,2},{2,0},{4,6},{6,4},{1,3},{3,1},{5,7},{7,5},{8,10},{10,8},{12,... | collective-permute-start | bytes 786440 | tf_op jit(solution)/shard_map/ppermute | solution.py:497
  8.2 8.6 %collective-permute-start.10 = (bf16[128,512]{1,0:T(8,128)(2,1)S(1)}, bf16[128,512]{1,0:T(8,128)(2,1)S(1)}, u32[]{:S(2)}, u32[]{:S(2)}) collective-permute-start(bf16[128,512]{1,0:T(8,128)(2,1)S(1)} %get-tuple-element.27.rest_0_), channel_id=1, source_target_pairs={{0,4},{2,6},{4,0},{6,2},{1,5},{3,7},{5,1},{7,3},{8,12},{10,14},{12... | collective-permute-start | bytes 393224 | tf_op jit(solution)/shard_map/ppermute | solution.py:497
  10.3 6.5 %collective-permute-start.4 = (bf16[96,512]{1,0:T(8,128)(2,1)S(1)}, bf16[96,512]{1,0:T(8,128)(2,1)S(1)}, u32[]{:S(2)}, u32[]{:S(2)}) collective-permute-start(bf16[96,512]{1,0:T(8,128)(2,1)S(1)} %get-tuple-element.19.rest_0_), channel_id=1, source_target_pairs={{0,4},{2,6},{4,0},{6,2},{1,5},{3,7},{5,1},{7,3},{8,12},{10,14},{12... | collective-permute-start | bytes 294920 | tf_op jit(solution)/shard_map/ppermute | solution.py:497
  10.4 14.8 %collective-permute-start.7 = (bf16[256,512]{1,0:T(8,128)(2,1)S(1)}, bf16[256,512]{1,0:T(8,128)(2,1)S(1)}, u32[]{:S(2)}, u32[]{:S(2)}) collective-permute-start(bf16[256,512]{1,0:T(8,128)(2,1)S(1)} %get-tuple-element.20.rest_4_), channel_id=1, source_target_pairs={{0,4},{2,6},{4,0},{6,2},{1,5},{3,7},{5,1},{7,3},{8,12},{10,14},{12... | collective-permute-start | bytes 786440 | tf_op jit(solution)/shard_map/ppermute | solution.py:497
  12.4 4.9 %collective-permute-start.3 = (bf16[96,512]{1,0:T(8,128)(2,1)S(1)}, bf16[96,512]{1,0:T(8,128)(2,1)S(1)}, u32[]{:S(2)}, u32[]{:S(2)}) collective-permute-start(bf16[96,512]{1,0:T(8,128)(2,1)S(1)} %get-tuple-element.19.rest_0_), channel_id=1, source_target_pairs={{0,2},{2,0},{4,6},{6,4},{1,3},{3,1},{5,7},{7,5},{8,10},{10,8},{12,... | collective-permute-start | bytes 294920 | tf_op jit(solution)/shard_map/ppermute | solution.py:497
  16.8 3.3 %collective-permute-start.9 = (bf16[128,512]{1,0:T(8,128)(2,1)S(1)}, bf16[128,512]{1,0:T(8,128)(2,1)S(1)}, u32[]{:S(2)}, u32[]{:S(2)}) collective-permute-start(bf16[128,512]{1,0:T(8,128)(2,1)S(1)} %get-tuple-element.27.rest_0_), channel_id=1, source_target_pairs={{0,2},{2,0},{4,6},{6,4},{1,3},{3,1},{5,7},{7,5},{8,10},{10,8},{12,... | collective-permute-start | bytes 393224 | tf_op jit(solution)/shard_map/ppermute | solution.py:497
  16.8 3.3 %collective-permute-start.11 = (bf16[128,512]{1,0:T(8,128)(2,1)S(1)}, bf16[128,512]{1,0:T(8,128)(2,1)S(1)}, u32[]{:S(2)}, u32[]{:S(2)}) collective-permute-start(bf16[128,512]{1,0:T(8,128)(2,1)S(1)} %collective-permute-done.10.rest_2_), channel_id=1, source_target_pairs={{0,2},{2,0},{4,6},{6,4},{1,3},{3,1},{5,7},{7,5},{8,10},{10,8},{12,... | collective-permute-start | bytes 393224 | tf_op jit(solution)/shard_map/ppermute | solution.py:497
  17.3 1.3 %collective-permute-start.5 = (bf16[96,512]{1,0:T(8,128)(2,1)S(1)}, bf16[96,512]{1,0:T(8,128)(2,1)S(1)}, u32[]{:S(2)}, u32[]{:S(2)}) collective-permute-start(bf16[96,512]{1,0:T(8,128)(2,1)S(1)} %collective-permute-done.4.rest_2_), channel_id=1, source_target_pairs={{0,2},{2,0},{4,6},{6,4},{1,3},{3,1},{5,7},{7,5},{8,10},{10,8},{12,... | collective-permute-start | bytes 294920 | tf_op jit(solution)/shard_map/ppermute | solution.py:497
  20.5 9.7 %collective-permute-start.12 = (bf16[80,512]{1,0:T(8,128)(2,1)S(1)}, bf16[80,512]{1,0:T(8,128)(2,1)S(1)}, u32[]{:S(2)}, u32[]{:S(2)}) collective-permute-start(bf16[80,512]{1,0:T(8,128)(2,1)S(1)} %get-tuple-element.29), channel_id=1, source_target_pairs={{0,16},{8,24},{16,0},{24,8},{1,17},{9,25},{17,1},{25,9},{2,18},{10... | collective-permute-start | bytes 245768 | tf_op jit(solution)/shard_map/ppermute | solution.py:497
  23.6 6.9 %collective-permute-start.13 = (bf16[80,512]{1,0:T(8,128)(2,1)S(1)}, bf16[80,512]{1,0:T(8,128)(2,1)S(1)}, u32[]{:S(2)}, u32[]{:S(2)}) collective-permute-start(bf16[80,512]{1,0:T(8,128)(2,1)S(1)} %get-tuple-element.30), channel_id=1, source_target_pairs={{0,24},{8,16},{16,8},{24,0},{1,25},{9,17},{17,9},{25,1},{2,26},{10... | collective-permute-start | bytes 245768 | tf_op jit(solution)/shard_map/ppermute | solution.py:497
  25.0 6.3 %collective-permute-start.14 = (bf16[80,512]{1,0:T(8,128)(2,1)S(1)}, bf16[80,512]{1,0:T(8,128)(2,1)S(1)}, u32[]{:S(2)}, u32[]{:S(2)}) collective-permute-start(bf16[80,512]{1,0:T(8,128)(2,1)S(1)} %get-tuple-element.31), channel_id=1, source_target_pairs={{0,8},{8,0},{16,24},{24,16},{1,9},{9,1},{17,25},{25,17},{2,10},{10... | collective-permute-start | bytes 245768 | tf_op jit(solution)/shard_map/ppermute | solution.py:497
  25.2 6.8 %collective-permute-start.8 = (bf16[256,512]{1,0:T(8,128)(2,1)S(1)}, bf16[256,512]{1,0:T(8,128)(2,1)S(1)}, u32[]{:S(2)}, u32[]{:S(2)}) collective-permute-start(bf16[256,512]{1,0:T(8,128)(2,1)S(1)} %collective-permute-done.7.pair_ref), channel_id=1, source_target_pairs={{0,2},{2,0},{4,6},{6,4},{1,3},{3,1},{5,7},{7,5},{8,10},{10,8},{12,... | collective-permute-start | bytes 786440 | tf_op jit(solution)/shard_map/ppermute | solution.py:497

commit v7 on v6

--- a/solution.py
+++ b/solution.py
@@ -247,34 +247,51 @@
     rows_ref[feature_rows - slots : feature_rows, last:] = tail
 
 
-def cross_kernel(sizes, meta_ref, q_ref, cot_ref, *rest):
-    kv_local, group_size, slots, blocks = sizes
-    key_refs, weights_ref, grad_refs = rest[:blocks], rest[blocks], rest[blocks + 1 :]
-    share = kv_local // len(grad_refs)
-    seq_at = lax.axis_index("seq")
-    tok_rows = q_ref.shape[0]
-    first, count = meta_ref[1:2, :], meta_ref[2:3, :] - meta_ref[1:2, :]
-    chosen = [
-        jnp.concatenate([first == (seq_at ^ x) * slots] * group_size, axis=1)
-        for x in range(blocks)
-    ]
-    slot_ids = lax.broadcasted_iota(jnp.int32, (slots, tok_rows), 0)
-    bias = jnp.where(slot_ids < count, 0.0, MASK_FILL)
-    bias = jnp.concatenate([bias] * group_size, axis=1)
-    scale = HD ** (-0.5) * LOG2E
-    spans = [slice(group * HD, (group + 1) * HD) for group in range(kv_local)]
-    scores = [
+def chosen_columns(meta_ref, seq_at, slots, x, group_size):
+    return jnp.concatenate([meta_ref[1:2, :] == (seq_at ^ x) * slots] * group_size, axis=1)
+
+
+def block_scores(spans, group_size, q_ref, key_refs):
+    return [
         dot_nt(
             jnp.concatenate([ref[:, columns] for ref in key_refs], axis=0),
             stacked_heads(q_ref, group, group_size),
         )
         for group, columns in enumerate(spans)
     ]
+
+
+def pick_kernel(sizes, meta_ref, q_ref, *rest):
+    kv_local, group_size, slots = sizes
+    key_refs, out_ref = rest[:-1], rest[-1]
+    seq_at = lax.axis_index("seq")
+    spans = [slice(group * HD, (group + 1) * HD) for group in range(kv_local)]
+    scores = block_scores(spans, group_size, q_ref, key_refs)
+    for group in range(kv_local):
+        picked = scores[group][:slots]
+        for x in range(1, len(key_refs)):
+            pick = chosen_columns(meta_ref, seq_at, slots, x, group_size)
+            picked = jnp.where(pick, scores[group][x * slots : (x + 1) * slots], picked)
+        out_ref[group] = picked
+
+
+def cross_kernel(sizes, meta_ref, q_ref, cot_ref, picked_ref, key_ref, weights_ref, grad_ref):
+    kv_local, group_size, slots, blocks = sizes
+    seq_at = lax.axis_index("seq")
+    tok_rows = q_ref.shape[0]
+    chosen = [
+        chosen_columns(meta_ref, seq_at, slots, x, group_size) for x in range(blocks)
+    ]
+    count = meta_ref[2:3, :] - meta_ref[1:2, :]
+    slot_ids = lax.broadcasted_iota(jnp.int32, (slots, tok_rows), 0)
+    bias = jnp.where(slot_ids < count, 0.0, MASK_FILL)
+    bias = jnp.concatenate([bias] * group_size, axis=1)
+    scale = HD ** (-0.5) * LOG2E
+    spans = [slice(group * HD, (group + 1) * HD) for group in range(kv_local)]
+    scores = block_scores(spans, group_size, q_ref, (key_ref,))
     flags = [jnp.where(pick, 1.0, 0.0).astype(jnp.bfloat16) for pick in chosen]
     for group in range(kv_local):
-        picked = scores[group][(blocks - 1) * slots :]
-        for x in range(blocks - 1):
-            picked = jnp.where(chosen[x], scores[group][x * slots : (x + 1) * slots], picked)
+        picked = jnp.where(chosen[blocks - 1], scores[group], picked_ref[group])
         scaled = picked * scale + bias
         exps = jnp.exp2(scaled - jnp.max(scaled, axis=0, keepdims=True))
         inverse = 1.0 / jnp.sum(exps, axis=0, keepdims=True)
@@ -287,9 +304,7 @@
         )
         for x in range(blocks):
             at = pl.multiple_of((seq_at ^ x) * slots, slots)
-            grad_refs[group // share][pl.ds(at, slots), spans[group % share]] = grads[
-                x * slots : (x + 1) * slots
-            ]
+            grad_ref[pl.ds(at, slots), columns] = grads[x * slots : (x + 1) * slots]
 
 
 def stacked_features(rows, part, slots, cut):
@@ -434,9 +449,16 @@
         copy.wait()
 
 
+def presum_kernel(*refs):
+    total = refs[0][...].astype(jnp.float32)
+    for ref in refs[1:-1]:
+        total = total + ref[...].astype(jnp.float32)
+    refs[-1][...] = total
+
+
 def product_kernel(sizes, turned_ref, *rest):
     slots, out_rows, steps, blocks = sizes
-    terms, outs, sum_ref = rest[:blocks], rest[blocks:-1], rest[-1]
+    terms, outs, sum_ref = rest[:2], rest[2:-1], rest[-1]
     seq_at, dp_at = lax.axis_index("seq"), lax.axis_index("dp")
     total = terms[0][...].astype(jnp.float32)
     for ref in terms[1:]:
@@ -530,22 +552,30 @@
     )
     row_blocks = gathered(rows_own)
 
-    halves = 1
-    half_width = width // halves
-    weights, *grad_terms = pl.pallas_call(
+    halves, half_width = 1, width
+    columns = group_size * tok_rows
+    *keys_in, keys_last = key_blocks
+    picked = pl.pallas_call(
+        functools.partial(pick_kernel, (kv_local, group_size, slots)),
+        out_shape=jax.ShapeDtypeStruct((kv_local, slots, columns), jnp.float32),
+        in_specs=vmem_specs(1 + seq_size),
+        out_specs=vmem_specs(1)[0],
+        compiler_params=pltpu.CompilerParams(vmem_limit_bytes=16 << 20),
+        name="pick",
+    )(meta, q_cross[0], *keys_in)
+    weights, grad_terms = pl.pallas_call(
         functools.partial(cross_kernel, (kv_local, group_size, slots, seq_size)),
         out_shape=(
-            jax.ShapeDtypeStruct((kv_local, key_count, group_size * tok_rows), jnp.bfloat16),
-        )
-        + (jax.ShapeDtypeStruct((key_count, half_width), jnp.bfloat16),) * halves,
-        in_specs=vmem_specs(3 + seq_size),
-        out_specs=tuple(vmem_specs(1 + halves)),
-        compiler_params=pltpu.CompilerParams(vmem_limit_bytes=24 << 20),
+            jax.ShapeDtypeStruct((kv_local, key_count, columns), jnp.bfloat16),
+            jax.ShapeDtypeStruct((key_count, width), jnp.bfloat16),
+        ),
+        in_specs=vmem_specs(5),
+        out_specs=tuple(vmem_specs(2)),
+        compiler_params=pltpu.CompilerParams(vmem_limit_bytes=16 << 20),
         name="cross",
-    )(meta, q_cross[0], cotangent[0], *key_blocks)
+    )(meta, q_cross[0], cotangent[0], picked, keys_last)
     kv_blocks = gathered(kv_own)
     chip = seq_size // 2
-    columns = group_size * tok_rows
     partial_shape = jax.ShapeDtypeStruct((kv_local, HD, columns), jnp.float32)
     stats_shape = jax.ShapeDtypeStruct((kv_local + 1, 8, columns), jnp.float32)
     cross_out, partial, stats, turned = pl.pallas_call(
@@ -562,8 +592,17 @@
         name="early",
     )(meta, q_self[0], w_value, weights, *row_blocks, *kv_blocks[:chip])
     sums = []
-    for half in range(halves):
-        term_blocks = gathered(grad_terms[half])
+    for _ in range(halves):
+        *terms_in, terms_last = gathered(grad_terms)
+        terms_sum = pl.pallas_call(
+            presum_kernel,
+            out_shape=jax.ShapeDtypeStruct((key_count, half_width), jnp.float32),
+            in_specs=vmem_specs(seq_size - 1),
+            out_specs=vmem_specs(1)[0],
+            compiler_params=pltpu.CompilerParams(vmem_limit_bytes=8 << 20),
+            name="presum",
+        )(*terms_in)
+        term_blocks = (terms_sum, terms_last)
         blocks_out = pl.pallas_call(
             functools.partial(product_kernel, (slots, out_rows, dp_size, seq_size)),
             out_shape=tuple(
@@ -572,7 +611,7 @@
                 )
                 for x in range(dp_size)
             ),
-            in_specs=vmem_specs(1 + seq_size),
+            in_specs=vmem_specs(3),
             out_specs=tuple(vmem_specs(dp_size)),
             scratch_shapes=[pltpu.VMEM((key_count, half_width), jnp.bfloat16)],
             compiler_params=pltpu.CompilerParams(vmem_limit_bytes=16 << 20),

time: 33.7 us -> 40 us (1.19)
  waiting for transfers between devices: 13.2 us -> 19.7 us
  starting transfers between devices: 13.1 us -> 12.7 us
    ppermute x15, waiting for transfers between devices: 13.2 us -> 19.7 us  [swapped(): return lax.ppermute(array, axis, [(i, i ^ x) for i in range(size)])]
  transfers between devices with their start and end apart: 15 -> 15, of which waited for: 6 -> 7; matrix products, arithmetic and copies ran while one was open for 2% -> 2% of each run, Pallas kernels for 13% -> 11%
where the time goes in v7:
time: 40 us; the launch traced here: 39.8 us
  waiting for transfers between devices  19.7 us (49%)
  starting transfers between devices  12.7 us (32%)
  Pallas kernels  5.97 us (15%)
  between operations  0.76 us (2%)
  other arithmetic  0.71 us (2%)
    ppermute x15, waiting for transfers between devices, swapped(): return lax.ppermute(array, axis, [(i, i ^ x) for i in range(size)])  19.7 us
    ppermute x15, starting transfers between devices, swapped(): return lax.ppermute(array, axis, [(i, i ^ x) for i in range(size)])  12.7 us
    pallas_call x1, Pallas kernels, on_device_small(): pl.pallas_call(functools.partial(late_kernel, (kv_local, group_size, chip...  1.55 us
    pallas_call x1, Pallas kernels, on_device_small(): pl.pallas_call(functools.partial(early_kernel, (kv_local, group_size, slo...  1.48 us
    pallas_call x1, Pallas kernels, on_device_small(): pl.pallas_call(functools.partial(pack_kernel, (slots, parts, key_count //...  1.11 us
  transfers between devices with their start and end apart: 15, of which 7 were waited for; matrix products, arithmetic and copies ran while one was open for 2% of the time, Pallas kernels for 11%

profile of v7, /device:TPU:0, one launch (start us, length us, event | category | flops | bytes accessed | tf_op | source)
XLA Modules:
  0.0 39.8 jit_solution(12303468676435525861)
XLA Ops:
  0.7 3.1 %collective-permute-start.1 = (bf16[32,512]{1,0:T(8,128)(2,1)}, bf16[32,512]{1,0:T(8,128)(2,1)S(1)}, u32[]{:S(2)}, u32[]{:S(2)}) collective-permute-start(bf16[32,512]{1,0:T(8,128)(2,1)} %bitcast.11), channel_id=1, source_target_pairs={{0,4},{2,6},{4,0},{6,2},{1,5},{3,7},{5,1},{7,3},{8,12},{10,14},{12... | collective-permute-start | bytes 98312 | tf_op jit(solution)/shard_map/ppermute | solution.py:519
  3.7 2.1 %collective-permute-done.1.rest_2_ = bf16[32,512]{1,0:T(8,128)(2,1)S(1)} collective-permute-done((bf16[32,512]{1,0:T(8,128)(2,1)}, bf16[32,512]{1,0:T(8,128)(2,1)S(1)}, u32[]{:S(2)}, u32[]{:S(2)}) %collective-permute-start.1) | collective-permute-done | bytes 32800 | tf_op jit(solution)/shard_map/ppermute | solution.py:519
  5.8 1.1 %pack.1 = (bf16[96,512]{1,0:T(8,128)(2,1)S(1)}, bf16[256,512]{1,0:T(8,128)(2,1)S(1)}, s32[8,128]{1,0:T(8,128)S(1)}) custom-call(s32[1,128]{1,0:T(1,128)} %docs_hbm.1, s32[1,4]{1,0:T(1,128)} %tiles_hbm.1, s32[1,4]{1,0:T(1,128)} %cite_hbm.1, bf16[1,32,1280]{2,1,0:T(8,128)(2,1)} %features_hbm.1, bf16[1,128,512]{2,1,0:T(8,128)(2,1)} %k_hbm.1, ...), custom_call_target="tpu_custom_call" | custom-call | flops 4294967296 | bytes 16777216 | tf_op jit(solution)/shard_map/pack/pallas_call | solution.py:529
  7.0 0.6 %collective-permute-start.6 = (bf16[256,512]{1,0:T(8,128)(2,1)S(1)}, bf16[256,512]{1,0:T(8,128)(2,1)S(1)}, u32[]{:S(2)}, u32[]{:S(2)}) collective-permute-start(bf16[256,512]{1,0:T(8,128)(2,1)S(1)} %get-tuple-element.20.rest_4_), channel_id=1, source_target_pairs={{0,2},{2,0},{4,6},{6,4},{1,3},{3,1},{5,7},{7,5},{8,10},{10,8},{12,... | collective-permute-start | bytes 786440 | tf_op jit(solution)/shard_map/ppermute | solution.py:519
  7.6 0.3 pick.1.picked_ref
  7.9 0.5 %cross.1 = (bf16[4,128,512]{2,1,0:T(8,128)(2,1)S(1)}, bf16[128,512]{1,0:T(8,128)(2,1)S(1)}) custom-call(s32[8,128]{1,0:T(8,128)S(1)} %get-tuple-element.17.meta_ref, bf16[128,2048]{1,0:T(8,128)(2,1)S(1)} %bitcast.9, bf16[128,2048]{1,0:T(8,128)(2,1)S(1)} %bitcast.10, f32[4,32,512]{2,1,0:T(8,128)S(1)} %pick.1.picked_ref, ...), custom_call_target="tpu_custom_call" | custom-call | tf_op jit(solution)/shard_map/cross/pallas_call | solution.py:566
  8.4 2.1 %collective-permute-start.10 = (bf16[128,512]{1,0:T(8,128)(2,1)S(1)}, bf16[128,512]{1,0:T(8,128)(2,1)S(1)}, u32[]{:S(2)}, u32[]{:S(2)}) collective-permute-start(bf16[128,512]{1,0:T(8,128)(2,1)S(1)} %get-tuple-element.27.refs_0_), channel_id=1, source_target_pairs={{0,4},{2,6},{4,0},{6,2},{1,5},{3,7},{5,1},{7,3},{8,12},{10,14},{12... | collective-permute-start | bytes 393224 | tf_op jit(solution)/shard_map/ppermute | solution.py:519
  10.5 0.2 collective-permute-start.7
  10.7 1.9 %collective-permute-start.4 = (bf16[96,512]{1,0:T(8,128)(2,1)S(1)}, bf16[96,512]{1,0:T(8,128)(2,1)S(1)}, u32[]{:S(2)}, u32[]{:S(2)}) collective-permute-start(bf16[96,512]{1,0:T(8,128)(2,1)S(1)} %get-tuple-element.19.rest_0_), channel_id=1, source_target_pairs={{0,4},{2,6},{4,0},{6,2},{1,5},{3,7},{5,1},{7,3},{8,12},{10,14},{12... | collective-permute-start | bytes 294920 | tf_op jit(solution)/shard_map/ppermute | solution.py:519
  12.5 2.3 %collective-permute-done.10.refs_2_ = bf16[128,512]{1,0:T(8,128)(2,1)S(1)} collective-permute-done((bf16[128,512]{1,0:T(8,128)(2,1)S(1)}, bf16[128,512]{1,0:T(8,128)(2,1)S(1)}, u32[]{:S(2)}, u32[]{:S(2)}) %collective-permute-start.10) | collective-permute-done | bytes 131104 | tf_op jit(solution)/shard_map/ppermute | solution.py:519
  14.8 7.1 %collective-permute-done.4.rest_2_ = bf16[96,512]{1,0:T(8,128)(2,1)S(1)} collective-permute-done((bf16[96,512]{1,0:T(8,128)(2,1)S(1)}, bf16[96,512]{1,0:T(8,128)(2,1)S(1)}, u32[]{:S(2)}, u32[]{:S(2)}) %collective-permute-start.4) | collective-permute-done | bytes 98336 | tf_op jit(solution)/shard_map/ppermute | solution.py:519
  21.9 0.5 %collective-permute-start.5 = (bf16[96,512]{1,0:T(8,128)(2,1)S(1)}, bf16[96,512]{1,0:T(8,128)(2,1)S(1)}, u32[]{:S(2)}, u32[]{:S(2)}) collective-permute-start(bf16[96,512]{1,0:T(8,128)(2,1)S(1)} %collective-permute-done.4.rest_2_), channel_id=1, source_target_pairs={{0,2},{2,0},{4,6},{6,4},{1,3},{3,1},{5,7},{7,5},{8,10},{10,8},{12,... | collective-permute-start | bytes 294920 | tf_op jit(solution)/shard_map/ppermute | solution.py:519
  22.5 0.7 %collective-permute-done.3.rest_1_ = bf16[96,512]{1,0:T(8,128)(2,1)S(1)} collective-permute-done((bf16[96,512]{1,0:T(8,128)(2,1)S(1)}, bf16[96,512]{1,0:T(8,128)(2,1)S(1)}, u32[]{:S(2)}, u32[]{:S(2)}) %collective-permute-start.3) | collective-permute-done | bytes 98336 | tf_op jit(solution)/shard_map/ppermute | solution.py:519
  23.2 0.2 collective-permute-done.5.rest_3_
  23.4 1.5 %early.1 = (f32[4,128,512]{2,1,0:T(8,128)S(1)}, f32[4,128,512]{2,1,0:T(8,128)S(1)}, f32[5,8,512]{2,1,0:T(8,128)S(1)}, bf16[1280,128]{1,0:T(8,128)(2,1)S(1)}) custom-call(s32[8,128]{1,0:T(8,128)S(1)} %get-tuple-element.17.meta_ref, bf16[128,2048]{1,0:T(8,128)(2,1)S(1)} %bitcast.5, bf16[1280,512]{1,0:T(8,128)(2,1)S(1)} %copy-done.2, ...), custom_call_target="tpu_custom_call" | custom-call | tf_op jit(solution)/shard_map/early/pallas_call | solution.py:581
  24.9 0.3 product.1
  25.2 1.8 %collective-permute-start.14 = (bf16[80,512]{1,0:T(8,128)(2,1)S(1)}, bf16[80,512]{1,0:T(8,128)(2,1)S(1)}, u32[]{:S(2)}, u32[]{:S(2)}) collective-permute-start(bf16[80,512]{1,0:T(8,128)(2,1)S(1)} %get-tuple-element.31), channel_id=1, source_target_pairs={{0,8},{8,0},{16,24},{24,16},{1,9},{9,1},{17,25},{25,17},{2,10},{10... | collective-permute-start | bytes 245768 | tf_op jit(solution)/shard_map/ppermute | solution.py:519
  27.0 2.5 %collective-permute-start.13 = (bf16[80,512]{1,0:T(8,128)(2,1)S(1)}, bf16[80,512]{1,0:T(8,128)(2,1)S(1)}, u32[]{:S(2)}, u32[]{:S(2)}) collective-permute-start(bf16[80,512]{1,0:T(8,128)(2,1)S(1)} %get-tuple-element.30), channel_id=1, source_target_pairs={{0,24},{8,16},{16,8},{24,0},{1,25},{9,17},{17,9},{25,1},{2,26},{10... | collective-permute-start | bytes 245768 | tf_op jit(solution)/shard_map/ppermute | solution.py:519
  29.5 0.1 collective-permute-start.12
  29.6 0.7 %middle.1 = (f32[4,128,512]{2,1,0:T(8,128)S(1)}, f32[5,8,512]{2,1,0:T(8,128)S(1)}) custom-call(bf16[128,2048]{1,0:T(8,128)(2,1)S(1)} %bitcast.6, f32[4,128,512]{2,1,0:T(8,128)S(1)} %get-tuple-element.22.self_ref, f32[5,8,512]{2,1,0:T(8,128)S(1)} %get-tuple-element.23.stats_ref, bf16[256,512]{1,0:T(8,128)(2,1)S(1)} %collective-permute-done.7.pair_ref), custom_call_target="tpu_custom_call" | custom-call | tf_op jit(solution)/shard_map/middle/pallas_call | solution.py:626
  30.3 4.3 %collective-permute-done.13 = bf16[80,512]{1,0:T(8,128)(2,1)S(1)} collective-permute-done((bf16[80,512]{1,0:T(8,128)(2,1)S(1)}, bf16[80,512]{1,0:T(8,128)(2,1)S(1)}, u32[]{:S(2)}, u32[]{:S(2)}) %collective-permute-start.13) | collective-permute-done | bytes 81952 | tf_op jit(solution)/shard_map/ppermute | solution.py:519
  34.7 2.9 %collective-permute-done.12 = bf16[80,512]{1,0:T(8,128)(2,1)S(1)} collective-permute-done((bf16[80,512]{1,0:T(8,128)(2,1)S(1)}, bf16[80,512]{1,0:T(8,128)(2,1)S(1)}, u32[]{:S(2)}, u32[]{:S(2)}) %collective-permute-start.12) | collective-permute-done | bytes 81952 | tf_op jit(solution)/shard_map/ppermute | solution.py:519
  37.6 0.7 %convert_add_fusion = f32[80,512]{1,0:T(8,128)} fusion(bf16[80,512]{1,0:T(8,128)(2,1)S(1)} %collective-permute-done.14, bf16[80,512]{1,0:T(8,128)(2,1)S(1)} %collective-permute-done.13, f32[80,512]{1,0:T(8,128)S(1)} %get-tuple-element.28, bf16[80,512]{1,0:T(8,128)(2,1)S(1)} %collective-permute-done.12), kind=kLoop, calls=%fused_computation | loop fusion | flops 245760 | bytes 573440 | tf_op jit(solution)/shard_map/add | solution.py:623
  38.3 1.5 %late.1 = bf16[128,2048]{1,0:T(8,128)(2,1)} custom-call(bf16[128,2048]{1,0:T(8,128)(2,1)S(1)} %bitcast.7, f32[4,128,512]{2,1,0:T(8,128)S(1)} %get-tuple-element.21.cross_ref, f32[4,128,512]{2,1,0:T(8,128)S(1)} %get-tuple-element.24.self_ref, f32[5,8,512]{2,1,0:T(8,128)S(1)} %get-tuple-element.25.stats_ref, bf16[256,512]{1,0:T(8,128)(2,1)S(1)} %collective-permute-done.8.pair_ref), custom_call_target="tpu_custom_call" | custom-call | tf_op jit(solution)/shard_map/late/pallas_call | solution.py:634
  (25 shorter events, 0.1 us)
Async XLA Ops:
  0.6 6.9 %copy-start.1 = (bf16[1,128,2048]{2,1,0:T(8,128)(2,1)S(1)}, bf16[1,128,2048]{2,1,0:T(8,128)(2,1)}, u32[]{:S(2)}) copy-start(bf16[1,128,2048]{2,1,0:T(8,128)(2,1)} %param.15) | copy-start | bytes 1572868
  0.6 6.9 %copy-start.4 = (bf16[1,32,512]{2,1,0:T(8,128)(2,1)S(1)}, bf16[1,32,512]{2,1,0:T(8,128)(2,1)}, u32[]{:S(2)}) copy-start(bf16[1,32,512]{2,1,0:T(8,128)(2,1)} %param.17) | copy-start | bytes 98308
  0.7 7.2 %copy-start.3 = (bf16[1,128,2048]{2,1,0:T(8,128)(2,1)S(1)}, bf16[1,128,2048]{2,1,0:T(8,128)(2,1)}, u32[]{:S(2)}) copy-start(bf16[1,128,2048]{2,1,0:T(8,128)(2,1)} %param.16) | copy-start | bytes 1572868
  0.7 5.2 %collective-permute-start.1 = (bf16[32,512]{1,0:T(8,128)(2,1)}, bf16[32,512]{1,0:T(8,128)(2,1)S(1)}, u32[]{:S(2)}, u32[]{:S(2)}) collective-permute-start(bf16[32,512]{1,0:T(8,128)(2,1)} %bitcast.11), channel_id=1, source_target_pairs={{0,4},{2,6},{4,0},{6,2},{1,5},{3,7},{5,1},{7,3},{8,12},{10,14},{12... | collective-permute-start | bytes 98312 | tf_op jit(solution)/shard_map/ppermute | solution.py:519
  3.7 3.8 %collective-permute-start = (bf16[32,512]{1,0:T(8,128)(2,1)}, bf16[32,512]{1,0:T(8,128)(2,1)S(1)}, u32[]{:S(2)}, u32[]{:S(2)}) collective-permute-start(bf16[32,512]{1,0:T(8,128)(2,1)} %bitcast.12), channel_id=1, source_target_pairs={{0,2},{2,0},{4,6},{6,4},{1,3},{3,1},{5,7},{7,5},{8,10},{10,8},{12,... | collective-permute-start | bytes 98312 | tf_op jit(solution)/shard_map/ppermute | solution.py:519
  5.8 2.0 %collective-permute-start.2 = (bf16[32,512]{1,0:T(8,128)(2,1)S(1)}, bf16[32,512]{1,0:T(8,128)(2,1)S(1)}, u32[]{:S(2)}, u32[]{:S(2)}) collective-permute-start(bf16[32,512]{1,0:T(8,128)(2,1)S(1)} %collective-permute-done.1.rest_2_), channel_id=1, source_target_pairs={{0,2},{2,0},{4,6},{6,4},{1,3},{3,1},{5,7},{7,5},{8,10},{10,8},{12,... | collective-permute-start | bytes 98312 | tf_op jit(solution)/shard_map/ppermute | solution.py:519
  7.0 16.4 %collective-permute-start.6 = (bf16[256,512]{1,0:T(8,128)(2,1)S(1)}, bf16[256,512]{1,0:T(8,128)(2,1)S(1)}, u32[]{:S(2)}, u32[]{:S(2)}) collective-permute-start(bf16[256,512]{1,0:T(8,128)(2,1)S(1)} %get-tuple-element.20.rest_4_), channel_id=1, source_target_pairs={{0,2},{2,0},{4,6},{6,4},{1,3},{3,1},{5,7},{7,5},{8,10},{10,8},{12,... | collective-permute-start | bytes 786440 | tf_op jit(solution)/shard_map/ppermute | solution.py:519
  7.5 15.9 %copy-start = (bf16[1,128,2048]{2,1,0:T(8,128)(2,1)S(1)}, bf16[1,128,2048]{2,1,0:T(8,128)(2,1)}, u32[]{:S(2)}) copy-start(bf16[1,128,2048]{2,1,0:T(8,128)(2,1)} %param.11) | copy-start | bytes 1572868
  7.5 15.9 %copy-start.2 = (bf16[1280,512]{1,0:T(8,128)(2,1)S(1)}, bf16[1280,512]{1,0:T(8,128)(2,1)}, u32[]{:S(2)}) copy-start(bf16[1280,512]{1,0:T(8,128)(2,1)} %w_ref.1) | copy-start | bytes 3932164
  8.4 6.4 %collective-permute-start.10 = (bf16[128,512]{1,0:T(8,128)(2,1)S(1)}, bf16[128,512]{1,0:T(8,128)(2,1)S(1)}, u32[]{:S(2)}, u32[]{:S(2)}) collective-permute-start(bf16[128,512]{1,0:T(8,128)(2,1)S(1)} %get-tuple-element.27.refs_0_), channel_id=1, source_target_pairs={{0,4},{2,6},{4,0},{6,2},{1,5},{3,7},{5,1},{7,3},{8,12},{10,14},{12... | collective-permute-start | bytes 393224 | tf_op jit(solution)/shard_map/ppermute | solution.py:519
  10.5 11.4 %collective-permute-start.9 = (bf16[128,512]{1,0:T(8,128)(2,1)S(1)}, bf16[128,512]{1,0:T(8,128)(2,1)S(1)}, u32[]{:S(2)}, u32[]{:S(2)}) collective-permute-start(bf16[128,512]{1,0:T(8,128)(2,1)S(1)} %get-tuple-element.27.refs_0_), channel_id=1, source_target_pairs={{0,2},{2,0},{4,6},{6,4},{1,3},{3,1},{5,7},{7,5},{8,10},{10,8},{12,... | collective-permute-start | bytes 393224 | tf_op jit(solution)/shard_map/ppermute | solution.py:519
  10.5 19.1 %collective-permute-start.7 = (bf16[256,512]{1,0:T(8,128)(2,1)S(1)}, bf16[256,512]{1,0:T(8,128)(2,1)S(1)}, u32[]{:S(2)}, u32[]{:S(2)}) collective-permute-start(bf16[256,512]{1,0:T(8,128)(2,1)S(1)} %get-tuple-element.20.rest_4_), channel_id=1, source_target_pairs={{0,4},{2,6},{4,0},{6,2},{1,5},{3,7},{5,1},{7,3},{8,12},{10,14},{12... | collective-permute-start | bytes 786440 | tf_op jit(solution)/shard_map/ppermute | solution.py:519
  10.7 11.3 %collective-permute-start.4 = (bf16[96,512]{1,0:T(8,128)(2,1)S(1)}, bf16[96,512]{1,0:T(8,128)(2,1)S(1)}, u32[]{:S(2)}, u32[]{:S(2)}) collective-permute-start(bf16[96,512]{1,0:T(8,128)(2,1)S(1)} %get-tuple-element.19.rest_0_), channel_id=1, source_target_pairs={{0,4},{2,6},{4,0},{6,2},{1,5},{3,7},{5,1},{7,3},{8,12},{10,14},{12... | collective-permute-start | bytes 294920 | tf_op jit(solution)/shard_map/ppermute | solution.py:519
  14.8 10.1 %collective-permute-start.11 = (bf16[128,512]{1,0:T(8,128)(2,1)S(1)}, bf16[128,512]{1,0:T(8,128)(2,1)S(1)}, u32[]{:S(2)}, u32[]{:S(2)}) collective-permute-start(bf16[128,512]{1,0:T(8,128)(2,1)S(1)} %collective-permute-done.10.refs_2_), channel_id=1, source_target_pairs={{0,2},{2,0},{4,6},{6,4},{1,3},{3,1},{5,7},{7,5},{8,10},{10,8},{12,... | collective-permute-start | bytes 393224 | tf_op jit(solution)/shard_map/ppermute | solution.py:519
  21.9 1.3 %collective-permute-start.3 = (bf16[96,512]{1,0:T(8,128)(2,1)S(1)}, bf16[96,512]{1,0:T(8,128)(2,1)S(1)}, u32[]{:S(2)}, u32[]{:S(2)}) collective-permute-start(bf16[96,512]{1,0:T(8,128)(2,1)S(1)} %get-tuple-element.19.rest_0_), channel_id=1, source_target_pairs={{0,2},{2,0},{4,6},{6,4},{1,3},{3,1},{5,7},{7,5},{8,10},{10,8},{12,... | collective-permute-start | bytes 294920 | tf_op jit(solution)/shard_map/ppermute | solution.py:519
  21.9 1.5 %collective-permute-start.5 = (bf16[96,512]{1,0:T(8,128)(2,1)S(1)}, bf16[96,512]{1,0:T(8,128)(2,1)S(1)}, u32[]{:S(2)}, u32[]{:S(2)}) collective-permute-start(bf16[96,512]{1,0:T(8,128)(2,1)S(1)} %collective-permute-done.4.rest_2_), channel_id=1, source_target_pairs={{0,2},{2,0},{4,6},{6,4},{1,3},{3,1},{5,7},{7,5},{8,10},{10,8},{12,... | collective-permute-start | bytes 294920 | tf_op jit(solution)/shard_map/ppermute | solution.py:519
  25.2 5.1 %collective-permute-start.14 = (bf16[80,512]{1,0:T(8,128)(2,1)S(1)}, bf16[80,512]{1,0:T(8,128)(2,1)S(1)}, u32[]{:S(2)}, u32[]{:S(2)}) collective-permute-start(bf16[80,512]{1,0:T(8,128)(2,1)S(1)} %get-tuple-element.31), channel_id=1, source_target_pairs={{0,8},{8,0},{16,24},{24,16},{1,9},{9,1},{17,25},{25,17},{2,10},{10... | collective-permute-start | bytes 245768 | tf_op jit(solution)/shard_map/ppermute | solution.py:519
  27.0 7.6 %collective-permute-start.13 = (bf16[80,512]{1,0:T(8,128)(2,1)S(1)}, bf16[80,512]{1,0:T(8,128)(2,1)S(1)}, u32[]{:S(2)}, u32[]{:S(2)}) collective-permute-start(bf16[80,512]{1,0:T(8,128)(2,1)S(1)} %get-tuple-element.30), channel_id=1, source_target_pairs={{0,24},{8,16},{16,8},{24,0},{1,25},{9,17},{17,9},{25,1},{2,26},{10... | collective-permute-start | bytes 245768 | tf_op jit(solution)/shard_map/ppermute | solution.py:519
  29.5 8.1 %collective-permute-start.12 = (bf16[80,512]{1,0:T(8,128)(2,1)S(1)}, bf16[80,512]{1,0:T(8,128)(2,1)S(1)}, u32[]{:S(2)}, u32[]{:S(2)}) collective-permute-start(bf16[80,512]{1,0:T(8,128)(2,1)S(1)} %get-tuple-element.29), channel_id=1, source_target_pairs={{0,16},{8,24},{16,0},{24,8},{1,17},{9,25},{17,1},{25,9},{2,18},{10... | collective-permute-start | bytes 245768 | tf_op jit(solution)/shard_map/ppermute | solution.py:519
  29.6 8.7 %collective-permute-start.8 = (bf16[256,512]{1,0:T(8,128)(2,1)S(1)}, bf16[256,512]{1,0:T(8,128)(2,1)S(1)}, u32[]{:S(2)}, u32[]{:S(2)}) collective-permute-start(bf16[256,512]{1,0:T(8,128)(2,1)S(1)} %collective-permute-done.7.pair_ref), channel_id=1, source_target_pairs={{0,2},{2,0},{4,6},{6,4},{1,3},{3,1},{5,7},{7,5},{8,10},{10,8},{12,... | collective-permute-start | bytes 786440 | tf_op jit(solution)/shard_map/ppermute | solution.py:519

commit v8 on v7

--- a/solution.py
+++ b/solution.py
@@ -298,10 +298,9 @@
         weights = (exps * inverse).astype(jnp.bfloat16)
         for x in range(blocks):
             weights_ref[group, x * slots : (x + 1) * slots] = weights * flags[x]
-    for group, columns in enumerate(spans):
-        grads = dot_nn(weights_ref[group], stacked_heads(cot_ref, group, group_size)).astype(
-            jnp.bfloat16
-        )
+        columns = spans[group]
+        full = jnp.concatenate([weights * flag for flag in flags], axis=0)
+        grads = dot_nn(full, stacked_heads(cot_ref, group, group_size)).astype(jnp.bfloat16)
         for x in range(blocks):
             at = pl.multiple_of((seq_at ^ x) * slots, slots)
             grad_ref[pl.ds(at, slots), columns] = grads[x * slots : (x + 1) * slots]

time: 40 us -> 40 us (level)
  no operation moved by 1% of the time
where the time goes in v8:
time: 40 us; the launch traced here: 39.8 us
  waiting for transfers between devices  19.7 us (49%)
  starting transfers between devices  12.7 us (32%)
  Pallas kernels  5.96 us (15%)
  between operations  0.76 us (2%)
  other arithmetic  0.71 us (2%)
    ppermute x15, waiting for transfers between devices, swapped(): return lax.ppermute(array, axis, [(i, i ^ x) for i in range(size)])  19.7 us
    ppermute x15, starting transfers between devices, swapped(): return lax.ppermute(array, axis, [(i, i ^ x) for i in range(size)])  12.7 us
    pallas_call x1, Pallas kernels, on_device_small(): pl.pallas_call(functools.partial(late_kernel, (kv_local, group_size, chip...  1.55 us
    pallas_call x1, Pallas kernels, on_device_small(): pl.pallas_call(functools.partial(early_kernel, (kv_local, group_size, slo...  1.48 us
    pallas_call x1, Pallas kernels, on_device_small(): pl.pallas_call(functools.partial(pack_kernel, (slots, parts, key_count //...  1.11 us
  transfers between devices with their start and end apart: 15, of which 7 were waited for; matrix products, arithmetic and copies ran while one was open for 2% of the time, Pallas kernels for 11%

profile of v8, /device:TPU:0, one launch (start us, length us, event | category | flops | bytes accessed | tf_op | source)
XLA Modules:
  0.0 39.8 jit_solution(1360436802325640154)
XLA Ops:
  0.7 3.1 %collective-permute-start.1 = (bf16[32,512]{1,0:T(8,128)(2,1)}, bf16[32,512]{1,0:T(8,128)(2,1)S(1)}, u32[]{:S(2)}, u32[]{:S(2)}) collective-permute-start(bf16[32,512]{1,0:T(8,128)(2,1)} %bitcast.11), channel_id=1, source_target_pairs={{0,4},{2,6},{4,0},{6,2},{1,5},{3,7},{5,1},{7,3},{8,12},{10,14},{12... | collective-permute-start | bytes 98312 | tf_op jit(solution)/shard_map/ppermute | solution.py:518
  3.7 2.1 %collective-permute-done.1.rest_2_ = bf16[32,512]{1,0:T(8,128)(2,1)S(1)} collective-permute-done((bf16[32,512]{1,0:T(8,128)(2,1)}, bf16[32,512]{1,0:T(8,128)(2,1)S(1)}, u32[]{:S(2)}, u32[]{:S(2)}) %collective-permute-start.1) | collective-permute-done | bytes 32800 | tf_op jit(solution)/shard_map/ppermute | solution.py:518
  5.8 1.1 %pack.1 = (bf16[96,512]{1,0:T(8,128)(2,1)S(1)}, bf16[256,512]{1,0:T(8,128)(2,1)S(1)}, s32[8,128]{1,0:T(8,128)S(1)}) custom-call(s32[1,128]{1,0:T(1,128)} %docs_hbm.1, s32[1,4]{1,0:T(1,128)} %tiles_hbm.1, s32[1,4]{1,0:T(1,128)} %cite_hbm.1, bf16[1,32,1280]{2,1,0:T(8,128)(2,1)} %features_hbm.1, bf16[1,128,512]{2,1,0:T(8,128)(2,1)} %k_hbm.1, ...), custom_call_target="tpu_custom_call" | custom-call | flops 4294967296 | bytes 16777216 | tf_op jit(solution)/shard_map/pack/pallas_call | solution.py:528
  7.0 0.6 %collective-permute-start.6 = (bf16[256,512]{1,0:T(8,128)(2,1)S(1)}, bf16[256,512]{1,0:T(8,128)(2,1)S(1)}, u32[]{:S(2)}, u32[]{:S(2)}) collective-permute-start(bf16[256,512]{1,0:T(8,128)(2,1)S(1)} %get-tuple-element.20.rest_4_), channel_id=1, source_target_pairs={{0,2},{2,0},{4,6},{6,4},{1,3},{3,1},{5,7},{7,5},{8,10},{10,8},{12,... | collective-permute-start | bytes 786440 | tf_op jit(solution)/shard_map/ppermute | solution.py:518
  7.6 0.3 pick.1.picked_ref
  7.9 0.5 %cross.1 = (bf16[4,128,512]{2,1,0:T(8,128)(2,1)S(1)}, bf16[128,512]{1,0:T(8,128)(2,1)S(1)}) custom-call(s32[8,128]{1,0:T(8,128)S(1)} %get-tuple-element.17.meta_ref, bf16[128,2048]{1,0:T(8,128)(2,1)S(1)} %bitcast.9, bf16[128,2048]{1,0:T(8,128)(2,1)S(1)} %bitcast.10, f32[4,32,512]{2,1,0:T(8,128)S(1)} %pick.1.picked_ref, ...), custom_call_target="tpu_custom_call" | custom-call | tf_op jit(solution)/shard_map/cross/pallas_call | solution.py:565
  8.4 2.1 %collective-permute-start.10 = (bf16[128,512]{1,0:T(8,128)(2,1)S(1)}, bf16[128,512]{1,0:T(8,128)(2,1)S(1)}, u32[]{:S(2)}, u32[]{:S(2)}) collective-permute-start(bf16[128,512]{1,0:T(8,128)(2,1)S(1)} %get-tuple-element.27.refs_0_), channel_id=1, source_target_pairs={{0,4},{2,6},{4,0},{6,2},{1,5},{3,7},{5,1},{7,3},{8,12},{10,14},{12... | collective-permute-start | bytes 393224 | tf_op jit(solution)/shard_map/ppermute | solution.py:518
  10.5 0.2 collective-permute-start.7
  10.7 1.9 %collective-permute-start.4 = (bf16[96,512]{1,0:T(8,128)(2,1)S(1)}, bf16[96,512]{1,0:T(8,128)(2,1)S(1)}, u32[]{:S(2)}, u32[]{:S(2)}) collective-permute-start(bf16[96,512]{1,0:T(8,128)(2,1)S(1)} %get-tuple-element.19.rest_0_), channel_id=1, source_target_pairs={{0,4},{2,6},{4,0},{6,2},{1,5},{3,7},{5,1},{7,3},{8,12},{10,14},{12... | collective-permute-start | bytes 294920 | tf_op jit(solution)/shard_map/ppermute | solution.py:518
  12.5 2.3 %collective-permute-done.10.refs_2_ = bf16[128,512]{1,0:T(8,128)(2,1)S(1)} collective-permute-done((bf16[128,512]{1,0:T(8,128)(2,1)S(1)}, bf16[128,512]{1,0:T(8,128)(2,1)S(1)}, u32[]{:S(2)}, u32[]{:S(2)}) %collective-permute-start.10) | collective-permute-done | bytes 131104 | tf_op jit(solution)/shard_map/ppermute | solution.py:518
  14.8 7.1 %collective-permute-done.4.rest_2_ = bf16[96,512]{1,0:T(8,128)(2,1)S(1)} collective-permute-done((bf16[96,512]{1,0:T(8,128)(2,1)S(1)}, bf16[96,512]{1,0:T(8,128)(2,1)S(1)}, u32[]{:S(2)}, u32[]{:S(2)}) %collective-permute-start.4) | collective-permute-done | bytes 98336 | tf_op jit(solution)/shard_map/ppermute | solution.py:518
  21.9 0.5 %collective-permute-start.5 = (bf16[96,512]{1,0:T(8,128)(2,1)S(1)}, bf16[96,512]{1,0:T(8,128)(2,1)S(1)}, u32[]{:S(2)}, u32[]{:S(2)}) collective-permute-start(bf16[96,512]{1,0:T(8,128)(2,1)S(1)} %collective-permute-done.4.rest_2_), channel_id=1, source_target_pairs={{0,2},{2,0},{4,6},{6,4},{1,3},{3,1},{5,7},{7,5},{8,10},{10,8},{12,... | collective-permute-start | bytes 294920 | tf_op jit(solution)/shard_map/ppermute | solution.py:518
  22.5 0.7 %collective-permute-done.3.rest_1_ = bf16[96,512]{1,0:T(8,128)(2,1)S(1)} collective-permute-done((bf16[96,512]{1,0:T(8,128)(2,1)S(1)}, bf16[96,512]{1,0:T(8,128)(2,1)S(1)}, u32[]{:S(2)}, u32[]{:S(2)}) %collective-permute-start.3) | collective-permute-done | bytes 98336 | tf_op jit(solution)/shard_map/ppermute | solution.py:518
  23.2 0.2 collective-permute-done.5.rest_3_
  23.4 1.5 %early.1 = (f32[4,128,512]{2,1,0:T(8,128)S(1)}, f32[4,128,512]{2,1,0:T(8,128)S(1)}, f32[5,8,512]{2,1,0:T(8,128)S(1)}, bf16[1280,128]{1,0:T(8,128)(2,1)S(1)}) custom-call(s32[8,128]{1,0:T(8,128)S(1)} %get-tuple-element.17.meta_ref, bf16[128,2048]{1,0:T(8,128)(2,1)S(1)} %bitcast.5, bf16[1280,512]{1,0:T(8,128)(2,1)S(1)} %copy-done.2, ...), custom_call_target="tpu_custom_call" | custom-call | tf_op jit(solution)/shard_map/early/pallas_call | solution.py:580
  24.9 0.3 product.1
  25.2 1.9 %collective-permute-start.14 = (bf16[80,512]{1,0:T(8,128)(2,1)S(1)}, bf16[80,512]{1,0:T(8,128)(2,1)S(1)}, u32[]{:S(2)}, u32[]{:S(2)}) collective-permute-start(bf16[80,512]{1,0:T(8,128)(2,1)S(1)} %get-tuple-element.31), channel_id=1, source_target_pairs={{0,8},{8,0},{16,24},{24,16},{1,9},{9,1},{17,25},{25,17},{2,10},{10... | collective-permute-start | bytes 245768 | tf_op jit(solution)/shard_map/ppermute | solution.py:518
  27.0 2.5 %collective-permute-start.13 = (bf16[80,512]{1,0:T(8,128)(2,1)S(1)}, bf16[80,512]{1,0:T(8,128)(2,1)S(1)}, u32[]{:S(2)}, u32[]{:S(2)}) collective-permute-start(bf16[80,512]{1,0:T(8,128)(2,1)S(1)} %get-tuple-element.30), channel_id=1, source_target_pairs={{0,24},{8,16},{16,8},{24,0},{1,25},{9,17},{17,9},{25,1},{2,26},{10... | collective-permute-start | bytes 245768 | tf_op jit(solution)/shard_map/ppermute | solution.py:518
  29.5 0.1 collective-permute-start.12
  29.6 0.7 %middle.1 = (f32[4,128,512]{2,1,0:T(8,128)S(1)}, f32[5,8,512]{2,1,0:T(8,128)S(1)}) custom-call(bf16[128,2048]{1,0:T(8,128)(2,1)S(1)} %bitcast.6, f32[4,128,512]{2,1,0:T(8,128)S(1)} %get-tuple-element.22.self_ref, f32[5,8,512]{2,1,0:T(8,128)S(1)} %get-tuple-element.23.stats_ref, bf16[256,512]{1,0:T(8,128)(2,1)S(1)} %collective-permute-done.7.pair_ref), custom_call_target="tpu_custom_call" | custom-call | tf_op jit(solution)/shard_map/middle/pallas_call | solution.py:625
  30.3 4.3 %collective-permute-done.13 = bf16[80,512]{1,0:T(8,128)(2,1)S(1)} collective-permute-done((bf16[80,512]{1,0:T(8,128)(2,1)S(1)}, bf16[80,512]{1,0:T(8,128)(2,1)S(1)}, u32[]{:S(2)}, u32[]{:S(2)}) %collective-permute-start.13) | collective-permute-done | bytes 81952 | tf_op jit(solution)/shard_map/ppermute | solution.py:518
  34.7 2.9 %collective-permute-done.12 = bf16[80,512]{1,0:T(8,128)(2,1)S(1)} collective-permute-done((bf16[80,512]{1,0:T(8,128)(2,1)S(1)}, bf16[80,512]{1,0:T(8,128)(2,1)S(1)}, u32[]{:S(2)}, u32[]{:S(2)}) %collective-permute-start.12) | collective-permute-done | bytes 81952 | tf_op jit(solution)/shard_map/ppermute | solution.py:518
  37.6 0.7 %convert_add_fusion = f32[80,512]{1,0:T(8,128)} fusion(bf16[80,512]{1,0:T(8,128)(2,1)S(1)} %collective-permute-done.14, bf16[80,512]{1,0:T(8,128)(2,1)S(1)} %collective-permute-done.13, f32[80,512]{1,0:T(8,128)S(1)} %get-tuple-element.28, bf16[80,512]{1,0:T(8,128)(2,1)S(1)} %collective-permute-done.12), kind=kLoop, calls=%fused_computation | loop fusion | flops 245760 | bytes 573440 | tf_op jit(solution)/shard_map/add | solution.py:622
  38.3 1.6 %late.1 = bf16[128,2048]{1,0:T(8,128)(2,1)} custom-call(bf16[128,2048]{1,0:T(8,128)(2,1)S(1)} %bitcast.7, f32[4,128,512]{2,1,0:T(8,128)S(1)} %get-tuple-element.21.cross_ref, f32[4,128,512]{2,1,0:T(8,128)S(1)} %get-tuple-element.24.self_ref, f32[5,8,512]{2,1,0:T(8,128)S(1)} %get-tuple-element.25.stats_ref, bf16[256,512]{1,0:T(8,128)(2,1)S(1)} %collective-permute-done.8.pair_ref), custom_call_target="tpu_custom_call" | custom-call | tf_op jit(solution)/shard_map/late/pallas_call | solution.py:633
  (25 shorter events, 0.1 us)
Async XLA Ops:
  0.6 6.9 %copy-start.1 = (bf16[1,128,2048]{2,1,0:T(8,128)(2,1)S(1)}, bf16[1,128,2048]{2,1,0:T(8,128)(2,1)}, u32[]{:S(2)}) copy-start(bf16[1,128,2048]{2,1,0:T(8,128)(2,1)} %param.15) | copy-start | bytes 1572868
  0.6 6.9 %copy-start.4 = (bf16[1,32,512]{2,1,0:T(8,128)(2,1)S(1)}, bf16[1,32,512]{2,1,0:T(8,128)(2,1)}, u32[]{:S(2)}) copy-start(bf16[1,32,512]{2,1,0:T(8,128)(2,1)} %param.17) | copy-start | bytes 98308
  0.7 7.2 %copy-start.3 = (bf16[1,128,2048]{2,1,0:T(8,128)(2,1)S(1)}, bf16[1,128,2048]{2,1,0:T(8,128)(2,1)}, u32[]{:S(2)}) copy-start(bf16[1,128,2048]{2,1,0:T(8,128)(2,1)} %param.16) | copy-start | bytes 1572868
  0.7 5.2 %collective-permute-start.1 = (bf16[32,512]{1,0:T(8,128)(2,1)}, bf16[32,512]{1,0:T(8,128)(2,1)S(1)}, u32[]{:S(2)}, u32[]{:S(2)}) collective-permute-start(bf16[32,512]{1,0:T(8,128)(2,1)} %bitcast.11), channel_id=1, source_target_pairs={{0,4},{2,6},{4,0},{6,2},{1,5},{3,7},{5,1},{7,3},{8,12},{10,14},{12... | collective-permute-start | bytes 98312 | tf_op jit(solution)/shard_map/ppermute | solution.py:518
  3.7 3.8 %collective-permute-start = (bf16[32,512]{1,0:T(8,128)(2,1)}, bf16[32,512]{1,0:T(8,128)(2,1)S(1)}, u32[]{:S(2)}, u32[]{:S(2)}) collective-permute-start(bf16[32,512]{1,0:T(8,128)(2,1)} %bitcast.12), channel_id=1, source_target_pairs={{0,2},{2,0},{4,6},{6,4},{1,3},{3,1},{5,7},{7,5},{8,10},{10,8},{12,... | collective-permute-start | bytes 98312 | tf_op jit(solution)/shard_map/ppermute | solution.py:518
  5.8 2.0 %collective-permute-start.2 = (bf16[32,512]{1,0:T(8,128)(2,1)S(1)}, bf16[32,512]{1,0:T(8,128)(2,1)S(1)}, u32[]{:S(2)}, u32[]{:S(2)}) collective-permute-start(bf16[32,512]{1,0:T(8,128)(2,1)S(1)} %collective-permute-done.1.rest_2_), channel_id=1, source_target_pairs={{0,2},{2,0},{4,6},{6,4},{1,3},{3,1},{5,7},{7,5},{8,10},{10,8},{12,... | collective-permute-start | bytes 98312 | tf_op jit(solution)/shard_map/ppermute | solution.py:518
  7.0 16.4 %collective-permute-start.6 = (bf16[256,512]{1,0:T(8,128)(2,1)S(1)}, bf16[256,512]{1,0:T(8,128)(2,1)S(1)}, u32[]{:S(2)}, u32[]{:S(2)}) collective-permute-start(bf16[256,512]{1,0:T(8,128)(2,1)S(1)} %get-tuple-element.20.rest_4_), channel_id=1, source_target_pairs={{0,2},{2,0},{4,6},{6,4},{1,3},{3,1},{5,7},{7,5},{8,10},{10,8},{12,... | collective-permute-start | bytes 786440 | tf_op jit(solution)/shard_map/ppermute | solution.py:518
  7.5 15.8 %copy-start = (bf16[1,128,2048]{2,1,0:T(8,128)(2,1)S(1)}, bf16[1,128,2048]{2,1,0:T(8,128)(2,1)}, u32[]{:S(2)}) copy-start(bf16[1,128,2048]{2,1,0:T(8,128)(2,1)} %param.11) | copy-start | bytes 1572868
  7.5 15.8 %copy-start.2 = (bf16[1280,512]{1,0:T(8,128)(2,1)S(1)}, bf16[1280,512]{1,0:T(8,128)(2,1)}, u32[]{:S(2)}) copy-start(bf16[1280,512]{1,0:T(8,128)(2,1)} %w_ref.1) | copy-start | bytes 3932164
  8.4 6.4 %collective-permute-start.10 = (bf16[128,512]{1,0:T(8,128)(2,1)S(1)}, bf16[128,512]{1,0:T(8,128)(2,1)S(1)}, u32[]{:S(2)}, u32[]{:S(2)}) collective-permute-start(bf16[128,512]{1,0:T(8,128)(2,1)S(1)} %get-tuple-element.27.refs_0_), channel_id=1, source_target_pairs={{0,4},{2,6},{4,0},{6,2},{1,5},{3,7},{5,1},{7,3},{8,12},{10,14},{12... | collective-permute-start | bytes 393224 | tf_op jit(solution)/shard_map/ppermute | solution.py:518
  10.5 11.4 %collective-permute-start.9 = (bf16[128,512]{1,0:T(8,128)(2,1)S(1)}, bf16[128,512]{1,0:T(8,128)(2,1)S(1)}, u32[]{:S(2)}, u32[]{:S(2)}) collective-permute-start(bf16[128,512]{1,0:T(8,128)(2,1)S(1)} %get-tuple-element.27.refs_0_), channel_id=1, source_target_pairs={{0,2},{2,0},{4,6},{6,4},{1,3},{3,1},{5,7},{7,5},{8,10},{10,8},{12,... | collective-permute-start | bytes 393224 | tf_op jit(solution)/shard_map/ppermute | solution.py:518
  10.5 19.1 %collective-permute-start.7 = (bf16[256,512]{1,0:T(8,128)(2,1)S(1)}, bf16[256,512]{1,0:T(8,128)(2,1)S(1)}, u32[]{:S(2)}, u32[]{:S(2)}) collective-permute-start(bf16[256,512]{1,0:T(8,128)(2,1)S(1)} %get-tuple-element.20.rest_4_), channel_id=1, source_target_pairs={{0,4},{2,6},{4,0},{6,2},{1,5},{3,7},{5,1},{7,3},{8,12},{10,14},{12... | collective-permute-start | bytes 786440 | tf_op jit(solution)/shard_map/ppermute | solution.py:518
  10.7 11.3 %collective-permute-start.4 = (bf16[96,512]{1,0:T(8,128)(2,1)S(1)}, bf16[96,512]{1,0:T(8,128)(2,1)S(1)}, u32[]{:S(2)}, u32[]{:S(2)}) collective-permute-start(bf16[96,512]{1,0:T(8,128)(2,1)S(1)} %get-tuple-element.19.rest_0_), channel_id=1, source_target_pairs={{0,4},{2,6},{4,0},{6,2},{1,5},{3,7},{5,1},{7,3},{8,12},{10,14},{12... | collective-permute-start | bytes 294920 | tf_op jit(solution)/shard_map/ppermute | solution.py:518
  14.8 10.1 %collective-permute-start.11 = (bf16[128,512]{1,0:T(8,128)(2,1)S(1)}, bf16[128,512]{1,0:T(8,128)(2,1)S(1)}, u32[]{:S(2)}, u32[]{:S(2)}) collective-permute-start(bf16[128,512]{1,0:T(8,128)(2,1)S(1)} %collective-permute-done.10.refs_2_), channel_id=1, source_target_pairs={{0,2},{2,0},{4,6},{6,4},{1,3},{3,1},{5,7},{7,5},{8,10},{10,8},{12,... | collective-permute-start | bytes 393224 | tf_op jit(solution)/shard_map/ppermute | solution.py:518
  21.9 1.3 %collective-permute-start.3 = (bf16[96,512]{1,0:T(8,128)(2,1)S(1)}, bf16[96,512]{1,0:T(8,128)(2,1)S(1)}, u32[]{:S(2)}, u32[]{:S(2)}) collective-permute-start(bf16[96,512]{1,0:T(8,128)(2,1)S(1)} %get-tuple-element.19.rest_0_), channel_id=1, source_target_pairs={{0,2},{2,0},{4,6},{6,4},{1,3},{3,1},{5,7},{7,5},{8,10},{10,8},{12,... | collective-permute-start | bytes 294920 | tf_op jit(solution)/shard_map/ppermute | solution.py:518
  21.9 1.5 %collective-permute-start.5 = (bf16[96,512]{1,0:T(8,128)(2,1)S(1)}, bf16[96,512]{1,0:T(8,128)(2,1)S(1)}, u32[]{:S(2)}, u32[]{:S(2)}) collective-permute-start(bf16[96,512]{1,0:T(8,128)(2,1)S(1)} %collective-permute-done.4.rest_2_), channel_id=1, source_target_pairs={{0,2},{2,0},{4,6},{6,4},{1,3},{3,1},{5,7},{7,5},{8,10},{10,8},{12,... | collective-permute-start | bytes 294920 | tf_op jit(solution)/shard_map/ppermute | solution.py:518
  25.2 5.1 %collective-permute-start.14 = (bf16[80,512]{1,0:T(8,128)(2,1)S(1)}, bf16[80,512]{1,0:T(8,128)(2,1)S(1)}, u32[]{:S(2)}, u32[]{:S(2)}) collective-permute-start(bf16[80,512]{1,0:T(8,128)(2,1)S(1)} %get-tuple-element.31), channel_id=1, source_target_pairs={{0,8},{8,0},{16,24},{24,16},{1,9},{9,1},{17,25},{25,17},{2,10},{10... | collective-permute-start | bytes 245768 | tf_op jit(solution)/shard_map/ppermute | solution.py:518
  27.0 7.6 %collective-permute-start.13 = (bf16[80,512]{1,0:T(8,128)(2,1)S(1)}, bf16[80,512]{1,0:T(8,128)(2,1)S(1)}, u32[]{:S(2)}, u32[]{:S(2)}) collective-permute-start(bf16[80,512]{1,0:T(8,128)(2,1)S(1)} %get-tuple-element.30), channel_id=1, source_target_pairs={{0,24},{8,16},{16,8},{24,0},{1,25},{9,17},{17,9},{25,1},{2,26},{10... | collective-permute-start | bytes 245768 | tf_op jit(solution)/shard_map/ppermute | solution.py:518
  29.5 8.1 %collective-permute-start.12 = (bf16[80,512]{1,0:T(8,128)(2,1)S(1)}, bf16[80,512]{1,0:T(8,128)(2,1)S(1)}, u32[]{:S(2)}, u32[]{:S(2)}) collective-permute-start(bf16[80,512]{1,0:T(8,128)(2,1)S(1)} %get-tuple-element.29), channel_id=1, source_target_pairs={{0,16},{8,24},{16,0},{24,8},{1,17},{9,25},{17,1},{25,9},{2,18},{10... | collective-permute-start | bytes 245768 | tf_op jit(solution)/shard_map/ppermute | solution.py:518
  29.6 8.7 %collective-permute-start.8 = (bf16[256,512]{1,0:T(8,128)(2,1)S(1)}, bf16[256,512]{1,0:T(8,128)(2,1)S(1)}, u32[]{:S(2)}, u32[]{:S(2)}) collective-permute-start(bf16[256,512]{1,0:T(8,128)(2,1)S(1)} %collective-permute-done.7.pair_ref), channel_id=1, source_target_pairs={{0,2},{2,0},{4,6},{6,4},{1,3},{3,1},{5,7},{7,5},{8,10},{10,8},{12,... | collective-permute-start | bytes 786440 | tf_op jit(solution)/shard_map/ppermute | solution.py:518
